TPU v7x, 32 devices: a whole 2x2x4 slice. The times are simulated.
32 devices in a mesh: batch: 4 (over x, core), blk: 8 (over z, y).
Axes of the slice: x: 2, y: 2, z: 4, core: 2. Of those that a mesh axis runs over, the one named last changes fastest.
Arguments:
- latent: bfloat16 [4, 1024, 1536], P('batch', 'blk'), may hold values from -15 to 15
- time_embed: bfloat16 [4, 64], P('batch'), may hold values from -6 to 6
- text_tokens: bfloat16 [4, 77, 1280], P('batch'), may hold values from -6 to 6
- grid_shape: int32 [4, 2], P('batch'), may hold values from 8 to 112, as said below
- depth_weight: bfloat16 [9, 1536], replicated, may hold values from -5 to 5
- depth_bias: bfloat16 [1536], replicated, may hold values from -4 to 4
- widen_weight: bfloat16 [1536, 6144], P('batch'), may hold values from -0.15625 to 0.15625
- widen_bias: bfloat16 [6144], replicated, may hold values from -6 to 6
- response_gain: bfloat16 [2, 6144], replicated, may hold values from -6 to 6
- narrow_weight: bfloat16 [6144, 1536], P('batch'), may hold values from -0.078125 to 0.078125
- narrow_bias: bfloat16 [1536], replicated, may hold values from -4 to 4
- time_weight: bfloat16 [64, 3072], replicated, may hold values from -0.75 to 0.75
- time_bias: bfloat16 [3072], replicated, may hold values from -4 to 4
- text_weight: bfloat16 [1280, 1536], P('batch'), may hold values from -0.15625 to 0.15625
- text_bias: bfloat16 [1536], replicated, may hold values from -6 to 6
- project_weight: bfloat16 [1536, 4608], P('batch'), may hold values from -0.15625 to 0.15625
- project_bias: bfloat16 [3072], replicated, may hold values from -6 to 6
- output_weight: bfloat16 [1536, 1536], P('batch'), may hold values from -3 to 3
- output_bias: bfloat16 [1536], replicated, may hold values from -4 to 4
- cotangent: bfloat16 [4, 1024, 1536], P('batch', 'blk'), may hold values from -6 to 6
Outputs:
- block_output: bfloat16 [4, 1024, 1536], P('batch', 'blk')
- latent_grad: bfloat16 [4, 1024, 1536], P('batch', 'blk')
- depth_weight_grad: float32 [9, 1536], replicated
- depth_bias_grad: float32 [1536], replicated
- widen_weight_grad: float32 [1536, 6144], P('batch', 'blk')
- widen_bias_grad: float32 [6144], replicated
- response_gain_grad: float32 [2, 6144], replicated
- narrow_weight_grad: float32 [6144, 1536], P('batch', 'blk')
- narrow_bias_grad: float32 [1536], replicated
- time_weight_grad: float32 [64, 3072], replicated
- time_bias_grad: float32 [3072], replicated
- text_weight_grad: float32 [1280, 1536], P('batch', 'blk')
- text_bias_grad: float32 [1536], replicated
- project_weight_grad: float32 [1536, 4608], P('batch', 'blk')
- project_bias_grad: float32 [3072], replicated
- output_weight_grad: float32 [1536, 1536], P('batch', 'blk')
- output_bias_grad: float32 [1536], replicated
Inputs may be any that keep to these rules, and one draw needn't show every extreme that they name: `grid_shape`: column 0 is a latent's width w, from 56 to 112, and column 1 its height h = 896 // w; both ends of the widths occur in every draw.
All inputs are finite; a program needn't handle non-finite values.
Results may differ from a plain program's by a relative error of at most 0.017.
Values may be sent and summed in bfloat16 or wider, within the bound.
No kernel may reach another device: no remote copies, remote signals or barrier semaphores. Data moves between devices by JAX's collectives and lax.ppermute only.
A program may use at most 384 MiB of HBM per device.

v0:
```python
from functools import partial
import math

import jax
import jax.numpy as jnp
from jax import lax
from jax.sharding import PartitionSpec as P

HEADS = 24
HDIM = 64
WIDE = 112


norm_eps = 1e-06
masked_score = -1e30
highest = lax.Precision.HIGHEST


def padded(cells, sides, width):
    for axis, dim in sides:
        count = lax.axis_size(axis)
        ends = count - 1
        head = lax.slice_in_dim(cells, 0, width, axis=dim)
        tail = lax.slice_in_dim(cells, cells.shape[dim] - width, cells.shape[dim], axis=dim)
        cells = jnp.concatenate(
            [
                lax.ppermute(tail, axis, [(i, (i + 1) % count) for i in range(ends)]),
                cells,
                lax.ppermute(head, axis, [((i + 1) % count, i) for i in range(ends)]),
            ],
            axis=dim,
        )
    return cells


def row_norm(field_rows):
    average = jnp.mean(field_rows, axis=-1, keepdims=True)
    centred = field_rows - average
    spread = jnp.mean(centred * centred, axis=-1, keepdims=True)
    inverse = lax.rsqrt(spread + norm_eps)
    return (centred * inverse, inverse)


def row_norm_back(normed, inverse, upstream):
    first_mean = jnp.mean(upstream, axis=-1, keepdims=True)
    second_mean = jnp.mean(upstream * normed, axis=-1, keepdims=True)
    return inverse * (upstream - first_mean - normed * second_mean)


def tap_valid(row_index, grid_width, height, step_row, step_col):
    row_of = row_index // grid_width
    col_of = row_index % grid_width
    inside = (row_index >= 0) & (row_index < grid_width * height)
    return (
        inside
        & (row_of + step_row >= 0)
        & (row_of + step_row < height)
        & (col_of + step_col >= 0)
        & (col_of + step_col < grid_width)
    )


def depthwise(extended, grid_width, height, row_index, depth_taps, depth_shift, margin):
    row_total = row_index.shape[0]
    summed = jnp.zeros((row_total, extended.shape[1]), jnp.float32)
    for tap_index in range(9):
        step_row = tap_index // 3 - 1
        step_col = tap_index % 3 - 1
        offset = margin + step_row * grid_width + step_col
        shifted = lax.dynamic_slice_in_dim(extended, offset, row_total, 0).astype(jnp.float32)
        valid_tap = tap_valid(row_index, grid_width, height, step_row, step_col)
        summed = summed + jnp.where(valid_tap[:, None], shifted, 0.0) * depth_taps[tap_index]
    inside = (row_index >= 0) & (row_index < grid_width * height)
    return jnp.where(inside[:, None], summed + depth_shift, 0.0)


def depthwise_back(
    grad_ext, source_ext, grad_mine, grid_width, height, row_index, depth_taps, margin
):
    row_total = row_index.shape[0]
    into = jnp.zeros((row_total, grad_ext.shape[1]), jnp.float32)
    weight_rows = []
    for tap_index in range(9):
        step_row = tap_index // 3 - 1
        step_col = tap_index % 3 - 1
        tap_shift = step_row * grid_width + step_col
        shifted = lax.dynamic_slice_in_dim(source_ext, margin + tap_shift, row_total, 0).astype(
            jnp.float32
        )
        valid_tap = tap_valid(row_index, grid_width, height, step_row, step_col)
        weight_rows.append(jnp.sum(jnp.where(valid_tap[:, None], shifted, 0.0) * grad_mine, axis=0))
        moved = lax.dynamic_slice_in_dim(grad_ext, margin - tap_shift, row_total, 0)
        source_ok = tap_valid(row_index - tap_shift, grid_width, height, step_row, step_col)
        into = into + jnp.where(source_ok[:, None], moved, 0.0) * depth_taps[tap_index]
    return (into, jnp.stack(weight_rows))


def score_block(queries, key_block, key_live):
    scores = (
        jnp.einsum("irhd,iphd->ihrp", queries, key_block, preferred_element_type=jnp.float32)
        * 0.125
    )
    return jnp.where(key_live[:, None, None, :], scores, masked_score)


def fold_step(running, key_block, value_block, key_live, queries):
    running_top, running_sum, running_out = running
    scores = score_block(queries, key_block, key_live)
    new_top = jnp.maximum(running_top, jnp.max(scores, axis=-1))
    factor = jnp.exp(running_top - new_top)
    weights = jnp.exp(scores - new_top[..., None])
    running_sum = running_sum * factor + jnp.sum(weights, axis=-1)
    running_out = running_out * factor[..., None] + jnp.einsum(
        "ihrp,iphd->ihrd",
        weights.astype(jnp.bfloat16),
        value_block,
        preferred_element_type=jnp.float32,
    )
    return (new_top, running_sum, running_out)


def block_grads(queries, grad_heads, key_block, value_block, key_live, log_total, delta_rows):
    scores = score_block(queries, key_block, key_live)
    shares = jnp.exp(scores - log_total[..., None])
    dshares = jnp.einsum(
        "irhd,iphd->ihrp", grad_heads, value_block, preferred_element_type=jnp.float32
    )
    dscores = (shares * (dshares - delta_rows[..., None])).astype(jnp.bfloat16)
    return (shares.astype(jnp.bfloat16), dscores)


def live_rows(first_row, row_span, pixels):
    positions = first_row + jnp.arange(row_span, dtype=jnp.int32)
    return positions[None, :] < pixels[:, None]


def on_device(
    latent,
    time_embed,
    text_tokens,
    grid_shape,
    depth_weight,
    depth_bias,
    widen_weight,
    widen_bias,
    response_gain,
    narrow_weight,
    narrow_bias,
    time_weight,
    time_bias,
    text_weight,
    text_bias,
    project_weight,
    project_bias,
    output_weight,
    output_bias,
    cotangent,
):
    item_count, row_count, channels = latent.shape
    head_count = HEADS
    head_size = HDIM
    text_count = text_tokens.shape[1]
    wide_full, narrow_full, project_full, output_full, text_full = (
        lax.all_gather(widen_weight, "batch", axis=0, tiled=True),
        lax.all_gather(narrow_weight, "batch", axis=0, tiled=True),
        lax.all_gather(project_weight, "batch", axis=0, tiled=True),
        lax.all_gather(output_weight, "batch", axis=0, tiled=True),
        lax.all_gather(text_weight, "batch", axis=0, tiled=True),
    )
    blk_index = lax.axis_index("blk")
    row_index = blk_index * row_count + jnp.arange(row_count, dtype=jnp.int32)
    widths = grid_shape[:, 0]
    heights = grid_shape[:, 1]
    pixels = widths * heights
    inside = row_index[None, :] < pixels[:, None]
    keep_rows = inside.astype(jnp.float32)[..., None]
    margin = WIDE + 1
    depth_taps = depth_weight.astype(jnp.float32)
    extended = padded(latent, (("blk", 1),), margin)
    conv_all = jax.vmap(partial(depthwise, margin=margin), in_axes=(0, 0, 0, None, None, None))
    conved = conv_all(
        extended, widths, heights, row_index, depth_taps, depth_bias.astype(jnp.float32)
    )
    normed_one, inverse_one = row_norm(conved)
    first_in = normed_one.astype(jnp.bfloat16).reshape(item_count * row_count, channels)
    pre_act = jnp.dot(first_in, wide_full, preferred_element_type=jnp.float32) + widen_bias.astype(
        jnp.float32
    )
    pre_act = pre_act.reshape(item_count, row_count, -1)
    activated, gelu_pull = jax.vjp(partial(jax.nn.gelu, approximate=False), pre_act)
    hidden = activated * keep_rows
    squares = lax.psum(jnp.sum(hidden * hidden, axis=1), "blk")
    magnitude = jnp.sqrt(squares + norm_eps)
    mean_mag = jnp.mean(magnitude, axis=-1, keepdims=True) + norm_eps
    relative = (magnitude / mean_mag)[:, None, :]
    gains = response_gain.astype(jnp.float32)
    grn_out = gains[0] * (hidden * relative) + gains[1] + hidden
    second_in = grn_out.astype(jnp.bfloat16).reshape(item_count * row_count, -1)
    branch = jnp.dot(
        second_in, narrow_full, preferred_element_type=jnp.float32
    ) + narrow_bias.astype(jnp.float32)
    after_res = latent.astype(jnp.float32) + keep_rows * branch.reshape(
        item_count, row_count, channels
    )
    shift_scale = jnp.dot(
        time_embed, time_weight, preferred_element_type=jnp.float32
    ) + time_bias.astype(jnp.float32)
    scale_part = 1.0 + shift_scale[:, None, :channels]
    modulated = after_res * scale_part + shift_scale[:, None, channels:]
    normed_two, inverse_two = row_norm(modulated)
    attn_in = normed_two.astype(jnp.bfloat16).reshape(item_count * row_count, channels)
    project_all = jnp.dot(attn_in, project_full, preferred_element_type=jnp.float32)
    proj_bias = project_bias.astype(jnp.float32)
    head_shape = (item_count, row_count, head_count, head_size)
    queries = (
        (project_all[:, :channels] + proj_bias[:channels]).astype(jnp.bfloat16).reshape(head_shape)
    )
    key_local = project_all[:, channels : 2 * channels].astype(jnp.bfloat16).reshape(head_shape)
    value_local = (
        (project_all[:, 2 * channels :] + proj_bias[channels:])
        .astype(jnp.bfloat16)
        .reshape(head_shape)
    )
    soft_text = jax.nn.silu(text_tokens.astype(jnp.float32)).astype(jnp.bfloat16)
    text_feat = (
        jnp.einsum("itk,kc->itc", soft_text, text_full, preferred_element_type=jnp.float32)
        + text_bias.astype(jnp.float32)
    ).astype(jnp.bfloat16)
    text_proj = jnp.einsum(
        "itc,ck->itk", text_feat, project_full[:, channels:], preferred_element_type=jnp.float32
    )
    text_shape = (item_count, text_count, head_count, head_size)
    text_keys = text_proj[..., :channels].astype(jnp.bfloat16).reshape(text_shape)
    text_values = (
        (text_proj[..., channels:] + proj_bias[channels:]).astype(jnp.bfloat16).reshape(text_shape)
    )
    text_live = jnp.ones((item_count, text_count), dtype=bool)
    running = (
        jnp.full((item_count, head_count, row_count), masked_score, jnp.float32),
        jnp.zeros((item_count, head_count, row_count), jnp.float32),
        jnp.zeros((item_count, head_count, row_count, head_size), jnp.float32),
    )
    running = fold_step(running, text_keys, text_values, text_live, queries)
    seq_total = row_count * lax.axis_size("blk")
    block_rows = min(512, seq_total)
    key_piece = (
        lax.all_gather(key_local, "blk", axis=1, tiled=True),
        lax.all_gather(value_local, "blk", axis=1, tiled=True),
    )
    key_live = live_rows(jnp.int32(0), key_piece[0].shape[1], pixels)
    running = fold_step(running, key_piece[0], key_piece[1], key_live, queries)
    running_top, running_sum, running_out = running
    attended_heads = running_out / running_sum[..., None]
    log_total = running_top + jnp.log(running_sum)
    attended_low = (
        jnp.transpose(attended_heads, (0, 2, 1, 3))
        .reshape(item_count * row_count, channels)
        .astype(jnp.bfloat16)
    )
    att_out = jnp.dot(
        attended_low, output_full, preferred_element_type=jnp.float32
    ) + output_bias.astype(jnp.float32)
    block_output = (modulated + att_out.reshape(item_count, row_count, channels)).astype(
        jnp.bfloat16
    )
    upstream = cotangent.astype(jnp.float32)
    cot_rows = cotangent.reshape(item_count * row_count, channels)
    output_grad = jnp.einsum(
        "rc,rk->ck", attended_low, cot_rows, preferred_element_type=jnp.float32
    )
    output_bias_grad = jnp.sum(upstream, axis=(0, 1))
    grad_heads = (
        jnp.einsum("rk,ck->rc", cot_rows, output_full, preferred_element_type=jnp.float32)
        .astype(jnp.bfloat16)
        .reshape(head_shape)
    )
    delta_rows = jnp.sum(
        jnp.transpose(grad_heads, (0, 2, 1, 3)).astype(jnp.float32) * attended_heads, axis=-1
    )
    text_shares, text_dscores = block_grads(
        queries, grad_heads, text_keys, text_values, text_live, log_total, delta_rows
    )
    dq_text = jnp.einsum(
        "ihrp,iphd->irhd", text_dscores, text_keys, preferred_element_type=jnp.float32
    )
    dk_text = (
        jnp.einsum("ihrp,irhd->iphd", text_dscores, queries, preferred_element_type=jnp.float32)
        * 0.125
    )
    dv_text = jnp.einsum(
        "ihrp,irhd->iphd", text_shares, grad_heads, preferred_element_type=jnp.float32
    )
    dk_text, dv_text = (
        lax.psum(dk_text.astype(jnp.bfloat16), "blk").astype(jnp.float32),
        lax.psum(dv_text.astype(jnp.bfloat16), "blk").astype(jnp.float32),
    )
    keys_all, values_all = (
        lax.all_gather(key_local, "blk", axis=1, tiled=True),
        lax.all_gather(value_local, "blk", axis=1, tiled=True),
    )

    def query_block(block_index, running_grad):
        first_row = (block_index * block_rows).astype(jnp.int32)
        key_block = lax.dynamic_slice_in_dim(keys_all, first_row, block_rows, 1)
        value_block = lax.dynamic_slice_in_dim(values_all, first_row, block_rows, 1)
        shares_low, dscores = block_grads(
            queries,
            grad_heads,
            key_block,
            value_block,
            live_rows(first_row, block_rows, pixels),
            log_total,
            delta_rows,
        )
        return running_grad + jnp.einsum(
            "ihrp,iphd->irhd", dscores, key_block, preferred_element_type=jnp.float32
        )

    dq_pixels = lax.fori_loop(
        0, seq_total // block_rows, query_block, jnp.zeros(head_shape, jnp.float32)
    )
    dq_low = (
        ((dq_pixels + dq_text) * 0.125)
        .astype(jnp.bfloat16)
        .reshape(item_count * row_count, channels)
    )
    row_span = row_count * lax.axis_size("blk")
    span_rows = math.gcd(row_span, block_rows)

    def one_block(block_index):
        block_first = block_index * span_rows
        key_block = lax.dynamic_slice_in_dim(keys_all, block_first, span_rows, 1)
        value_block = lax.dynamic_slice_in_dim(values_all, block_first, span_rows, 1)
        shares_low, dscores = block_grads(
            queries,
            grad_heads,
            key_block,
            value_block,
            live_rows(block_first, span_rows, pixels),
            log_total,
            delta_rows,
        )
        key_grad = (
            jnp.einsum("ihrp,irhd->pihd", dscores, queries, preferred_element_type=jnp.float32)
            * 0.125
        )
        value_grad = jnp.einsum(
            "ihrp,irhd->pihd", shares_low, grad_heads, preferred_element_type=jnp.float32
        )
        return jnp.stack([key_grad, value_grad], axis=2).reshape(span_rows, item_count, 2, channels)

    stacked_blocks = lax.map(one_block, jnp.arange(row_span // span_rows, dtype=jnp.int32))
    key_sums = lax.psum_scatter(
        stacked_blocks.reshape(row_span, item_count, 2, channels).astype(jnp.bfloat16),
        "blk",
        scatter_dimension=0,
        tiled=True,
    ).astype(jnp.float32)
    key_sums = jnp.transpose(key_sums, (1, 0, 2, 3)).astype(jnp.bfloat16)
    dk_low = key_sums[:, :, 0].reshape(item_count * row_count, channels)
    dv_low = key_sums[:, :, 1].reshape(item_count * row_count, channels)
    stacked = jnp.concatenate([dq_low, dk_low, dv_low], axis=1)
    dnormed_two = jnp.einsum(
        "rk,ck->rc", stacked, project_full, preferred_element_type=jnp.float32
    ).reshape(item_count, row_count, channels)
    first_flag = (blk_index == 0).astype(jnp.float32)
    text_k_low = dk_text.astype(jnp.bfloat16).reshape(item_count * text_count, channels)
    text_v_low = dv_text.astype(jnp.bfloat16).reshape(item_count * text_count, channels)
    text_stack = jnp.concatenate([jnp.zeros_like(text_k_low), text_k_low, text_v_low], axis=1)
    text_feat_rows = text_feat.reshape(item_count * text_count, channels)
    dtext_feat = jnp.einsum(
        "rk,ck->rc", text_stack, project_full, preferred_element_type=jnp.float32
    ).astype(jnp.bfloat16)
    text_weight_grad = first_flag * jnp.einsum(
        "rk,rc->kc",
        soft_text.reshape(item_count * text_count, -1),
        dtext_feat,
        preferred_element_type=jnp.float32,
    )
    text_bias_grad = first_flag * jnp.sum(dtext_feat.astype(jnp.float32), axis=0)
    project_bias_grad = jnp.concatenate(
        [
            jnp.sum(dq_low.astype(jnp.float32), axis=0),
            jnp.sum(dv_low.astype(jnp.float32), axis=0)
            + first_flag * jnp.sum(text_v_low.astype(jnp.float32), axis=0),
        ]
    )
    dmodulated = upstream + row_norm_back(normed_two, inverse_two, dnormed_two)
    dshift = jnp.concatenate(
        [jnp.sum(dmodulated * after_res, axis=1), jnp.sum(dmodulated, axis=1)], axis=1
    )
    time_weight_grad = jnp.einsum(
        "ik,ic->kc", time_embed.astype(jnp.float32), dshift, precision=highest
    )
    time_bias_grad = jnp.sum(dshift, axis=0)
    dafter = dmodulated * scale_part
    dbranch = (keep_rows * dafter).astype(jnp.bfloat16).reshape(item_count * row_count, channels)
    narrow_grad = jnp.einsum("rf,rc->fc", second_in, dbranch, preferred_element_type=jnp.float32)
    narrow_bias_grad = jnp.sum(dbranch.astype(jnp.float32), axis=0)
    dgrn = jnp.einsum(
        "rc,fc->rf", dbranch, narrow_full, preferred_element_type=jnp.float32
    ).reshape(item_count, row_count, -1)
    gain_grad = jnp.stack(
        [jnp.sum(dgrn * hidden * relative, axis=(0, 1)), jnp.sum(dgrn, axis=(0, 1))]
    )
    dhidden = dgrn * (gains[0] * relative + 1.0)
    drelative = lax.psum(jnp.sum(dgrn * gains[0] * hidden, axis=1), "blk")
    unit_count = magnitude.shape[-1]
    dmagnitude = drelative / mean_mag - jnp.sum(drelative * magnitude, axis=-1, keepdims=True) / (
        mean_mag * mean_mag * unit_count
    )
    dhidden = dhidden + hidden * (dmagnitude / magnitude)[:, None, :]
    dpre = (
        gelu_pull(dhidden * keep_rows)[0].astype(jnp.bfloat16).reshape(item_count * row_count, -1)
    )
    widen_bias_grad = jnp.sum(dpre.astype(jnp.float32), axis=0)
    dnormed_one = jnp.einsum(
        "rf,cf->rc", dpre, wide_full, preferred_element_type=jnp.float32
    ).reshape(item_count, row_count, channels)
    dconved = jnp.where(inside[..., None], row_norm_back(normed_one, inverse_one, dnormed_one), 0.0)
    depth_bias_grad = jnp.sum(dconved, axis=(0, 1))
    grad_ext = padded(dconved.astype(jnp.bfloat16), (("blk", 1),), margin).astype(dconved.dtype)
    back_all = jax.vmap(partial(depthwise_back, margin=margin), in_axes=(0, 0, 0, 0, 0, None, None))
    dlatent_conv, depth_rows = back_all(
        grad_ext, extended, dconved, widths, heights, row_index, depth_taps
    )
    depth_weight_grad = jnp.sum(depth_rows, axis=0)
    latent_grad = (dafter + dlatent_conv).astype(jnp.bfloat16)
    widen_grad = jnp.einsum("rc,rf->cf", first_in, dpre, preferred_element_type=jnp.float32)
    project_grad = jnp.einsum(
        "rc,rk->ck", attn_in, stacked, preferred_element_type=jnp.float32
    ) + first_flag * jnp.einsum(
        "rc,rk->ck", text_feat_rows, text_stack, preferred_element_type=jnp.float32
    )
    widen_sum, narrow_sum, project_sum, output_sum, text_sum = (
        lax.psum_scatter(
            widen_grad.astype(jnp.bfloat16), "blk", scatter_dimension=1, tiled=True
        ).astype(jnp.float32),
        lax.psum_scatter(
            narrow_grad.astype(jnp.bfloat16), "blk", scatter_dimension=1, tiled=True
        ).astype(jnp.float32),
        lax.psum_scatter(
            project_grad.astype(jnp.bfloat16), "blk", scatter_dimension=1, tiled=True
        ).astype(jnp.float32),
        lax.psum_scatter(
            output_grad.astype(jnp.bfloat16), "blk", scatter_dimension=1, tiled=True
        ).astype(jnp.float32),
        lax.psum_scatter(
            text_weight_grad.astype(jnp.bfloat16), "blk", scatter_dimension=1, tiled=True
        ).astype(jnp.float32),
    )
    widen_sum, narrow_sum, project_sum, output_sum, text_sum = (
        lax.psum_scatter(
            widen_sum.astype(jnp.bfloat16), "batch", scatter_dimension=0, tiled=True
        ).astype(jnp.float32),
        lax.psum_scatter(
            narrow_sum.astype(jnp.bfloat16), "batch", scatter_dimension=0, tiled=True
        ).astype(jnp.float32),
        lax.psum_scatter(
            project_sum.astype(jnp.bfloat16), "batch", scatter_dimension=0, tiled=True
        ).astype(jnp.float32),
        lax.psum_scatter(
            output_sum.astype(jnp.bfloat16), "batch", scatter_dimension=0, tiled=True
        ).astype(jnp.float32),
        lax.psum_scatter(
            text_sum.astype(jnp.bfloat16), "batch", scatter_dimension=0, tiled=True
        ).astype(jnp.float32),
    )
    (
        depth_weight_sum,
        depth_bias_sum,
        widen_bias_sum,
        gain_sum,
        narrow_bias_sum,
        time_weight_sum,
        time_bias_sum,
        text_bias_sum,
        project_bias_sum,
        output_bias_sum,
    ) = lax.psum(
        (
            depth_weight_grad,
            depth_bias_grad,
            widen_bias_grad,
            gain_grad,
            narrow_bias_grad,
            time_weight_grad,
            time_bias_grad,
            text_bias_grad,
            project_bias_grad,
            output_bias_grad,
        ),
        ("batch", "blk"),
    )
    return (
        block_output,
        latent_grad,
        depth_weight_sum,
        depth_bias_sum,
        widen_sum,
        widen_bias_sum,
        gain_sum,
        narrow_sum,
        narrow_bias_sum,
        time_weight_sum,
        time_bias_sum,
        text_sum,
        text_bias_sum,
        project_sum,
        project_bias_sum,
        output_sum,
        output_bias_sum,
    )


def solution(mesh):
    placed = (
        P("batch", "blk", None),
        P("batch", None),
        P("batch", None, None),
        P("batch", None),
        P(),
        P(),
        P("batch", None),
        P(),
        P(),
        P("batch", None),
        P(),
        P(),
        P(),
        P("batch", None),
        P(),
        P("batch", None),
        P(),
        P("batch", None),
        P(),
        P("batch", "blk", None),
    )
    return jax.shard_map(
        on_device,
        mesh=mesh,
        in_specs=placed,
        out_specs=(
            P("batch", "blk", None),
            P("batch", "blk", None),
            P(),
            P(),
            P("batch", "blk"),
            P(),
            P(),
            P("batch", "blk"),
            P(),
            P(),
            P(),
            P("batch", "blk"),
            P(),
            P("batch", "blk"),
            P(),
            P("batch", "blk"),
            P(),
        ),
        check_vma=False,
    )
```

profile of v0, /device:TPU:9, one launch (start us, length us, event | category | flops | bytes accessed | tf_op | source)
XLA Modules:
  0.0 2252.4 jit_solution(7200997537969798391)
XLA Ops:
  37.6 93.7 %all-gather.8.cloned.1.call-done = bf16[1536,6144]{1,0:T(8,128)(2,1)} async-done(((bf16[384,6144]{1,0:T(8,128)(2,1)}), bf16[1536,6144]{1,0:T(8,128)(2,1)}) %all-gather.8.cloned.1.call-update) | async-done | bytes 18874384 | tf_op jit(solution)/shard_map/all_gather | solution.py:164
  131.3 16.3 multiply_reduce_fusion.2
  147.6 29.4 %psum.98 = f32[1,6144]{1,0:T(1,128)} all-reduce(f32[1,6144]{1,0:T(1,128)} %bitcast.619), channel_id=1, replica_groups=mesh['batch'=4,'blk'=8] {'blk'}, use_global_device_ids=true, to_apply=%region_3.6 | all-reduce | flops 6144 | bytes 49152 | tf_op jit(solution)/shard_map/psum | solution.py:192
  180.4 72.5 %all-gather.10.cloned.1.call-done = bf16[6144,1536]{1,0:T(8,128)(2,1)} async-done(((bf16[1536,1536]{1,0:T(8,128)(2,1)}), bf16[6144,1536]{1,0:T(8,128)(2,1)}) %all-gather.10.cloned.1.call-update) | async-done | bytes 18874384 | tf_op jit(solution)/shard_map/all_gather | solution.py:165
  262.1 83.4 %all-gather.12.cloned.1.call-done = bf16[1536,4608]{1,0:T(8,128)(2,1)} async-done(((bf16[384,4608]{1,0:T(8,128)(2,1)}), bf16[1536,4608]{1,0:T(8,128)(2,1)}) %all-gather.12.cloned.1.call-update) | async-done | bytes 14155792 | tf_op jit(solution)/shard_map/all_gather | solution.py:166
  355.1 24.8 %all-gather.14.cloned.1.call-done = bf16[1280,1536]{1,0:T(8,128)(2,1)} async-done(((bf16[320,1536]{1,0:T(8,128)(2,1)}), bf16[1280,1536]{1,0:T(8,128)(2,1)}) %all-gather.14.cloned.1.call-update) | async-done | bytes 3932176 | tf_op jit(solution)/shard_map/all_gather | solution.py:168
  383.0 35.9 %all-gather.20.cloned.1.call-done = bf16[1536,1536]{1,0:T(8,128)(2,1)} async-done(((bf16[384,1536]{1,0:T(8,128)(2,1)}), bf16[1536,1536]{1,0:T(8,128)(2,1)}) %all-gather.20.cloned.1.call-update) | async-done | bytes 4718608 | tf_op jit(solution)/shard_map/all_gather | solution.py:167
  430.3 51.4 %all-gather.16.cloned.1.call-done = bf16[1,1024,24,64]{1,3,2,0:T(8,128)(2,1)} async-done(((bf16[1,128,24,64]{1,3,2,0:T(8,128)(2,1)}), bf16[1,1024,24,64]{1,3,2,0:T(8,128)(2,1)}) %all-gather.16.cloned.1.call-update) | async-done | bytes 3145744 | tf_op jit(solution)/shard_map/all_gather | solution.py:247
  493.0 52.7 %all-gather.18.cloned.1.call-done = bf16[1,1024,24,64]{1,3,2,0:T(8,128)(2,1)} async-done(((bf16[1,128,24,64]{1,3,2,0:T(8,128)(2,1)}), bf16[1,1024,24,64]{1,3,2,0:T(8,128)(2,1)}) %all-gather.18.cloned.1.call-update) | async-done | bytes 3145744 | tf_op jit(solution)/shard_map/all_gather | solution.py:248
  559.6 41.1 %while.42 = (s32[]{:T(128)}, bf16[2,512,1,2,1536]{4,1,0,3,2:T(8,128)(2,1)}, s32[2]{0:T(128)S(1)}, s32[1]{0:T(128)}, bf16[1,1024,24,64]{1,3,2,0:T(8,128)(2,1)}, /...) while((s32[]{:T(128)}, ...), condition=%wide.region_15.18_spmd, body=%wide.region_14.17_spmd.sunk | while | flops 824181760 | bytes 70819608 | solution.py:352
  600.8 32.1 %all-reduce.10.cloned.1.call-done = (bf16[1,77,24,64]{1,3,2,0:T(8,128)(2,1)}, bf16[77,1536]{0,1:T(8,128)(2,1)}) async-done(((bf16[1,77,24,64]{1,3,2,0:T(8,128)(2,1)}, bf16[77,1536]{0,1:T(8,128)(2,1)}), (bf16[1,77,24,64]{1,3,2,0:T(8,128)(2,1)}, bf16[77,1536]{0,1:T(8,128)(2,1)})) %all-reduce.10.cloned.1.call-update) | async-done | bytes 473104 | tf_op jit(solution)/shard_map/psum | solution.py:295
  653.8 24.6 %while.43 = (s32[]{:T(128)}, f32[1,128,24,64]{1,3,2,0:T(8,128)}, bf16[1,1024,24,64]{1,3,2,0:T(8,128)(2,1)}, s32[1]{0:T(128)}, bf16[1,128,24,64]{1,3,2,0:T(8,128)...) while((s32[]{:T(128)}, f32[1,128,24,64]{1,3,2,0:T(8,128)}, ...), condition=%wide.region_13.16_spmd.clone, body=%wide.region_12.15_spmd.clone.sunk | while | flops 613811200 | bytes 19688136 | solution.py:319
  696.0 58.8 %reduce-scatter.18.cloned.1.call-done = bf16[128,1,2,1536]{3,0,2,1:T(8,128)(2,1)} async-done(((bf16[1024,1,2,1536]{3,0,2,1:T(8,128)(2,1)}), bf16[128,1,2,1536]{3,0,2,1:T(8,128)(2,1)}) %reduce-scatter.18.cloned.1.call-update) | async-done | bytes 786448 | tf_op jit(solution)/shard_map/reduce_scatter | solution.py:353
  756.0 16.4 add_convert_fusion
  804.5 28.7 %psum.99 = f32[1,6144]{1,0:T(1,128)} all-reduce(f32[1,6144]{1,0:T(1,128)} %bitcast.613), channel_id=1, replica_groups=mesh['batch'=4,'blk'=8] {'blk'}, use_global_device_ids=true, to_apply=%region_20.25 | all-reduce | flops 6144 | bytes 49152 | tf_op jit(solution)/shard_map/psum | solution.py:407
  864.2 78.3 %reduce-scatter.32.cloned.1.call-done = bf16[1536,192]{0,1:T(8,128)(2,1)} async-done(((bf16[1536,1536]{0,1:T(8,128)(2,1)}), bf16[1536,192]{0,1:T(8,128)(2,1)}) %reduce-scatter.32.cloned.1.call-update) | async-done | bytes 589840 | tf_op jit(solution)/shard_map/reduce_scatter | solution.py:445
  945.0 228.2 %reduce-scatter.30.cloned.1.call-done = bf16[1536,576]{0,1:T(8,128)(2,1)} async-done(((bf16[1536,4608]{0,1:T(8,128)(2,1)}), bf16[1536,576]{0,1:T(8,128)(2,1)}) %reduce-scatter.30.cloned.1.call-update) | async-done | bytes 1769488 | tf_op jit(solution)/shard_map/reduce_scatter | solution.py:442
  1177.2 312.7 %reduce-scatter.20.cloned.1.call-done = bf16[1536,768]{1,0:T(8,128)(2,1)} async-done(((bf16[1536,6144]{1,0:T(8,128)(2,1)}), bf16[1536,768]{1,0:T(8,128)(2,1)}) %reduce-scatter.20.cloned.1.call-update) | async-done | bytes 2359312 | tf_op jit(solution)/shard_map/reduce_scatter | solution.py:436
  1504.5 301.6 %reduce-scatter.24.cloned.1.call-done = bf16[6144,192]{0,1:T(8,128)(2,1)} async-done(((bf16[6144,1536]{0,1:T(8,128)(2,1)}), bf16[6144,192]{0,1:T(8,128)(2,1)}) %reduce-scatter.24.cloned.1.call-update) | async-done | bytes 2359312 | tf_op jit(solution)/shard_map/reduce_scatter | solution.py:439
  1861.8 28.7 %reduce-scatter.36.cloned.1.call-done = bf16[384,576]{1,0:T(8,128)(2,1)} async-done(((bf16[1536,576]{1,0:T(8,128)(2,1)}), bf16[384,576]{1,0:T(8,128)(2,1)}) %reduce-scatter.36.cloned.1.call-update) | async-done | bytes 442384
  1892.8 33.2 %reduce-scatter.22.cloned.1.call-done = bf16[384,768]{1,0:T(8,128)(2,1)} async-done(((bf16[1536,768]{1,0:T(8,128)(2,1)}), bf16[384,768]{1,0:T(8,128)(2,1)}) %reduce-scatter.22.cloned.1.call-update) | async-done | bytes 589840 | tf_op jit(solution)/shard_map/reduce_scatter | solution.py:453
  1928.1 33.6 %reduce-scatter.26.cloned.1.call-done = bf16[1536,192]{0,1:T(8,128)(2,1)} async-done(((bf16[6144,192]{0,1:T(8,128)(2,1)}), bf16[1536,192]{0,1:T(8,128)(2,1)}) %reduce-scatter.26.cloned.1.call-update) | async-done | bytes 589840 | tf_op jit(solution)/shard_map/reduce_scatter | solution.py:456
  1963.9 133.3 %all-reduce.8.cloned.1.call-done = (f32[9,1536]{1,0:T(8,128)}, f32[1536]{0:T(1024)}, f32[6144]{0:T(1024)}, f32[2,6144]{1,0:T(2,128)}, f32[1536]{0:T(1024)}, /*in...) async-done(((f32[9,1536]{1,0:T(8,128)}, f32[1536]{0:T(1024)}, f32[6144]{0:T(1024)}, f32[2,6144]{1,0:T(2,128)}, f32[1536]{0:T(1024)}, ...) | async-done | bytes 178192 | tf_op jit(solution)/shard_map/psum | solution.py:480
  2097.3 133.9 %all-reduce.6.cloned.1.call-done = f32[64,3072]{1,0:T(8,128)} async-done(((f32[64,3072]{1,0:T(8,128)}), f32[64,3072]{1,0:T(8,128)}) %all-reduce.6.cloned.1.call-update) | async-done | bytes 786448 | tf_op jit(solution)/shard_map/psum | solution.py:480
  (460 shorter events, 343.7 us)
Async XLA Ops:
  7.2 124.1 %all-gather.8.cloned.1.call-start = ((), (), s32[]{:S(2)}) async-start(), calls=%async_computation.11 | async-start | bytes 23592960 | tf_op jit(solution)/shard_map/all_gather | solution.py:164
  7.9 244.9 %all-gather.10.cloned.1.call-start = ((), (), s32[]{:S(2)}) async-start(), calls=%async_computation.12 | async-start | bytes 23592960 | tf_op jit(solution)/shard_map/all_gather | solution.py:165
  8.8 336.7 %all-gather.12.cloned.1.call-start = ((), (), s32[]{:S(2)}) async-start(), calls=%async_computation.13 | async-start | bytes 17694720 | tf_op jit(solution)/shard_map/all_gather | solution.py:166
  9.5 370.4 %all-gather.14.cloned.1.call-start = ((), (), s32[]{:S(2)}) async-start(), calls=%async_computation.14 | async-start | bytes 4915200 | tf_op jit(solution)/shard_map/all_gather | solution.py:168
  10.1 408.7 %all-gather.20.cloned.1.call-start = ((), (), s32[]{:S(2)}) async-start(), calls=%async_computation.17 | async-start | bytes 5898240 | tf_op jit(solution)/shard_map/all_gather | solution.py:167
  10.2 19.9 collective-permute-start.1
  15.6 466.2 %all-gather.16.cloned.1.call-start = ((), (), s32[]{:S(2)}) async-start(), calls=%async_computation.15 | async-start | bytes 3538944 | tf_op jit(solution)/shard_map/all_gather | solution.py:247
  353.9 191.7 %all-gather.18.cloned.1.call-start = ((), (), s32[]{:S(2)}) async-start(), calls=%async_computation.16 | async-start | bytes 3538944 | tf_op jit(solution)/shard_map/all_gather | solution.py:248
  355.1 277.9 %all-reduce.10.cloned.1.call-start = ((), (), s32[]{:S(2)}) async-start(), calls=%async_computation.31 | async-start | bytes 1572864 | tf_op jit(solution)/shard_map/psum | solution.py:295
  559.3 195.4 %reduce-scatter.18.cloned.1.call-start = ((), (), s32[]{:S(2)}) async-start(), calls=%async_computation.18 | async-start | bytes 7077888 | tf_op jit(solution)/shard_map/reduce_scatter | solution.py:353
  600.7 261.2 %reduce-scatter.28.cloned.1.call-start = ((), (), s32[]{:S(2)}) async-start(), calls=%async_computation.24 | async-start | bytes 4423680 | tf_op jit(solution)/shard_map/reduce_scatter | solution.py:448
  647.3 295.2 %reduce-scatter.32.cloned.1.call-start = ((), (), s32[]{:S(2)}) async-start(), calls=%async_computation.26 | async-start | bytes 5308416 | tf_op jit(solution)/shard_map/reduce_scatter | solution.py:445
  651.9 521.3 %reduce-scatter.30.cloned.1.call-start = ((), (), s32[]{:S(2)}) async-start(), calls=%async_computation.25 | async-start | bytes 15925248 | tf_op jit(solution)/shard_map/reduce_scatter | solution.py:442
  772.4 717.5 %reduce-scatter.20.cloned.1.call-start = ((), (), s32[]{:S(2)}) async-start(), calls=%async_computation.19 | async-start | bytes 21233664 | tf_op jit(solution)/shard_map/reduce_scatter | solution.py:436
  851.9 954.2 %reduce-scatter.24.cloned.1.call-start = ((), (), s32[]{:S(2)}) async-start(), calls=%async_computation.21 | async-start | bytes 21233664 | tf_op jit(solution)/shard_map/reduce_scatter | solution.py:439
  861.9 981.1 %reduce-scatter.34.cloned.1.call-start = ((), (), s32[]{:S(2)}) async-start(), calls=%async_computation.27 | async-start | bytes 819200
  864.2 993.1 %reduce-scatter.38.cloned.1.call-start = ((), (), s32[]{:S(2)}) async-start(), calls=%async_computation.29 | async-start | bytes 983040
  944.8 945.7 %reduce-scatter.36.cloned.1.call-start = ((), (), s32[]{:S(2)}) async-start(), calls=%async_computation.28 | async-start | bytes 2457600
  1177.2 748.8 %reduce-scatter.22.cloned.1.call-start = ((), (), s32[]{:S(2)}) async-start(), calls=%async_computation.20 | async-start | bytes 2949120 | tf_op jit(solution)/shard_map/reduce_scatter | solution.py:453
  1489.9 471.8 %reduce-scatter.26.cloned.1.call-start = ((), (), s32[]{:S(2)}) async-start(), calls=%async_computation.22 | async-start | bytes 2949120 | tf_op jit(solution)/shard_map/reduce_scatter | solution.py:456
  1826.1 33.0 %collective-permute-start.3 = (bf16[1,113,1536]{2,1,0:T(8,128)(2,1)S(1)}, bf16[1,113,1536]{2,1,0:T(8,128)(2,1)S(1)}, u32[]{:S(2)}, u32[]{:S(2)}) collective-permute-start(bf16[1,113,1536]{2,1,0:T(8,128)(2,1)S(1)} %get-tuple-element.606), channel_id=1, source_target_pairs={{1,0},{2,1},{3,2},{4,3},{5,4},{6,5},{7,6},{9,8},{10,9},{11,10},{12... | collective-permute-start | bytes 1041416 | tf_op jit(solution)/shard_map/ppermute | solution.py:29
  1830.7 28.4 %collective-permute-start.2 = (bf16[1,113,1536]{2,1,0:T(8,128)(2,1)S(1)}, bf16[1,113,1536]{2,1,0:T(8,128)(2,1)S(1)}, u32[]{:S(2)}, u32[]{:S(2)}) collective-permute-start(bf16[1,113,1536]{2,1,0:T(8,128)(2,1)S(1)} %get-tuple-element.605), channel_id=1, source_target_pairs={{0,1},{1,2},{2,3},{3,4},{4,5},{5,6},{6,7},{8,9},{9,10},{10,11},{11... | collective-permute-start | bytes 1041416 | tf_op jit(solution)/shard_map/ppermute | solution.py:27
  1837.9 259.3 %all-reduce.8.cloned.1.call-start = ((), (), s32[]{:S(2)}) async-start(), calls=%async_computation.30 | async-start | bytes 458752 | tf_op jit(solution)/shard_map/psum | solution.py:480
  1838.5 392.6 %all-reduce.6.cloned.1.call-start = ((), (), s32[]{:S(2)}) async-start(), calls=%async_computation.23 | async-start | bytes 1572864 | tf_op jit(solution)/shard_map/psum | solution.py:480
  (123 other events, 6449.8 us)
Sparse Core Ops, SparseCore 0:
  9.6 121.6 all-gather.7
  132.9 119.9 all-gather.9
  254.4 91.0 all-gather.11
  346.9 32.9 all-gather.13
  381.3 37.4 all-gather.19
  421.3 60.3 all-gather.15
  484.4 61.2 all-gather.17
  559.5 73.4 all-reduce.9
  636.9 117.8 reduce-scatter.17
  758.8 84.8 reduce-scatter.27
  847.4 95.0 reduce-scatter.31
  946.0 227.1 reduce-scatter.29
  1177.1 312.8 reduce-scatter.19
  1493.6 312.4 reduce-scatter.23
  1808.5 23.0 reduce-scatter.33
  1834.0 23.2 reduce-scatter.37
  1859.8 30.6 reduce-scatter.35
  1892.9 33.0 reduce-scatter.21
  1928.7 33.0 reduce-scatter.25
  1969.1 128.0 all-reduce.7
  2103.8 127.2 all-reduce.5
where the time goes:
time: 2270 us; the launch traced here: 2250 us
  waiting for transfers between devices  1800 us (79%)
  matrix products  224 us (10%)
  other arithmetic  67 us (3%)
  blocking collectives  58.1 us (3%)
  local copies, waits for them, and re-layouts  55.6 us (2%)
  between operations  27.9 us (1%)
    reduce_scatter x1, waiting for transfers between devices, on_device(): lax.psum_scatter(widen_grad.astype(jnp.bfloat16), 'blk', scatter_dimensio...  313 us
    reduce_scatter x1, waiting for transfers between devices, on_device(): lax.psum_scatter(narrow_grad.astype(jnp.bfloat16), 'blk', scatter_dimensi...  302 us
    psum x2, waiting for transfers between devices, on_device(): lax.psum((depth_weight_grad, depth_bias_grad, widen_bias_grad, gain_grad,...  267 us
    reduce_scatter x1, waiting for transfers between devices, on_device(): lax.psum_scatter(project_grad.astype(jnp.bfloat16), 'blk', scatter_dimens...  228 us
    all_gather x1, waiting for transfers between devices, on_device(): lax.all_gather(widen_weight, 'batch', axis=0, tiled=True)  93.7 us
    all_gather x1, waiting for transfers between devices, on_device(): lax.all_gather(project_weight, 'batch', axis=0, tiled=True)  83.4 us
    reduce_scatter x1, waiting for transfers between devices, on_device(): lax.psum_scatter(output_grad.astype(jnp.bfloat16), 'blk', scatter_dimensi...  78.3 us
    all_gather x1, waiting for transfers between devices, on_device(): lax.all_gather(narrow_weight, 'batch', axis=0, tiled=True)  72.5 us
  transfers between devices with their start and end apart: 25, of which 20 were waited for; matrix products, arithmetic and copies ran while one was open for 14% of the time, Pallas kernels for 0%

commit v1 on v0

v1 whole, which is shorter than its diff:
```python
import jax
import jax.numpy as jnp
from jax import lax
from jax.sharding import PartitionSpec as P

HEADS = 24
HDIM = 64
WIDE = 112

norm_eps = 1e-06
masked_score = -1e30
f32 = jnp.float32
bf16 = jnp.bfloat16


def mm(left, right, dims):
    return lax.dot_general(left, right, (dims, ((), ())), preferred_element_type=f32)


def swap(cells, axis, distance):
    count = lax.axis_size(axis)
    return lax.ppermute(cells, axis, [(i, i ^ distance) for i in range(count)])


def bits_of(count):
    return [1 << n for n in range(count.bit_length() - 1)]


def gather_batch(cells):
    held = {0: cells}
    for bit in reversed(bits_of(lax.axis_size("batch"))[1:]):
        for place in list(held):
            held[place ^ bit] = swap(held[place], "batch", bit)
    for place in list(held):
        held[place ^ 1] = swap(held[place], "batch", 1)
    return [held[d] for d in range(len(held))]


def scatter_batch(parts):
    held = dict(enumerate(parts))
    for bit in bits_of(lax.axis_size("batch")):
        held = {
            place: cells + swap(held[place ^ bit].astype(bf16), "batch", bit).astype(f32)
            for place, cells in held.items()
            if not place & bit
        }
    return held[0]


def tree_sum(pieces):
    pieces = list(pieces)
    while len(pieces) > 1:
        pieces = [pieces[i] + pieces[i + 1] for i in range(0, len(pieces), 2)]
    return pieces[0]


def sum_over(cells, axis):
    count = lax.axis_size(axis)
    if axis == "blk" and count == 8:
        cells = cells + swap(cells, axis, 1)
        return tree_sum([cells] + [swap(cells, axis, d) for d in (2, 4, 6)])
    if count <= 4:
        return tree_sum([cells] + [swap(cells, axis, d) for d in range(1, count)])
    for bit in bits_of(count):
        cells = cells + swap(cells, axis, bit)
    return cells


def take(cells, place, axis=0):
    return lax.dynamic_index_in_dim(cells, place, axis, keepdims=False)


def put(cells, piece, place):
    return lax.dynamic_update_index_in_dim(cells, piece, place, 0)


def scatter_rows(shards):
    count = shards.shape[0]
    if count != 8:
        return lax.psum_scatter(shards, "blk", scatter_dimension=0, tiled=False).astype(f32)
    place = lax.axis_index("blk")
    depth, side = place // 2, place % 2
    pairs = shards.reshape((4, 2) + shards.shape[1:])
    other = swap(take(pairs, 1 - side, 1), "blk", 1)
    halves = (take(pairs, side, 1).astype(f32) + other.astype(f32)).astype(bf16)
    up = down = None
    for step in (1, 2, 3):
        rise = take(halves, jnp.clip(depth + 4 - step, 0, 3))
        fall = take(halves, jnp.clip(depth - 4 + step, 0, 3))
        if step > 1:
            rise = (rise.astype(f32) + up.astype(f32)).astype(bf16)
            fall = (fall.astype(f32) + down.astype(f32)).astype(bf16)
        senders = [(2 * d + s, 2 * d + 2 + s) for d in range(step) for s in range(2)]
        up = lax.ppermute(rise, "blk", senders)
        down = lax.ppermute(fall, "blk", [(7 - i, 7 - j) for i, j in senders])
    return take(halves, depth).astype(f32) + up.astype(f32) + down.astype(f32)


def row_norm(field_rows):
    average = jnp.mean(field_rows, axis=-1, keepdims=True)
    centred = field_rows - average
    spread = jnp.mean(centred * centred, axis=-1, keepdims=True)
    inverse = lax.rsqrt(spread + norm_eps)
    return (centred * inverse, inverse)


def row_norm_back(normed, inverse, upstream):
    first_mean = jnp.mean(upstream, axis=-1, keepdims=True)
    second_mean = jnp.mean(upstream * normed, axis=-1, keepdims=True)
    return inverse * (upstream - first_mean - normed * second_mean)


def halo(cells, margin):
    count = lax.axis_size("blk")
    head = cells[:margin]
    tail = cells[cells.shape[0] - margin :]
    before = lax.ppermute(tail, "blk", [(i, i + 1) for i in range(count - 1)])
    after = lax.ppermute(head, "blk", [(i + 1, i) for i in range(count - 1)])
    return jnp.concatenate([before, cells, after], axis=0)


def attend(queries, keys, values, grad_heads, live):
    scores = mm(queries, keys, ((1,), (1,))) * 0.125
    scores = jnp.where(live, scores, masked_score)
    raised = jnp.exp(scores - jnp.max(scores, axis=1, keepdims=True))
    shares = raised / jnp.sum(raised, axis=1, keepdims=True)
    shares_low = shares.astype(bf16)
    attended = mm(shares_low, values, ((1,), (0,)))
    delta = jnp.sum(grad_heads.astype(f32) * attended, axis=1, keepdims=True)
    dshares = mm(grad_heads, values, ((1,), (1,)))
    dscores = (shares * (dshares - delta)).astype(bf16)
    return (
        attended,
        mm(dscores, keys, ((1,), (0,))) * 0.125,
        mm(dscores, queries, ((0,), (0,))) * 0.125,
        mm(shares_low, grad_heads, ((0,), (0,))),
    )


def colour(sources, targets, degree):
    left = list(range(len(sources)))
    rounds = []
    for _ in range(degree):
        owner = {}

        def grow(node, seen):
            for edge in left:
                if sources[edge] != node or targets[edge] in seen:
                    continue
                seen.add(targets[edge])
                taken = owner.get(targets[edge])
                if taken is None or grow(sources[taken], seen):
                    owner[targets[edge]] = edge
                    return True
            return False

        for node in range(max(sources) + 1):
            grow(node, set())
        rounds.append(sorted(owner.values()))
        left = [edge for edge in left if edge not in set(rounds[-1])]
    return rounds


def on_device(
    latent,
    time_embed,
    text_tokens,
    grid_shape,
    depth_weight,
    depth_bias,
    widen_weight,
    widen_bias,
    response_gain,
    narrow_weight,
    narrow_bias,
    time_weight,
    time_bias,
    text_weight,
    text_bias,
    project_weight,
    project_bias,
    output_weight,
    output_bias,
    cotangent,
):
    _, rows, channels = latent.shape
    batch, blk = lax.axis_size("batch"), lax.axis_size("blk")
    bi, ki = lax.axis_index("batch"), lax.axis_index("blk")
    units = widen_weight.shape[1]
    mine = units // batch
    wide_rows = channels // batch
    own_heads = HEADS // batch
    per = -(-batch * own_heads // blk)
    groups = own_heads // per
    span = per * HDIM
    used = batch * groups
    clip_rows = text_weight.shape[0]
    text_count = text_tokens.shape[1]
    ring = blk // batch
    lat = latent[0]
    cot = cotangent[0]

    facts = jnp.concatenate(
        [
            grid_shape.astype(f32),
            time_embed.astype(f32),
            jnp.zeros((1, 126 - time_embed.shape[1]), f32),
        ],
        axis=1,
    )
    facts = gather_batch(facts)
    pixels = jnp.stack([cells[0, 0] * cells[0, 1] for cells in facts])
    times = [cells[0, 2 : 2 + time_embed.shape[1]] for cells in facts]

    margin = WIDE + 1
    source_ext = halo(lat, margin)

    wide = jnp.zeros((batch, wide_rows, mine), bf16)
    for d in range(batch):
        piece = lax.dynamic_slice(widen_weight, (0, (bi ^ d) * mine), (wide_rows, mine))
        if d:
            piece = swap(piece, "batch", d)
        wide = put(wide, piece, bi ^ d)
    wide = wide.reshape(channels, mine)

    grid_w = grid_shape[0, 0]
    grid_h = grid_shape[0, 1]
    row_index = ki * rows + jnp.arange(rows, dtype=jnp.int32)
    row_of = jnp.floor((row_index.astype(f32) + 0.5) / grid_w.astype(f32)).astype(jnp.int32)
    col_of = row_index - row_of * grid_w
    inside = row_index < grid_w * grid_h
    keep_own = inside.astype(f32)[:, None]

    def valid(step_row, step_col):
        return (
            inside
            & (row_of + step_row >= 0)
            & (row_of + step_row < grid_h)
            & (col_of + step_col >= 0)
            & (col_of + step_col < grid_w)
        )[:, None]

    taps = [(tap // 3 - 1, tap % 3 - 1) for tap in range(9)]
    depth_taps = depth_weight.astype(f32)

    def window(ext, step_row, step_col):
        start = margin + step_row * grid_w + step_col
        moved = lax.dynamic_slice_in_dim(ext, start, rows, 0).astype(f32)
        return jnp.where(valid(step_row, step_col), moved, 0.0)

    conved = jnp.zeros((rows, channels), f32)
    for tap, (step_row, step_col) in enumerate(taps):
        conved = conved + window(source_ext, step_row, step_col) * depth_taps[tap]
    conved = jnp.where(inside[:, None], conved + depth_bias.astype(f32), 0.0)
    normed_one, inverse_one = row_norm(conved)
    first_in = jnp.concatenate(gather_batch(normed_one.astype(bf16)), axis=0)

    keep = (row_index.astype(f32)[None, :] < pixels[:, None]).astype(f32).reshape(-1, 1)
    widen_shift = lax.dynamic_slice(widen_bias, (bi * mine,), (mine,)).astype(f32)
    pre_act = mm(first_in, wide, ((1,), (0,))) + widen_shift
    gauss = 0.5 * (1.0 + lax.erf(pre_act * (0.5**0.5)))
    hidden = pre_act * gauss * keep

    def per_latent(cells):
        return jnp.sum(cells.reshape(batch, rows, -1), axis=1)

    order = bi ^ jnp.arange(batch, dtype=jnp.int32)
    place_of = (order[:, None] == jnp.arange(batch, dtype=jnp.int32)[None, :]).astype(f32)

    def total_over_units(cells):
        own = jnp.sum(cells, axis=1)
        natural = jnp.sum(place_of * own[:, None], axis=0)
        summed = sum_over(jnp.broadcast_to(natural[:, None], (batch, 128)), "batch")[:, 0]
        return jnp.sum(place_of * summed[None, :], axis=1)[:, None]

    squares = sum_over(per_latent(hidden * hidden), "blk")
    magnitude = jnp.sqrt(squares + norm_eps)
    mean_mag = total_over_units(magnitude) / units + norm_eps
    relative = magnitude / mean_mag

    def spread(cells):
        return jnp.repeat(cells, rows, axis=0)

    gains = lax.dynamic_slice(response_gain, (0, bi * mine), (2, mine)).astype(f32)
    second_in = (gains[0] * (hidden * spread(relative)) + gains[1] + hidden).astype(bf16)
    branch_part = mm(second_in, narrow_weight, ((1,), (0,)))

    def split(cells):
        return [cells[d * rows : (d + 1) * rows] for d in range(batch)]

    branch = scatter_batch(split(branch_part)) + narrow_bias.astype(f32)
    after_res = lat.astype(f32) + keep_own * branch
    shift_scale = mm(time_embed, time_weight, ((1,), (0,))) + time_bias.astype(f32)
    scale_part = 1.0 + shift_scale[:, :channels]
    modulated = after_res * scale_part + shift_scale[:, channels:]
    normed_two, inverse_two = row_norm(modulated)
    attn_in = jnp.concatenate(gather_batch(normed_two.astype(bf16)), axis=0)

    def project_piece(member):
        pieces = [
            lax.dynamic_slice(
                project_weight,
                (0, third * channels + member * wide_rows + group * span),
                (wide_rows, span),
            )
            for group in range(groups)
            for third in range(3)
        ]
        return jnp.concatenate(pieces, axis=1)

    project = jnp.zeros((batch, wide_rows, 3 * wide_rows), bf16)
    for d in range(batch):
        piece = project_piece(bi ^ d)
        if d:
            piece = swap(piece, "batch", d)
        project = put(project, piece, bi ^ d)
    project = project.reshape(channels, 3 * wide_rows)
    shift_q = lax.dynamic_slice(project_bias, (bi * wide_rows,), (wide_rows,)).astype(f32)
    shift_v = lax.dynamic_slice(project_bias, (channels + bi * wide_rows,), (wide_rows,)).astype(
        f32
    )
    project_shift = jnp.concatenate(
        [
            cells
            for group in range(groups)
            for cells in (
                shift_q[group * span : (group + 1) * span],
                jnp.zeros((span,), f32),
                shift_v[group * span : (group + 1) * span],
            )
        ]
    )

    def slot_of(member):
        return jnp.minimum(member // groups, batch - 1), member % groups

    def to_heads(cells):
        received = []
        for e in range(blk):
            item, group = slot_of(ki ^ e)
            piece = take(take(cells, group), item ^ bi)
            received.append(swap(piece, "blk", e) if e else piece)
        return jnp.concatenate(received, axis=0)

    def to_rows(cells):
        held = jnp.zeros((used + 1, rows, cells.shape[1]), cells.dtype)
        for e in range(blk):
            piece = cells[e * rows : (e + 1) * rows]
            if e:
                piece = swap(piece, "blk", e)
            item, group = slot_of(ki ^ e)
            slot = jnp.where((ki ^ e) < used, group * batch + (item ^ bi), used)
            held = put(held, piece, slot)
        return held[:used].reshape(groups, batch, rows, cells.shape[1])

    item, group = slot_of(ki)
    working = (ki < used).astype(f32)

    soft = jax.nn.silu(text_tokens[0].astype(f32)).astype(bf16)
    soft_mine = []
    for d in range(batch):
        piece = lax.dynamic_slice(soft, (0, (bi ^ d) * clip_rows), (text_count, clip_rows))
        soft_mine.append(swap(piece, "batch", d) if d else piece)
    soft_mine = jnp.stack(soft_mine)
    text_sum = mm(take(soft_mine, item ^ bi), text_weight, ((1,), (0,)))
    for bit in bits_of(batch):
        text_sum = text_sum + swap(text_sum, "batch", bit)
    text_feat = (text_sum + text_bias.astype(f32)).astype(bf16)
    text_proj = (mm(text_feat, project, ((1,), (0,))) + project_shift).astype(bf16)
    text_proj = jnp.stack(
        [text_proj[:, g * 3 * span : (g + 1) * 3 * span] for g in range(groups)]
    )
    text_proj = take(text_proj, group)

    cot_rows = jnp.concatenate(gather_batch(cot), axis=0)
    grad_heads = jnp.stack(
        [
            mm(cot_rows, output_weight[g * span : (g + 1) * span], ((1,), (1,))).astype(bf16)
            for g in range(groups)
        ]
    ).reshape(groups, batch, rows, span)
    grad_heads = to_heads(grad_heads)

    projected = (mm(attn_in, project, ((1,), (0,))) + project_shift).astype(bf16)
    projected = jnp.stack(
        [projected[:, g * 3 * span : (g + 1) * 3 * span] for g in range(groups)]
    ).reshape(groups, batch, rows, 3 * span)
    projected = to_heads(projected)

    own_pixels = take(pixels, item ^ bi)
    seq_rows = jnp.concatenate(
        [((ki ^ e) * rows).astype(f32) + jnp.arange(rows, dtype=f32) for e in range(blk)]
        + [jnp.full((text_count,), -1.0, f32)]
    )
    live = (seq_rows < own_pixels)[None, :]
    keys = jnp.concatenate([projected[:, span : 2 * span], text_proj[:, span : 2 * span]], axis=0)
    values = jnp.concatenate([projected[:, 2 * span :], text_proj[:, 2 * span :]], axis=0)
    heads = []
    for head in range(per):
        cut = slice(head * HDIM, (head + 1) * HDIM)
        heads.append(
            attend(projected[:, cut], keys[:, cut], values[:, cut], grad_heads[:, cut], live)
        )
    attended, dq, dk, dv = (jnp.concatenate(cells, axis=1).astype(bf16) for cells in zip(*heads))
    seq = blk * rows
    dqkv = to_rows(jnp.concatenate([dq, dk[:seq], dv[:seq]], axis=1))
    dqkv = jnp.concatenate(
        [dqkv[g].reshape(batch * rows, 3 * span) for g in range(groups)], axis=1
    )
    attended = to_rows(attended)
    attended = jnp.concatenate(
        [attended[g].reshape(batch * rows, span) for g in range(groups)], axis=1
    )

    dnormed_two = scatter_batch(split(mm(dqkv, project, ((1,), (1,)))))

    att_out = scatter_batch(split(mm(attended, output_weight, ((1,), (0,)))))
    block_output = (modulated + att_out + output_bias.astype(f32)).astype(bf16)
    upstream = cot.astype(f32)
    output_grad = mm(cot_rows, attended, ((0,), (0,))).astype(bf16)
    output_sum = scatter_rows(output_grad.reshape(blk, channels // blk, wide_rows)).T

    dtext_low = jnp.concatenate([jnp.zeros((text_count, span), bf16), dk[seq:], dv[seq:]], axis=1)
    dtext_low = (dtext_low.astype(f32) * working).astype(bf16)
    dtext_cols = jnp.concatenate(
        [
            jnp.where(group == g, dtext_low, jnp.zeros_like(dtext_low))
            for g in range(groups)
        ],
        axis=1,
    )
    dtext_part = mm(dtext_cols, project, ((1,), (1,)))
    natural_items = jnp.arange(batch, dtype=jnp.int32)
    if blk == 2 * batch and groups == 2:
        part = dtext_part
        for axis, distance in (("blk", 1), ("batch", 1), ("batch", 2)):
            low = part.astype(bf16)
            part = low.astype(f32) + swap(low, axis, distance).astype(f32)
        low = part.astype(bf16)
        dtext_all = jnp.zeros((batch, text_count, channels), bf16)
        for d in range(batch):
            piece = swap(low, "blk", 2 * d) if d else low
            dtext_all = put(dtext_all, piece, item ^ d)
    else:
        placed = (natural_items == item).astype(f32)[:, None, None] * dtext_part[None]
        dtext_all = lax.psum(placed, ("batch", "blk")).astype(bf16)
    text_bias_sum = jnp.sum(dtext_all.astype(f32), axis=(0, 1))
    dtext_cut = lax.dynamic_slice(
        dtext_all, (0, 0, ki * (channels // blk)), (batch, text_count, channels // blk)
    )
    soft_natural = jnp.stack([take(soft_mine, l ^ bi) for l in range(batch)])
    text_sum_grad = mm(
        soft_natural.reshape(batch * text_count, clip_rows),
        dtext_cut.reshape(batch * text_count, channels // blk),
        ((0,), (0,)),
    )

    project_grad = mm(attn_in, dqkv, ((0,), (0,))) + mm(text_feat, dtext_cols, ((0,), (0,)))
    project_part = scatter_rows(
        project_grad.astype(bf16).reshape(blk, channels // blk, 3 * wide_rows)
    ).astype(bf16)

    dmodulated = upstream + row_norm_back(normed_two, inverse_two, dnormed_two)
    dshift = jnp.stack([jnp.sum(dmodulated * after_res, axis=0), jnp.sum(dmodulated, axis=0)])
    dafter = dmodulated * scale_part
    dbranch_own = (keep_own * dafter).astype(bf16)
    dbranch = jnp.concatenate(gather_batch(dbranch_own), axis=0)
    dgrn = mm(dbranch, narrow_weight, ((1,), (1,)))
    sums = jnp.concatenate(
        [per_latent(dgrn * hidden), jnp.sum(dgrn, axis=0, keepdims=True)], axis=0
    )
    sums = sum_over(sums, "blk")
    latent_sums = sums[:batch]
    drelative = gains[0] * latent_sums
    gain_rows = jnp.stack([tree_sum((latent_sums * relative)[d] for d in range(batch)), sums[batch]])
    dmagnitude = drelative / mean_mag - total_over_units(drelative * magnitude) / (
        mean_mag * mean_mag * units
    )
    dhidden = dgrn * spread(gains[0] * relative + 1.0) + hidden * spread(dmagnitude / magnitude)
    slope = gauss + pre_act * jnp.exp(-0.5 * pre_act * pre_act) * 0.3989422804014327
    dpre_wide = keep * dhidden * slope
    dpre = dpre_wide.astype(bf16)
    widen_bias_part = jnp.sum(dpre.astype(f32), axis=0)
    dnormed_one = scatter_batch(split(mm(dpre, wide, ((1,), (1,)))))

    widen_grad = mm(first_in, dpre, ((0,), (0,))).astype(bf16)
    widen_part = scatter_rows(widen_grad.reshape(blk, channels // blk, mine)).astype(bf16)
    narrow_grad = mm(dbranch, second_in, ((0,), (0,))).astype(bf16)
    narrow_sum = scatter_rows(narrow_grad.reshape(blk, channels // blk, mine)).T

    width = mine // ring
    widen_held = jnp.zeros((ring, channels // blk, width), bf16)
    cuts = jnp.stack([widen_part[:, j * width : (j + 1) * width] for j in range(ring)])
    for j in range(ring):
        hops = [
            (b * blk + k, (k // ring) * blk + b * ring + ((k % ring) ^ j))
            for b in range(batch)
            for k in range(blk)
        ]
        piece = lax.ppermute(take(cuts, (ki % ring) ^ j), ("batch", "blk"), hops)
        widen_held = put(widen_held, piece, (ki % ring) ^ j)
    widen_sum = widen_held.reshape(wide_rows, width).astype(f32)

    unit_count = 3 * groups
    out_cols = 3 * channels // blk
    units_of = jnp.stack([project_part[:, u * span : (u + 1) * span] for u in range(unit_count)])
    if out_cols % span == 0 and unit_count * ring == ring * ring * (out_cols // span):
        per_out = out_cols // span
        sources, targets, labels = [], [], []
        for b in range(batch):
            for k in range(blk):
                for unit in range(unit_count):
                    place = (unit % 3) * (channels // span) + b * groups + unit // 3
                    sources.append(b * blk + k)
                    targets.append((k // ring) * blk + place // per_out)
                    labels.append((unit, (k % ring) * per_out + place % per_out))
        me = bi * blk + ki
        project_held = jnp.zeros((ring * per_out, channels // blk, span), bf16)
        for matching in colour(sources, targets, unit_count):
            pick = [0] * (batch * blk)
            drop = [0] * (batch * blk)
            for edge in matching:
                pick[sources[edge]], drop[targets[edge]] = labels[edge][0], labels[edge][1]
            hops = [(sources[edge], targets[edge]) for edge in matching]
            piece = take(units_of, jnp.array(pick, jnp.int32)[me])
            piece = lax.ppermute(piece, ("batch", "blk"), hops)
            project_held = put(project_held, piece, jnp.array(drop, jnp.int32)[me])
        project_sum = jnp.concatenate(
            [
                jnp.concatenate([project_held[r * per_out + p] for p in range(per_out)], axis=1)
                for r in range(ring)
            ],
            axis=0,
        )
    else:
        thirds = jnp.stack(
            [
                jnp.concatenate([units_of[3 * g + third] for g in range(groups)], axis=1)
                for third in range(3)
            ]
        )
        thirds = lax.all_gather(thirds, "batch", axis=2, tiled=True)
        thirds = thirds.reshape(3, channels // blk, channels)
        whole = jnp.concatenate([thirds[third] for third in range(3)], axis=1)
        whole = lax.all_to_all(whole, "blk", split_axis=1, concat_axis=0, tiled=True)
        project_sum = lax.dynamic_slice(whole, (bi * wide_rows, 0), (wide_rows, out_cols))
    project_sum = project_sum.astype(f32)

    dconved = keep_own * row_norm_back(normed_one, inverse_one, dnormed_one)
    grad_ext = halo(dconved.astype(bf16), margin)
    dlatent = dafter
    depth_rows = []
    for tap, (step_row, step_col) in enumerate(taps):
        depth_rows.append(jnp.sum(window(source_ext, step_row, step_col) * dconved, axis=0))
        dlatent = dlatent + window(grad_ext, -step_row, -step_col) * depth_taps[tap]
    latent_grad = dlatent.astype(bf16)

    sums_cols = jnp.sum(dqkv.astype(f32), axis=0) + jnp.sum(dtext_cols.astype(f32), axis=0)
    shift_part = jnp.concatenate(
        [
            sums_cols[g * 3 * span + third * span : g * 3 * span + (third + 1) * span]
            for third in (0, 2)
            for g in range(groups)
        ]
    )
    narrow_units = mine
    pad = max(channels, narrow_units, 2 * wide_rows)

    def line(cells):
        return jnp.pad(cells, (0, pad - cells.shape[0]))

    late = jnp.stack(
        [line(dshift[0]), line(dshift[1])]
        + [
            line(cells)
            for cells in [
                jnp.sum(upstream, axis=0),
                jnp.sum(dbranch_own.astype(f32), axis=0),
                jnp.sum(dconved, axis=0),
            ]
            + depth_rows
            + [shift_part, widen_bias_part]
        ]
    )
    late = sum_over(late, "blk")
    late = jnp.concatenate([late, jnp.stack([line(gain_rows[0]), line(gain_rows[1])])], axis=0)
    members = gather_batch(late)
    both = tree_sum(members)
    output_bias_sum = both[2, :channels]
    narrow_bias_sum = both[3, :channels]
    depth_bias_sum = both[4, :channels]
    depth_weight_sum = both[5:14, :channels]
    outer = [
        jnp.concatenate(
            [
                times[d][:, None] * members[d][0, None, :channels],
                times[d][:, None] * members[d][1, None, :channels],
            ],
            axis=1,
        )
        for d in range(batch)
    ]
    time_weight_sum = tree_sum(outer)
    time_bias_sum = tree_sum(
        jnp.concatenate([members[d][0, :channels], members[d][1, :channels]])
        for d in range(batch)
    )
    ordered = jnp.stack([take(jnp.stack(members), l ^ bi) for l in range(batch)])
    project_bias_sum = jnp.concatenate(
        [
            ordered[:, 14, :wide_rows].reshape(-1),
            ordered[:, 14, wide_rows : 2 * wide_rows].reshape(-1),
        ]
    )
    widen_bias_sum = ordered[:, 15, :mine].reshape(-1)
    gain_sum = jnp.stack([ordered[:, 16, :mine].reshape(-1), ordered[:, 17, :mine].reshape(-1)])

    return (
        block_output[None],
        latent_grad[None],
        depth_weight_sum,
        depth_bias_sum,
        widen_sum,
        widen_bias_sum,
        gain_sum,
        narrow_sum,
        narrow_bias_sum,
        time_weight_sum,
        time_bias_sum,
        text_sum_grad,
        text_bias_sum,
        project_sum,
        project_bias_sum,
        output_sum,
        output_bias_sum,
    )


def solution(mesh):
    rows = P("batch", "blk", None)
    first = P("batch", None)
    both = P("batch", "blk")
    everywhere = P()
    placed = (
        rows,
        first,
        P("batch", None, None),
        first,
        everywhere,
        everywhere,
        first,
        everywhere,
        everywhere,
        first,
        everywhere,
        everywhere,
        everywhere,
        first,
        everywhere,
        first,
        everywhere,
        first,
        everywhere,
        rows,
    )
    given = (
        rows,
        rows,
        everywhere,
        everywhere,
        both,
        everywhere,
        everywhere,
        both,
        everywhere,
        everywhere,
        everywhere,
        both,
        everywhere,
        both,
        everywhere,
        both,
        everywhere,
    )
    return jax.shard_map(
        on_device, mesh=mesh, in_specs=placed, out_specs=given, check_vma=False
    )
```

time: 2270 us -> 955 us (0.42)
  the two profiles are of different devices: /device:TPU:9 before, /device:TPU:2 now
where the time goes in v1:
time: 955 us; the launch traced here: 944 us
  waiting for transfers between devices  308 us (32%)
  starting transfers between devices  228 us (24%)
  local copies, waits for them, and re-layouts  221 us (23%)
  other arithmetic  79 us (8%)
  matrix products  69.1 us (7%)
  between operations  39.7 us (4%)
    ppermute x97, waiting for transfers between devices, swap(): return lax.ppermute(cells, axis, [(i, i ^ distance) for i in range(count)])  188 us
    ppermute x97, starting transfers between devices, swap(): return lax.ppermute(cells, axis, [(i, i ^ distance) for i in range(count)])  129 us
    dynamic_update_slice x35, local copies, waits for them, and re-layouts, put(): return lax.dynamic_update_index_in_dim(cells, piece, place, 0)  115 us
    dot_general x37, matrix products, mm(): lax.dot_general(left, right, (dims, ((), ())), preferred_element_type=f32)  69.1 us
    ppermute x12, waiting for transfers between devices, scatter_rows(): up = lax.ppermute(rise, 'blk', senders)  44.7 us
    ppermute x12, starting transfers between devices, scatter_rows(): up = lax.ppermute(rise, 'blk', senders)  43 us
    ppermute x2, waiting for transfers between devices, on_device(): piece = lax.ppermute(take(cuts, ki % ring ^ j), ('batch', 'blk'), hops)  31.9 us
    ppermute x6, starting transfers between devices, on_device(): piece = lax.ppermute(piece, ('batch', 'blk'), hops)  27 us
  transfers between devices with their start and end apart: 133, of which 51 were waited for; matrix products, arithmetic and copies ran while one was open for 35% of the time, Pallas kernels for 0%

profile of v1, /device:TPU:2, one launch (start us, length us, event | category | flops | bytes accessed | tf_op | source)
XLA Modules:
  0.0 943.8 jit_solution(2120279899097952406)
XLA Ops:
  124.1 13.0 %collective-permute-done = bf16[113,1536]{1,0:T(8,128)(2,1)S(1)} collective-permute-done((bf16[113,1536]{1,0:T(8,128)(2,1)}, bf16[113,1536]{1,0:T(8,128)(2,1)S(1)}, u32[]{:S(2)}, u32[]{:S(2)}) %collective-permute-start) | collective-permute-done | bytes 347168 | tf_op jit(solution)/shard_map/ppermute | solution.py:117
  184.8 6.8 collective-permute-start.25
  194.2 34.9 %collective-permute-done.3 = bf16[128,1536]{1,0:T(8,128)(2,1)S(1)} collective-permute-done((bf16[128,1536]{1,0:T(8,128)(2,1)}, bf16[128,1536]{1,0:T(8,128)(2,1)S(1)}, u32[]{:S(2)}, u32[]{:S(2)}) %collective-permute-start.3) | collective-permute-done | bytes 393248 | tf_op jit(solution)/shard_map/ppermute | solution.py:22
  263.4 16.8 %collective-permute-done.16 = f32[4,128]{0,1:T(8,128)S(1)} collective-permute-done((f32[4,128]{0,1:T(8,128)S(1)}, f32[4,128]{0,1:T(8,128)S(1)}, u32[]{:S(2)}, u32[]{:S(2)}) %collective-permute-start.16) | collective-permute-done | bytes 2080 | tf_op jit(solution)/shard_map/ppermute | solution.py:22
  292.6 8.6 collective-permute-done.20
  337.3 11.1 %collective-permute-done.31 = bf16[128,576]{1,0:T(8,128)(2,1)S(1)} collective-permute-done((bf16[128,576]{1,0:T(8,128)(2,1)S(1)}, bf16[128,576]{1,0:T(8,128)(2,1)S(1)}, u32[]{:S(2)}, u32[]{:S(2)}) %collective-permute-start.31) | collective-permute-done | bytes 147488 | tf_op jit(solution)/shard_map/ppermute | solution.py:22
  376.8 6.6 collective-permute-start.40
  401.1 8.7 dynamic_update_slice.131
  478.4 8.7 dynamic_update_slice.132
  487.1 8.7 dynamic_update_slice.133
  495.7 8.7 dynamic_update_slice.134
  504.4 8.7 dynamic_update_slice.135
  513.1 8.7 dynamic_update_slice.136
  521.7 8.7 dynamic_update_slice.137
  530.4 8.8 dynamic_update_slice.138
  660.2 63.8 %collective-permute-done.84 = f32[16,1536]{1,0:T(8,128)S(1)} collective-permute-done((f32[16,1536]{1,0:T(8,128)S(1)}, f32[16,1536]{1,0:T(8,128)S(1)}, u32[]{:S(2)}, u32[]{:S(2)}) %collective-permute-start.84) | collective-permute-done | bytes 98336 | tf_op jit(solution)/shard_map/ppermute | solution.py:22
  768.8 11.9 %collective-permute-done.119 = bf16[192,1152]{1,0:T(8,128)(2,1)S(1)} collective-permute-done((bf16[192,1152]{1,0:T(8,128)(2,1)S(1)}, bf16[192,1152]{1,0:T(8,128)(2,1)S(1)}, u32[]{:S(2)}, u32[]{:S(2)}) %collective-permute-start.119) | collective-permute-done | bytes 442400 | tf_op jit(solution)/shard_map/ppermute | solution.py:95
  782.4 9.1 collective-permute-start.120
  825.8 9.2 collective-permute-done.92
  840.3 7.3 collective-permute-done.101
  852.2 8.0 collective-permute-done.93
  861.3 11.4 %collective-permute-done.102 = bf16[192,1536]{1,0:T(8,128)(2,1)S(1)} collective-permute-done((bf16[192,1536]{1,0:T(8,128)(2,1)S(1)}, bf16[192,1536]{1,0:T(8,128)(2,1)S(1)}, u32[]{:S(2)}, u32[]{:S(2)}) %collective-permute-start.102) | collective-permute-done | bytes 589856 | tf_op jit(solution)/shard_map/ppermute | solution.py:94
  898.2 8.6 collective-permute-start.98
  910.2 26.2 %collective-permute-done.98 = bf16[192,768]{1,0:T(8,128)(2,1)S(1)} collective-permute-done((bf16[192,768]{1,0:T(8,128)(2,1)S(1)}, bf16[192,768]{1,0:T(8,128)(2,1)S(1)}, u32[]{:S(2)}, u32[]{:S(2)}) %collective-permute-start.98) | collective-permute-done | bytes 294944 | tf_op jit(solution)/shard_map/ppermute | solution.py:500
  (1005 shorter events, 581.0 us)
Async XLA Ops:
  3.3 98.0 %collective-permute-start.9 = (f32[1,128]{1,0:T(1,128)}, f32[1,128]{1,0:T(1,128)}, u32[]{:S(2)}, u32[]{:S(2)}) collective-permute-start(f32[1,128]{1,0:T(1,128)} %bitcast_maximum_fusion), channel_id=1, source_target_pairs={{0,16},{8,24},{16,0},{24,8},{1,17},{9,25},{17,1},{25,9},{2,18},{10... | collective-permute-start | bytes 1544 | tf_op jit(solution)/shard_map/ppermute | solution.py:22
  3.3 100.6 %collective-permute-start.8 = (f32[1,128]{1,0:T(1,128)}, f32[1,128]{1,0:T(1,128)}, u32[]{:S(2)}, u32[]{:S(2)}) collective-permute-start(f32[1,128]{1,0:T(1,128)} %bitcast_maximum_fusion), channel_id=1, source_target_pairs={{0,8},{8,0},{16,24},{24,16},{1,9},{9,1},{17,25},{25,17},{2,10},{10... | collective-permute-start | bytes 1544 | tf_op jit(solution)/shard_map/ppermute | solution.py:22
  3.3 137.5 %collective-permute-start.50 = (bf16[128,1536]{1,0:T(8,128)(2,1)}, bf16[128,1536]{1,0:T(8,128)(2,1)}, u32[]{:S(2)}, u32[]{:S(2)}) collective-permute-start(bf16[128,1536]{1,0:T(8,128)(2,1)} %bitcast.452), channel_id=1, source_target_pairs={{0,16},{8,24},{16,0},{24,8},{1,17},{9,25},{17,1},{25,9},{2,18},{10... | collective-permute-start | bytes 1179656 | tf_op jit(solution)/shard_map/ppermute | solution.py:22
  5.4 143.9 %collective-permute-start.49 = (bf16[128,1536]{1,0:T(8,128)(2,1)}, bf16[128,1536]{1,0:T(8,128)(2,1)}, u32[]{:S(2)}, u32[]{:S(2)}) collective-permute-start(bf16[128,1536]{1,0:T(8,128)(2,1)} %bitcast.453), channel_id=1, source_target_pairs={{0,8},{8,0},{16,24},{24,16},{1,9},{9,1},{17,25},{25,17},{2,10},{10... | collective-permute-start | bytes 1179656 | tf_op jit(solution)/shard_map/ppermute | solution.py:22
  7.5 109.5 %collective-permute-start.34 = (bf16[77,320]{1,0:T(8,128)(2,1)}, bf16[77,320]{1,0:T(8,128)(2,1)}, u32[]{:S(2)}, u32[]{:S(2)}) collective-permute-start(bf16[77,320]{1,0:T(8,128)(2,1)} %get-tuple-element.218), channel_id=1, source_target_pairs={{0,8},{8,0},{16,24},{24,16},{1,9},{9,1},{17,25},{25,17},{2,10},{10... | collective-permute-start | bytes 147848 | tf_op jit(solution)/shard_map/ppermute | solution.py:22
  117.0 142.5 %collective-permute-start.24 = (bf16[384,1152]{1,0:T(8,128)(2,1)}, bf16[384,1152]{1,0:T(8,128)(2,1)}, u32[]{:S(2)}, u32[]{:S(2)}) collective-permute-start(bf16[384,1152]{1,0:T(8,128)(2,1)} %concatenate.152), channel_id=1, source_target_pairs={{0,8},{8,0},{16,24},{24,16},{1,9},{9,1},{17,25},{25,17},{2,10},{10... | collective-permute-start | bytes 2654216 | tf_op jit(solution)/shard_map/ppermute | solution.py:22
  137.1 54.5 %collective-permute-start.5 = (bf16[384,1536]{1,0:T(8,128)(2,1)}, bf16[384,1536]{1,0:T(8,128)(2,1)}, u32[]{:S(2)}, u32[]{:S(2)}) collective-permute-start(bf16[384,1536]{1,0:T(8,128)(2,1)} %get-tuple-element.90), channel_id=1, source_target_pairs={{0,8},{8,0},{16,24},{24,16},{1,9},{9,1},{17,25},{25,17},{2,10},{10... | collective-permute-start | bytes 3538952 | tf_op jit(solution)/shard_map/ppermute | solution.py:22
  148.2 80.9 %collective-permute-start.6 = (bf16[384,1536]{1,0:T(8,128)(2,1)}, bf16[384,1536]{1,0:T(8,128)(2,1)}, u32[]{:S(2)}, u32[]{:S(2)}) collective-permute-start(bf16[384,1536]{1,0:T(8,128)(2,1)} %get-tuple-element.91), channel_id=1, source_target_pairs={{0,16},{8,24},{16,0},{24,8},{1,17},{9,25},{17,1},{25,9},{2,18},{10... | collective-permute-start | bytes 3538952 | tf_op jit(solution)/shard_map/ppermute | solution.py:22
  149.2 82.8 %collective-permute-start.7 = (bf16[384,1536]{1,0:T(8,128)(2,1)}, bf16[384,1536]{1,0:T(8,128)(2,1)}, u32[]{:S(2)}, u32[]{:S(2)}) collective-permute-start(bf16[384,1536]{1,0:T(8,128)(2,1)} %get-tuple-element.89), channel_id=1, source_target_pairs={{0,24},{8,16},{16,8},{24,0},{1,25},{9,17},{17,9},{25,1},{2,26},{10... | collective-permute-start | bytes 3538952 | tf_op jit(solution)/shard_map/ppermute | solution.py:22
  184.8 103.5 %collective-permute-start.25 = (bf16[384,1152]{1,0:T(8,128)(2,1)}, bf16[384,1152]{1,0:T(8,128)(2,1)S(1)}, u32[]{:S(2)}, u32[]{:S(2)}) collective-permute-start(bf16[384,1152]{1,0:T(8,128)(2,1)} %concatenate.153), channel_id=1, source_target_pairs={{0,16},{8,24},{16,0},{24,8},{1,17},{9,25},{17,1},{25,9},{2,18},{10... | collective-permute-start | bytes 2654216 | tf_op jit(solution)/shard_map/ppermute | solution.py:22
  262.9 41.0 %collective-permute-start.38 = (f32[77,1536]{1,0:T(8,128)}, f32[77,1536]{1,0:T(8,128)S(1)}, u32[]{:S(2)}, u32[]{:S(2)}) collective-permute-start(f32[77,1536]{1,0:T(8,128)} %add.1654), channel_id=1, source_target_pairs={{0,16},{8,24},{16,0},{24,8},{1,17},{9,25},{17,1},{25,9},{2,18},{10... | collective-permute-start | bytes 1419272 | tf_op jit(solution)/shard_map/ppermute | solution.py:22
  410.8 46.0 %collective-permute-start.59 = (bf16[128,576]{0,1:T(8,128)(2,1)}, bf16[128,576]{0,1:T(8,128)(2,1)}, u32[]{:S(2)}, u32[]{:S(2)}) collective-permute-start(bf16[128,576]{0,1:T(8,128)(2,1)} %get-tuple-element.153), channel_id=1, source_target_pairs={{0,1},{1,0},{2,3},{3,2},{4,5},{5,4},{6,7},{7,6},{8,9},{9,8},{10,11... | collective-permute-start | bytes 442376 | tf_op jit(solution)/shard_map/ppermute | solution.py:22
  413.2 46.0 %collective-permute-start.60 = (bf16[128,576]{0,1:T(8,128)(2,1)}, bf16[128,576]{0,1:T(8,128)(2,1)}, u32[]{:S(2)}, u32[]{:S(2)}) collective-permute-start(bf16[128,576]{0,1:T(8,128)(2,1)} %get-tuple-element.152), channel_id=1, source_target_pairs={{0,2},{1,3},{2,0},{3,1},{4,6},{5,7},{6,4},{7,5},{8,10},{9,11},{10,... | collective-permute-start | bytes 442376 | tf_op jit(solution)/shard_map/ppermute | solution.py:22
  414.3 54.1 %collective-permute-start.61 = (bf16[128,576]{0,1:T(8,128)(2,1)}, bf16[128,576]{0,1:T(8,128)(2,1)}, u32[]{:S(2)}, u32[]{:S(2)}) collective-permute-start(bf16[128,576]{0,1:T(8,128)(2,1)} %get-tuple-element.151), channel_id=1, source_target_pairs={{0,3},{1,2},{2,1},{3,0},{4,7},{5,6},{6,5},{7,4},{8,11},{9,10},{10,... | collective-permute-start | bytes 442376 | tf_op jit(solution)/shard_map/ppermute | solution.py:22
  417.7 54.0 %collective-permute-start.62 = (bf16[128,576]{0,1:T(8,128)(2,1)}, bf16[128,576]{0,1:T(8,128)(2,1)}, u32[]{:S(2)}, u32[]{:S(2)}) collective-permute-start(bf16[128,576]{0,1:T(8,128)(2,1)} %get-tuple-element.150), channel_id=1, source_target_pairs={{0,4},{1,5},{2,6},{3,7},{4,0},{5,1},{6,2},{7,3},{8,12},{9,13},{10,... | collective-permute-start | bytes 442376 | tf_op jit(solution)/shard_map/ppermute | solution.py:22
  420.4 53.8 %collective-permute-start.63 = (bf16[128,576]{0,1:T(8,128)(2,1)}, bf16[128,576]{0,1:T(8,128)(2,1)}, u32[]{:S(2)}, u32[]{:S(2)}) collective-permute-start(bf16[128,576]{0,1:T(8,128)(2,1)} %get-tuple-element.149), channel_id=1, source_target_pairs={{0,5},{1,4},{2,7},{3,6},{4,1},{5,0},{6,3},{7,2},{8,13},{9,12},{10,... | collective-permute-start | bytes 442376 | tf_op jit(solution)/shard_map/ppermute | solution.py:22
  468.4 81.6 %collective-permute-start.107 = (bf16[77,1536]{1,0:T(8,128)(2,1)S(1)}, bf16[77,1536]{1,0:T(8,128)(2,1)}, u32[]{:S(2)}, u32[]{:S(2)}) collective-permute-start(bf16[77,1536]{1,0:T(8,128)(2,1)S(1)} %copy-done.27), channel_id=1, source_target_pairs={{0,1},{1,0},{2,3},{3,2},{4,5},{5,4},{6,7},{7,6},{8,9},{9,8},{10,11... | collective-permute-start | bytes 709640 | tf_op jit(solution)/shard_map/ppermute | solution.py:22
  471.7 83.4 %collective-permute-start.126 = (bf16[4,192,384]{2,1,0:T(8,128)(2,1)}, bf16[4,192,384]{2,1,0:T(8,128)(2,1)}, u32[]{:S(2)}, u32[]{:S(2)}) collective-permute-start(bf16[4,192,384]{2,1,0:T(8,128)(2,1)} %dynamic-slice_bitcast_fusion.3), channel_id=1, source_target_pairs={{0,1},{1,0},{2,3},{3,2},{4,5},{5,4},{6,7},{7,6},{8,9},{9,8},{10,11... | collective-permute-start | bytes 1769480 | tf_op jit(solution)/shard_map/ppermute | solution.py:22
  474.1 77.8 %collective-permute-start.47 = (bf16[128,1536]{1,0:T(8,128)(2,1)}, bf16[128,1536]{1,0:T(8,128)(2,1)}, u32[]{:S(2)}, u32[]{:S(2)}) collective-permute-start(bf16[128,1536]{1,0:T(8,128)(2,1)} %get-tuple-element.135), channel_id=1, source_target_pairs={{0,8},{8,0},{16,24},{24,16},{1,9},{9,1},{17,25},{25,17},{2,10},{10... | collective-permute-start | bytes 1179656 | tf_op jit(solution)/shard_map/ppermute | solution.py:22
  476.0 96.6 %collective-permute-start.46 = (bf16[128,1536]{1,0:T(8,128)(2,1)}, bf16[128,1536]{1,0:T(8,128)(2,1)}, u32[]{:S(2)}, u32[]{:S(2)}) collective-permute-start(bf16[128,1536]{1,0:T(8,128)(2,1)} %get-tuple-element.134), channel_id=1, source_target_pairs={{0,8},{8,0},{16,24},{24,16},{1,9},{9,1},{17,25},{25,17},{2,10},{10... | collective-permute-start | bytes 1179656 | tf_op jit(solution)/shard_map/ppermute | solution.py:22
  566.4 78.2 %collective-permute-start.113 = (bf16[4,192,1152]{2,1,0:T(8,128)(2,1)S(1)}, bf16[4,192,1152]{2,1,0:T(8,128)(2,1)S(1)}, u32[]{:S(2)}, u32[]{:S(2)}) collective-permute-start(bf16[4,192,1152]{2,1,0:T(8,128)(2,1)S(1)} %dynamic-slice_bitcast_fusion.2), channel_id=1, source_target_pairs={{0,1},{1,0},{2,3},{3,2},{4,5},{5,4},{6,7},{7,6},{8,9},{9,8},{10,11... | collective-permute-start | bytes 5308424 | tf_op jit(solution)/shard_map/ppermute | solution.py:22
  619.5 201.8 %collective-permute-start.100 = (bf16[4,192,1536]{2,1,0:T(8,128)(2,1)}, bf16[4,192,1536]{2,1,0:T(8,128)(2,1)}, u32[]{:S(2)}, u32[]{:S(2)}) collective-permute-start(bf16[4,192,1536]{2,1,0:T(8,128)(2,1)} %dynamic-slice_bitcast_fusion), channel_id=1, source_target_pairs={{0,1},{1,0},{2,3},{3,2},{4,5},{5,4},{6,7},{7,6},{8,9},{9,8},{10,11... | collective-permute-start | bytes 7077896 | tf_op jit(solution)/shard_map/ppermute | solution.py:22
  641.8 175.0 %collective-permute-start.91 = (bf16[4,192,1536]{2,1,0:T(8,128)(2,1)}, bf16[4,192,1536]{2,1,0:T(8,128)(2,1)}, u32[]{:S(2)}, u32[]{:S(2)}) collective-permute-start(bf16[4,192,1536]{2,1,0:T(8,128)(2,1)} %dynamic-slice_bitcast_fusion.1), channel_id=1, source_target_pairs={{0,1},{1,0},{2,3},{3,2},{4,5},{5,4},{6,7},{7,6},{8,9},{9,8},{10,11... | collective-permute-start | bytes 7077896 | tf_op jit(solution)/shard_map/ppermute | solution.py:22
  658.0 66.0 %collective-permute-start.84 = (f32[16,1536]{1,0:T(8,128)S(1)}, f32[16,1536]{1,0:T(8,128)S(1)}, u32[]{:S(2)}, u32[]{:S(2)}) collective-permute-start(f32[16,1536]{1,0:T(8,128)S(1)} %stack.222), channel_id=1, source_target_pairs={{0,1},{1,0},{2,3},{3,2},{4,5},{5,4},{6,7},{7,6},{8,9},{9,8},{10,11... | collective-permute-start | bytes 294920 | tf_op jit(solution)/shard_map/ppermute | solution.py:22
  (303 other events, 4985.1 us)

commit v2 on v1

v2 whole, which is shorter than its diff:
```python
import jax
import jax.numpy as jnp
from jax import lax
from jax.sharding import PartitionSpec as P

HEADS = 24
HDIM = 64
WIDE = 112

norm_eps = 1e-06
masked_score = -1e30
f32 = jnp.float32
bf16 = jnp.bfloat16


def mm(left, right, dims):
    return lax.dot_general(left, right, (dims, ((), ())), preferred_element_type=f32)


def swap(cells, axis, distance):
    count = lax.axis_size(axis)
    return lax.ppermute(cells, axis, [(i, i ^ distance) for i in range(count)])


def bits_of(count):
    return [1 << n for n in range(count.bit_length() - 1)]


def batch_pair(cells):
    if lax.axis_size("batch") == 4:
        return jnp.stack([cells, swap(cells, "batch", 2)])
    return cells[None]


def batch_all(pair):
    count = lax.axis_size("batch")
    if count == 4:
        mate = swap(pair, "batch", 1)
        return jnp.concatenate([pair[0], mate[0], pair[1], mate[1]], axis=0)
    return jnp.concatenate(
        [pair[0]] + [swap(pair[0], "batch", d) for d in range(1, count)], axis=0
    )


def gather_batch(cells):
    return batch_all(batch_pair(cells))


def gate(*arrays):
    return lax.optimization_barrier(arrays)


def scatter_batch(parts, sent=None, held=()):
    if len(parts) == 4:
        mate = swap(jnp.stack([parts[1], parts[3]]).astype(bf16), "batch", 1)
        far = (parts[2] + mate[1].astype(f32)).astype(bf16)
        if sent is not None:
            sent.extend(gate(far, *held))
            far = sent[0]
        return parts[0] + mate[0].astype(f32) + swap(far, "batch", 2).astype(f32)
    if sent is not None:
        sent.extend(gate(parts[0], *held))
    held = dict(enumerate(parts))
    for bit in bits_of(len(parts)):
        held = {
            place: cells + swap(held[place ^ bit].astype(bf16), "batch", bit).astype(f32)
            for place, cells in held.items()
            if not place & bit
        }
    return held[0]


class Relay:
    def __init__(self, piece, distance):
        me = lax.axis_index("batch")
        self.piece, self.distance = piece, distance
        self.side = (lax.axis_index("blk") // distance) % 2
        self.whole = lax.axis_size("batch") == 4
        self.pieces = [piece(me)]
        self.held = []

    def part(self, member):
        cells = self.piece(member)
        rows = cells.shape[0] // 2
        return lax.dynamic_slice_in_dim(cells, self.side * rows, rows, 0)

    def near(self, *then):
        if not self.whole:
            self.pieces = exchange_batch(self.piece)
            return
        me = lax.axis_index("batch")
        self.pieces.append(swap(after(self.piece(me ^ 1), *then), "batch", 1))

    def far(self, *then):
        if self.whole:
            me = lax.axis_index("batch")
            cells = jnp.stack([self.part(me ^ 2), self.part(me ^ 3)])
            self.held = [swap(after(cells, *then), "batch", 2)]

    def hand_on(self, *then):
        if self.whole:
            cells = after(self.held[0], *then)
            self.held = [cells, swap(cells, "blk", self.distance)]

    def gate(self, value):
        value, *self.held = gate(value, *self.held)
        return value

    def finish(self, *then):
        if self.whole:
            cells, other = self.held
            cells = after(cells, *then)
            low = jnp.where(self.side == 0, cells, other)
            high = jnp.where(self.side == 0, other, cells)
            cells = jnp.concatenate([low, high], axis=1)
            self.pieces = self.pieces + [cells[0], swap(cells[1], "batch", 1)]
        return self.pieces


def exchange_batch(piece):
    me, count = lax.axis_index("batch"), lax.axis_size("batch")
    return [piece(me)] + [swap(piece(me ^ d), "batch", d) for d in range(1, count)]


def tree_sum(pieces):
    pieces = list(pieces)
    while len(pieces) > 1:
        pieces = [pieces[i] + pieces[i + 1] for i in range(0, len(pieces), 2)]
    return pieces[0]


def sum_over(cells, axis):
    count = lax.axis_size(axis)
    if axis == "blk" and count == 8:
        cells = cells + swap(cells, axis, 1)
        return tree_sum([cells] + [swap(cells, axis, d) for d in (2, 4, 6)])
    if count <= 4:
        return tree_sum([cells] + [swap(cells, axis, d) for d in range(1, count)])
    for bit in bits_of(count):
        cells = cells + swap(cells, axis, bit)
    return cells


def after(cells, *others):
    return lax.optimization_barrier((cells,) + others)[0]


def choose(pieces, place):
    if len(pieces) == 2:
        return jnp.where(place == 0, pieces[0], pieces[1])
    return lax.dynamic_index_in_dim(jnp.stack(pieces), place, 0, keepdims=False)


def row_norm(field_rows):
    average = jnp.mean(field_rows, axis=-1, keepdims=True)
    centred = field_rows - average
    spread = jnp.mean(centred * centred, axis=-1, keepdims=True)
    inverse = lax.rsqrt(spread + norm_eps)
    return (centred * inverse, inverse)


def row_norm_back(normed, inverse, upstream):
    first_mean = jnp.mean(upstream, axis=-1, keepdims=True)
    second_mean = jnp.mean(upstream * normed, axis=-1, keepdims=True)
    return inverse * (upstream - first_mean - normed * second_mean)


def attend(queries, keys, values, grad_heads, live):
    scores = mm(queries, keys, ((1,), (1,))) * 0.125
    scores = jnp.where(live, scores, masked_score)
    raised = jnp.exp(scores - jnp.max(scores, axis=1, keepdims=True))
    shares = raised / jnp.sum(raised, axis=1, keepdims=True)
    shares_low = shares.astype(bf16)
    attended = mm(shares_low, values, ((1,), (0,)))
    delta = jnp.sum(grad_heads.astype(f32) * attended, axis=1, keepdims=True)
    dshares = mm(grad_heads, values, ((1,), (1,)))
    dscores = (shares * (dshares - delta)).astype(bf16)
    return (
        attended,
        mm(dscores, keys, ((1,), (0,))) * 0.125,
        mm(dscores, queries, ((0,), (0,))) * 0.125,
        mm(shares_low, grad_heads, ((0,), (0,))),
    )


def on_device(
    latent,
    time_embed,
    text_tokens,
    grid_shape,
    depth_weight,
    depth_bias,
    widen_weight,
    widen_bias,
    response_gain,
    narrow_weight,
    narrow_bias,
    time_weight,
    time_bias,
    text_weight,
    text_bias,
    project_weight,
    project_bias,
    output_weight,
    output_bias,
    cotangent,
):
    _, rows, channels = latent.shape
    batch, blk = lax.axis_size("batch"), lax.axis_size("blk")
    bi, ki = lax.axis_index("batch"), lax.axis_index("blk")
    ring = blk // batch
    plane, lane = ki // ring, ki % ring
    units = widen_weight.shape[1]
    mine = units // batch
    wide_rows = channels // batch
    own_heads = HEADS // batch
    per = -(-own_heads // ring)
    span = per * HDIM
    clip_rows = text_weight.shape[0]
    text_count = text_tokens.shape[1]
    half = batch * rows
    grid = [(b, p, l) for b in range(batch) for p in range(batch) for l in range(ring)]

    def spot(b, p, l):
        return b * blk + p * ring + l

    turned = [(spot(b, p, l), spot(p, b, l)) for b, p, l in grid]

    def turn(cells):
        return lax.ppermute(cells, ("batch", "blk"), turned)

    def lanes(cells):
        return [swap(cells[e - 1], "blk", e) for e in range(1, ring)]

    def by_lane(pieces):
        return [choose(pieces, lane ^ e) for e in range(ring)]

    def halo(cells, margin):
        order = [[spot(b, p, l) for b in range(batch) for l in range(ring)] for p in range(batch)]
        up = [(line[i], line[i + 1]) for line in order for i in range(len(line) - 1)]
        before = lax.ppermute(cells[rows - margin :], ("batch", "blk"), up)
        behind = lax.ppermute(cells[:margin], ("batch", "blk"), [(j, i) for i, j in up])
        return jnp.concatenate([before, cells, behind], axis=0)

    def over_planes(shards):
        members = [[p * ring + l for p in range(batch)] for l in range(ring)]
        return lax.psum_scatter(
            shards, "blk", scatter_dimension=0, tiled=False, axis_index_groups=members
        ).astype(f32)

    first_lane = (lane == 0).astype(f32)
    margin = WIDE + 1
    lat = turn(latent[0])
    facts = turn(
        jnp.concatenate(
            [
                grid_shape.astype(f32),
                time_embed.astype(f32),
                jnp.zeros((1, 126 - time_embed.shape[1]), f32),
            ],
            axis=1,
        )
    )
    source_ext = halo(lat, margin)

    def by_member(pieces):
        held = jnp.zeros((batch,) + pieces[0].shape, bf16)
        for d, piece in enumerate(pieces):
            held = lax.dynamic_update_index_in_dim(held, piece, bi ^ d, 0)
        return held.reshape((-1,) + pieces[0].shape[1:])

    def widen_piece(member):
        return lax.dynamic_slice(widen_weight, (0, member * mine), (wide_rows, mine))

    wide_relay = Relay(widen_piece, ring)
    wide_relay.far()
    wide_relay.near()
    source_ext = wide_relay.gate(source_ext)
    wide_relay.hand_on()
    wide_pieces = wide_relay.finish()

    def grouped(cells):
        extra = ring * span - wide_rows
        if extra:
            cells = [jnp.pad(part, ((0, 0), (0, extra))) for part in cells]
        return [
            jnp.concatenate([part[:, g * span : (g + 1) * span] for part in cells], axis=1)
            for g in range(ring)
        ]

    project_given = after(project_weight, lat)

    def project_piece(member):
        pieces = [
            lax.dynamic_slice(
                project_given, (0, third * channels + member * wide_rows), (wide_rows,) * 2
            )
            for third in range(3)
        ]
        return jnp.concatenate(by_lane(grouped(pieces)), axis=1)

    project_relay = Relay(project_piece, ring)
    project_relay.near()
    project_relay.far()

    grid_w = facts[0, 0].astype(jnp.int32)
    grid_h = facts[0, 1].astype(jnp.int32)
    pixels = grid_w * grid_h
    time_own = facts[:, 2 : 2 + time_embed.shape[1]]

    def rows_of(member_batch, member_lane):
        return (member_batch * ring + member_lane) * rows + jnp.arange(rows, dtype=jnp.int32)

    row_index = rows_of(bi, lane)
    row_of = jnp.floor((row_index.astype(f32) + 0.5) / facts[0, 0]).astype(jnp.int32)
    col_of = row_index - row_of * grid_w
    inside = row_index < pixels
    keep_own = inside.astype(f32)[:, None]

    def valid(step_row, step_col):
        return (
            inside
            & (row_of + step_row >= 0)
            & (row_of + step_row < grid_h)
            & (col_of + step_col >= 0)
            & (col_of + step_col < grid_w)
        )[:, None]

    taps = [(tap // 3 - 1, tap % 3 - 1) for tap in range(9)]
    depth_taps = depth_weight.astype(f32)

    def window(ext, step_row, step_col):
        start = margin + step_row * grid_w + step_col
        moved = lax.dynamic_slice_in_dim(ext, start, rows, 0).astype(f32)
        return jnp.where(valid(step_row, step_col), moved, 0.0)

    conved = jnp.zeros((rows, channels), f32)
    for tap, (step_row, step_col) in enumerate(taps):
        conved = conved + window(source_ext, step_row, step_col) * depth_taps[tap]
    conved = jnp.where(inside[:, None], conved + depth_bias.astype(f32), 0.0)
    normed_one, inverse_one = row_norm(conved)
    first_low = normed_one.astype(bf16)
    first_pair = batch_pair(first_low)
    first_in = batch_all(first_pair)
    first_in = project_relay.gate(first_in)
    project_relay.hand_on(first_in)
    (
        widen_bias,
        response_gain,
        narrow_bias,
        time_weight,
        time_bias,
        text_tokens,
        text_bias,
        project_weight,
        project_bias,
        output_weight,
        output_bias,
        _,
    ) = lax.optimization_barrier(
        (
            widen_bias,
            response_gain,
            narrow_bias,
            time_weight,
            time_bias,
            text_tokens,
            text_bias,
            project_weight,
            project_bias,
            output_weight,
            output_bias,
            first_low,
        )
    )

    half_rows = jnp.concatenate([rows_of(bi ^ d, lane) for d in range(batch)])
    keep = (half_rows < pixels).astype(f32)[:, None]
    widen_shift = lax.dynamic_slice(widen_bias, (bi * mine,), (mine,)).astype(f32)
    pre_act = widen_shift
    for d, piece in enumerate(wide_pieces):
        cells = lax.dynamic_slice(first_in, (0, (bi ^ d) * wide_rows), (half, wide_rows))
        pre_act = pre_act + mm(cells, piece, ((1,), (0,)))
    gauss = 0.5 * (1.0 + lax.erf(pre_act * (0.5**0.5)))
    hidden = pre_act * gauss * keep

    def total(cells):
        own = jnp.broadcast_to(jnp.sum(cells, axis=1, keepdims=True), (1, 128))
        return sum_over(own, "batch")[:, :1]

    def lane_sum(cells):
        bit = 1
        while bit < ring:
            cells = cells + swap(cells, "blk", bit)
            bit *= 2
        return cells

    shift_q = lax.dynamic_slice(project_bias, (bi * wide_rows,), (wide_rows,)).astype(f32)
    shift_v = lax.dynamic_slice(project_bias, (channels + bi * wide_rows,), (wide_rows,)).astype(
        f32
    )
    project_shift = jnp.concatenate(
        by_lane(grouped([shift_q[None], jnp.zeros((1, wide_rows), f32), shift_v[None]])), axis=1
    )
    squares = lane_sum(jnp.sum(hidden * hidden, axis=0, keepdims=True))
    magnitude = jnp.sqrt(squares + norm_eps)
    mean_mag = total(magnitude) / units + norm_eps
    mean_mag = project_relay.gate(mean_mag)
    first_sent = [swap(after(first_pair[0], squares), "blk", e) for e in range(1, ring)]
    mean_mag, *first_sent = gate(mean_mag, *first_sent)
    relative = magnitude / mean_mag

    gains = lax.dynamic_slice(response_gain, (0, bi * mine), (2, mine)).astype(f32)
    second_in = (gains[:1] * (hidden * relative) + gains[1:] + hidden).astype(bf16)
    branch_part = mm(second_in, narrow_weight, ((1,), (0,)))
    def split(cells):
        return [cells[d * rows : (d + 1) * rows] for d in range(batch)]

    cot = turn(after(cotangent[0], mean_mag))
    first_rest = []
    if batch == 4:
        first_rest = [swap(after(first_pair[1], second_in), "blk", e) for e in range(1, ring)]
    leaving = []
    branch = scatter_batch(split(branch_part), leaving, [cot])
    cot = leaving[1]
    branch, *first_rest = gate(branch, *first_rest)
    if batch == 4:
        first_sent = [jnp.stack(pair) for pair in zip(first_sent, first_rest)]
    else:
        first_sent = [cells[None] for cells in first_sent]
    branch = branch + narrow_bias.astype(f32)
    after_res = lat.astype(f32) + keep_own * branch
    shift_scale = mm(time_own.astype(bf16), time_weight, ((1,), (0,))) + time_bias.astype(f32)
    scale_part = 1.0 + shift_scale[:, :channels]
    modulated = after_res * scale_part + shift_scale[:, channels:]
    normed_two, inverse_two = row_norm(modulated)
    attn_low = normed_two.astype(bf16)
    attn_pair = batch_pair(attn_low)
    attn_in = batch_all(attn_pair)
    project_pieces = project_relay.finish(mean_mag)
    projected = project_shift
    for d, piece in enumerate(project_pieces):
        cells = lax.dynamic_slice(attn_in, (0, (bi ^ d) * wide_rows), (half, wide_rows))
        projected = projected + mm(cells, piece, ((1,), (0,)))
    projected = projected.astype(bf16)
    project = by_member([after(piece, projected) for piece in project_pieces])
    first_others = [batch_all(after(cells, projected)) for cells in first_sent]

    output_groups = [output_weight[g * span : (g + 1) * span] for g in range(ring)]
    output_groups = [
        jnp.pad(cells, ((0, span - cells.shape[0]), (0, 0))) for cells in output_groups
    ]
    output_own = jnp.concatenate(by_lane(output_groups), axis=0)

    cot_pair = batch_pair(after(cot, projected))
    cot_rows = batch_all(cot_pair)
    grad_heads = mm(cot_rows, output_own, ((1,), (1,))).astype(bf16)

    def cut(cells, width):
        return [cells[:, e * width : (e + 1) * width] for e in range(ring)]

    def to_heads(cells, width):
        pieces = cut(cells, width)
        return jnp.concatenate([pieces[0]] + lanes(pieces[1:]), axis=0)

    shard = channels // blk

    def lane_columns(cells):
        pieces = [
            jnp.concatenate(
                [
                    cells[..., (p * ring + g) * shard : (p * ring + g + 1) * shard]
                    for p in range(batch)
                ],
                axis=-1,
            )
            for g in range(ring)
        ]
        return by_lane(pieces)

    grad_heads = to_heads(grad_heads, span)

    tokens = lax.dynamic_slice(text_tokens[0], (0, plane * clip_rows), (text_count, clip_rows))
    tokens = turn(after(tokens, first_in))
    soft = jax.nn.silu(tokens.astype(f32)).astype(bf16)
    text_sum = mm(after(soft, second_in), text_weight, ((1,), (0,)))
    for bit in bits_of(batch):
        low = text_sum.astype(bf16)
        low = after(low, projected) if bit > 1 else low
        text_sum = low.astype(f32) + swap(low, "batch", bit).astype(f32)
    text_feat = (text_sum + text_bias.astype(f32)).astype(bf16)
    project_own = project[:, : 3 * span]
    text_proj = (mm(text_feat, project_own, ((1,), (0,))) + project_shift[:, : 3 * span]).astype(
        bf16
    )

    projected = to_heads(projected, 3 * span)
    attn_sent = [swap(after(attn_pair, projected), "blk", e) for e in range(1, ring)]

    projected, grad_heads = gate(projected, grad_heads)
    seq = ring * half
    seq_rows = jnp.concatenate(
        [rows_of(bi ^ d, lane ^ e) for e in range(ring) for d in range(batch)]
        + [jnp.full((text_count,), -1, jnp.int32)]
    )
    live = (seq_rows < pixels)[None, :]
    keys = jnp.concatenate([projected[:, span : 2 * span], text_proj[:, span : 2 * span]], axis=0)
    values = jnp.concatenate([projected[:, 2 * span :], text_proj[:, 2 * span :]], axis=0)
    heads = []
    for head in range(per):
        at = slice(head * HDIM, (head + 1) * HDIM)
        heads.append(attend(projected[:, at], keys[:, at], values[:, at], grad_heads[:, at], live))
        if head == per // 2:
            key_cells, *attn_sent = gate(heads[-1][2], *attn_sent)
            heads[-1] = heads[-1][:2] + (key_cells,) + heads[-1][3:]
    attended, dq, dk, dv = (jnp.concatenate(cells, axis=1).astype(bf16) for cells in zip(*heads))
    dqkv_seq = jnp.concatenate([dq, dk[:seq], dv[:seq]], axis=1)
    cot_sent = [
        swap(cells, "blk", e)
        for e, cells in enumerate(lane_columns(after(cot_pair, grad_heads))[1:], 1)
    ]
    dqkv_seq, *cot_sent = gate(dqkv_seq, *cot_sent)
    cot_lanes = [batch_all(after(cells, dqkv_seq)) for cells in cot_sent]
    sent = [dqkv_seq[e * half : (e + 1) * half] for e in range(ring)]
    dq_sent = lanes([cells[:, :span] for cells in sent[1:]])
    then_sent = lanes([cells[:, span:] for cells in sent[1:]])
    dqkv = [sent[0]]
    for first_cells, then_cells in zip(dq_sent, then_sent):
        dqkv = dqkv + [first_cells, then_cells]
    dqkv = jnp.concatenate(dqkv, axis=1)
    attended_sent = lanes([after(attended, dq_sent[0])] * (ring - 1))
    attn_others = [batch_all(after(cells, dqkv)) for cells in attn_sent]
    quarter = half // 4
    seconds = [second_in[n * quarter : (n + 1) * quarter] for n in range(4)]
    leaving = []
    dnormed_part = mm(dqkv, project, ((1,), (1,)))
    dnormed_two = scatter_batch(split(dnormed_part), leaving)
    second_sent = [lanes([after(seconds[0], leaving[0])] * (ring - 1))]
    dtext_low = jnp.concatenate([jnp.zeros((text_count, span), bf16), dk[seq:], dv[seq:]], axis=1)
    attn_all = jnp.concatenate([after(attn_in, *leaving)] + attn_others, axis=0)
    project_grad = mm(attn_all, dqkv_seq, ((0,), (0,))) + mm(text_feat, dtext_low, ((0,), (0,)))
    project_grad = project_grad.astype(bf16)
    dnormed_two = after(dnormed_two, project_grad)
    project_part = over_planes(project_grad.reshape(batch, wide_rows, 3 * span)).astype(bf16)
    dnormed_two, *held = gate(dnormed_two, *attended_sent, *second_sent[0])
    attended_sent, second_sent[0] = held[: ring - 1], held[ring - 1 :]
    second_sent.append(lanes([after(seconds[1], dnormed_two)] * (ring - 1)))
    attended_all = jnp.concatenate([attended] + attended_sent, axis=1)

    upstream = cot.astype(f32)

    dmodulated = upstream + row_norm_back(normed_two, inverse_two, dnormed_two)
    dshift = [jnp.sum(dmodulated * after_res, axis=0), jnp.sum(dmodulated, axis=0)]
    dafter = dmodulated * scale_part
    dbranch_own = (keep_own * dafter).astype(bf16)
    dbranch_pair = batch_pair(dbranch_own)
    dbranch_pair, *second_sent[1] = gate(dbranch_pair, *second_sent[1])
    second_sent.append(lanes([after(seconds[2], dbranch_own)] * (ring - 1)))
    dbranch = batch_all(dbranch_pair)
    dbranch, *second_sent[2] = gate(dbranch, *second_sent[2])
    dgrn = mm(dbranch, narrow_weight, ((1,), (1,)))
    sums = lane_sum(jnp.stack([jnp.sum(dgrn * hidden, axis=0), jnp.sum(dgrn, axis=0)]))
    drelative = gains[:1] * sums[:1]
    gain_rows = jnp.concatenate([sums[:1] * relative, sums[1:]]) * first_lane
    dmagnitude = drelative / mean_mag - total(drelative * magnitude) / (
        mean_mag * mean_mag * units
    )
    dhidden = dgrn * (gains[:1] * relative + 1.0) + hidden * (dmagnitude / magnitude)
    slope = gauss + pre_act * jnp.exp(-0.5 * pre_act * pre_act) * 0.3989422804014327
    attended_own = jnp.concatenate(
        [attended]
        + [
            jnp.concatenate(
                [
                    attended_all[(f ^ e) * half : ((f ^ e) + 1) * half, e * span : (e + 1) * span]
                    for f in range(ring)
                ],
                axis=0,
            )
            for e in range(1, ring)
        ],
        axis=1,
    )
    att_out = scatter_batch(
        split(mm(after(attended_own[:half], dbranch_own), output_own, ((1,), (0,))))
    )
    att_out = after(att_out, sums)
    block_low = (modulated + att_out + output_bias.astype(f32)).astype(bf16)
    dbranch_sent = [
        swap(cells, "blk", e)
        for e, cells in enumerate(lane_columns(after(dbranch_pair, sums))[1:], 1)
    ]
    dpre = (keep * dhidden * slope).astype(bf16)
    widen_bias_part = jnp.sum(dpre.astype(f32), axis=0)
    wide = by_member([after(piece, projected) for piece in wide_pieces])
    dnormed_part = mm(dpre, wide, ((1,), (1,)))
    dtext_part = mm(after(dtext_low, sums), project_own, ((1,), (1,)))
    for axis, count in (("blk", ring), ("batch", batch)):
        for bit in bits_of(count):
            low = dtext_part.astype(bf16)
            dtext_part = low.astype(f32) + swap(low, axis, bit).astype(f32)
    second_sent.append(lanes([after(seconds[3], sums)] * (ring - 1)))
    leaving = []
    dnormed_one = scatter_batch(
        split(dnormed_part), leaving, [dtext_part, *second_sent[3]]
    )
    dtext = leaving[1].astype(bf16)
    second_sent[3] = leaving[2:]
    second_others = [cells for chunk in zip(*second_sent) for cells in chunk]
    text_cut = [
        jnp.concatenate(
            [dtext[:, (p * ring + g) * shard : (p * ring + g + 1) * shard] for p in range(batch)],
            axis=1,
        )
        for g in range(ring)
    ]
    text_grad = mm(choose(text_cut, lane), soft, ((0,), (0,))).astype(bf16)
    text_sum_grad = over_planes(text_grad.reshape(batch, shard, clip_rows))
    dbranch_lanes = [batch_all(after(cells, leaving[0])) for cells in dbranch_sent]
    dbranch_lane = jnp.concatenate(
        [after(lane_columns(dbranch)[0], *leaving)] + dbranch_lanes, axis=0
    )
    second_all = jnp.concatenate([after(second_in, *leaving)] + second_others, axis=0)
    narrow_grad = mm(dbranch_lane, second_all, ((0,), (0,))).astype(bf16)
    project_part = after(project_part, *leaving)
    out_cols = 3 * channels // blk
    blocks = channels // span
    if out_cols == 3 * span and blocks == blk and blocks % 3 == 2:
        own_block = bi * ring + lane
        pieces = [project_part[:, third * span : (third + 1) * span] for third in range(3)]
        project_sum = []
        for place in range(3):
            hops = []
            for p in range(batch):
                for k in range(blk):
                    b, l = divmod((3 * k + place) % blocks, ring)
                    hops.append((spot(b, p, l), p * blk + k))
            third = (2 * (place - own_block + 3 * blocks)) % 3
            piece = jnp.where(
                third == 0, pieces[0], jnp.where(third == 1, pieces[1], pieces[2])
            )
            project_sum.append(lax.ppermute(piece, ("batch", "blk"), hops))
    else:
        whole = lax.all_gather(turn(project_part), "blk", axis=0, tiled=False)
        whole = whole.reshape(batch, ring, wide_rows, 3, span)
        whole = jnp.transpose(whole, (2, 3, 0, 1, 4)).reshape(wide_rows, 3, batch, ring * span)
        whole = whole[..., :wide_rows].reshape(wide_rows, 3 * channels)
        project_sum = lax.dynamic_slice(whole, (0, ki * out_cols), (wide_rows, out_cols))
        project_sum = [project_sum]

    width = mine // ring
    dpre_cuts = [
        lax.dynamic_slice(dpre, (0, (lane ^ e) * width), (half, width)) for e in range(ring)
    ]
    dpre_lane = jnp.concatenate(
        [after(dpre_cuts[0], narrow_grad)] + lanes(dpre_cuts[1:]), axis=0
    )
    first_all = jnp.concatenate([after(first_in, narrow_grad)] + first_others, axis=0)
    widen_grad = mm(first_all, dpre_lane, ((0,), (0,))).astype(bf16)
    widen_grad = widen_grad.reshape(batch, wide_rows, width)
    widen_pieces = exchange_batch(
        lambda member: lax.dynamic_index_in_dim(widen_grad, member, 0, keepdims=False)
    )
    dnormed_one = after(dnormed_one, widen_grad)
    dnormed_one, *project_sum = gate(dnormed_one, *project_sum)
    narrow_sum = over_planes(after(narrow_grad, text_sum_grad).reshape(batch, shard, mine))
    dconved = keep_own * row_norm_back(normed_one, inverse_one, dnormed_one)
    dconved_low, *widen_pieces[3:] = gate(dconved.astype(bf16), *widen_pieces[3:])

    attended_natural = jnp.concatenate(
        by_lane([attended_own[:, e * span : (e + 1) * span] for e in range(ring)]), axis=1
    )[:, :wide_rows]
    cot_lane = jnp.concatenate(
        [after(lane_columns(cot_rows)[0], dbranch_own)] + cot_lanes, axis=0
    )
    output_grad = mm(cot_lane, attended_natural, ((0,), (0,))).astype(bf16)
    output_sum = over_planes(output_grad.reshape(batch, shard, wide_rows))


    grad_ext = halo(dconved_low, margin)
    grad_ext, *widen_pieces[:3] = gate(grad_ext, *widen_pieces[:3])
    text_bias_part = jnp.sum(dtext.astype(f32), axis=0) * (first_lane * (bi == 0).astype(f32))
    block_output = turn(after(block_low, widen_pieces[2]))
    dlatent = dafter
    depth_rows = []
    for tap, (step_row, step_col) in enumerate(taps):
        depth_rows.append(jnp.sum(window(source_ext, step_row, step_col) * dconved, axis=0))
        dlatent = dlatent + window(grad_ext, -step_row, -step_col) * depth_taps[tap]
    latent_grad = turn(dlatent.astype(bf16))
    group_cols = jnp.sum(dqkv_seq.astype(f32), axis=0) + jnp.sum(dtext_low.astype(f32), axis=0)
    shift_part = []
    for third in (0, 2):
        cells = group_cols[third * span : (third + 1) * span]
        cells = [jnp.where(lane == g, cells, jnp.zeros_like(cells)) for g in range(ring)]
        shift_part.append(jnp.concatenate(cells)[:wide_rows])
    pad = max(channels, mine, 2 * wide_rows)

    def line(cells):
        return jnp.pad(cells, (0, pad - cells.shape[0]))

    late = [
        jnp.sum(upstream, axis=0),
        jnp.sum(dbranch_own.astype(f32), axis=0),
        text_bias_part,
        jnp.sum(dconved, axis=0),
    ] + depth_rows
    shared = len(late)
    late = late + [jnp.concatenate(shift_part), widen_bias_part, gain_rows[0], gain_rows[1]]
    sliced = len(late)
    once = first_lane * (bi == 0).astype(f32)
    late = lane_sum(jnp.stack([line(cells) for cells in late + dshift + [time_own[0] * once]]))
    members = gather_batch(late).reshape((batch,) + late.shape)
    both = tree_sum(members)
    late = jnp.concatenate(
        [both[:shared], members[:, shared:sliced].reshape(-1, pad), both[sliced:]]
    )
    by_plane = [late] + [swap(late, "blk", ring * d) for d in range(1, batch)]
    both = tree_sum(by_plane)
    members = both[shared : shared + batch * (sliced - shared)].reshape(batch, -1, pad)
    widen_held = jnp.stack(widen_pieces)

    def for_plane(member):
        return lax.dynamic_index_in_dim(widen_held, member ^ bi, 0, keepdims=False)

    widen_sum = over_planes(
        after(jnp.stack([for_plane(p) for p in range(batch)]), narrow_sum)
    )
    arrived = grad_ext

    output_bias_sum, narrow_bias_sum, text_bias_sum, depth_bias_sum = (
        both[i, :channels] for i in range(4)
    )
    depth_weight_sum = both[4:shared, :channels]
    shifts = [
        jnp.concatenate([by_plane[d][-3, :channels], by_plane[d][-2, :channels]])
        for d in range(batch)
    ]
    time_bias_sum = tree_sum(shifts)
    time_weight_sum = tree_sum(
        by_plane[d][-1, : time_embed.shape[1]][:, None] * shifts[d][None, :]
        for d in range(batch)
    )
    ordered = jnp.stack(
        [lax.dynamic_index_in_dim(members, l ^ bi, 0, keepdims=False) for l in range(batch)]
    )
    project_bias_sum = jnp.concatenate(
        [
            ordered[:, 0, :wide_rows].reshape(-1),
            ordered[:, 0, wide_rows : 2 * wide_rows].reshape(-1),
        ]
    )
    widen_bias_sum = ordered[:, 1, :mine].reshape(-1)
    gain_sum = jnp.stack([ordered[:, 2, :mine].reshape(-1), ordered[:, 3, :mine].reshape(-1)])

    project_sum = jnp.concatenate([after(project_sum[0], arrived)] + project_sum[1:], axis=1)
    project_sum = project_sum.astype(f32)

    return (
        block_output[None],
        latent_grad[None],
        depth_weight_sum,
        depth_bias_sum,
        widen_sum,
        widen_bias_sum,
        gain_sum,
        after(narrow_sum, arrived).T,
        narrow_bias_sum,
        time_weight_sum,
        time_bias_sum,
        after(text_sum_grad, arrived).T,
        text_bias_sum,
        project_sum,
        project_bias_sum,
        after(output_sum, arrived).T,
        output_bias_sum,
    )


def solution(mesh):
    rows = P("batch", "blk", None)
    first = P("batch", None)
    both = P("batch", "blk")
    everywhere = P()
    placed = (
        rows,
        first,
        P("batch", None, None),
        first,
        everywhere,
        everywhere,
        first,
        everywhere,
        everywhere,
        first,
        everywhere,
        everywhere,
        everywhere,
        first,
        everywhere,
        first,
        everywhere,
        first,
        everywhere,
        rows,
    )
    given = (
        rows,
        rows,
        everywhere,
        everywhere,
        both,
        everywhere,
        everywhere,
        both,
        everywhere,
        everywhere,
        everywhere,
        both,
        everywhere,
        both,
        everywhere,
        both,
        everywhere,
    )
    return jax.shard_map(
        on_device, mesh=mesh, in_specs=placed, out_specs=given, check_vma=False
    )
```

time: 955 us -> 569 us (0.60)
  the two profiles are of different devices: /device:TPU:2 before, /device:TPU:9 now
where the time goes in v2:
time: 569 us; the launch traced here: 564 us
  waiting for transfers between devices  175 us (31%)
  starting transfers between devices  150 us (26%)
  other arithmetic  78.5 us (14%)
  local copies, waits for them, and re-layouts  76.2 us (13%)
  matrix products  65.9 us (12%)
  between operations  19 us (3%)
    ppermute x65, waiting for transfers between devices, swap(): return lax.ppermute(cells, axis, [(i, i ^ distance) for i in range(count)])  168 us
    ppermute x65, starting transfers between devices, swap(): return lax.ppermute(cells, axis, [(i, i ^ distance) for i in range(count)])  118 us
    dot_general x42, matrix products, mm(): lax.dot_general(left, right, (dims, ((), ())), preferred_element_type=f32)  65.9 us
    unnamed x292, local copies, waits for them, and re-layouts  21.2 us
  transfers between devices with their start and end apart: 83, of which 20 were waited for; matrix products, arithmetic and copies ran while one was open for 37% of the time, Pallas kernels for 0%

profile of v2, /device:TPU:9, one launch (start us, length us, event | category | flops | bytes accessed | tf_op | source)
XLA Modules:
  0.0 564.1 jit_solution(1103029428628700639)
XLA Ops:
  14.0 6.1 %collective-permute-start.4 = (bf16[2,192,1536]{2,1,0:T(8,128)(2,1)}, bf16[2,192,1536]{2,1,0:T(8,128)(2,1)}, u32[]{:S(2)}, u32[]{:S(2)}) collective-permute-start(bf16[2,192,1536]{2,1,0:T(8,128)(2,1)} %pad_maximum_fusion.8), channel_id=1, source_target_pairs={{0,16},{8,24},{16,0},{24,8},{1,17},{9,25},{17,1},{25,9},{2,18},{10... | collective-permute-start | bytes 3538952 | tf_op jit(solution)/shard_map/ppermute | solution.py:22
  42.0 6.6 %collective-permute-start.7 = (bf16[2,192,1152]{2,1,0:T(8,128)(2,1)S(1)}, bf16[2,192,1152]{2,1,0:T(8,128)(2,1)S(1)}, u32[]{:S(2)}, u32[]{:S(2)}) collective-permute-start(bf16[2,192,1152]{2,1,0:T(8,128)(2,1)S(1)} %pad_maximum_fusion.14), channel_id=1, source_target_pairs={{0,16},{8,24},{16,0},{24,8},{1,17},{9,25},{17,1},{25,9},{2,18},{10... | collective-permute-start | bytes 2654216 | tf_op jit(solution)/shard_map/ppermute | solution.py:22
  50.5 5.1 collective-permute-start.9
  65.8 10.5 %collective-permute-done.5 = bf16[128,1536]{1,0:T(8,128)(2,1)S(1)} collective-permute-done((bf16[128,1536]{1,0:T(8,128)(2,1)S(1)}, bf16[128,1536]{1,0:T(8,128)(2,1)S(1)}, u32[]{:S(2)}, u32[]{:S(2)}) %collective-permute-start.5) | collective-permute-done | bytes 393248 | tf_op jit(solution)/shard_map/ppermute | solution.py:22
  92.6 4.9 collective-permute-start.11
  105.2 8.1 %collective-permute-start.23 = (bf16[384,1152]{1,0:T(8,128)(2,1)S(1)}, bf16[384,1152]{1,0:T(8,128)(2,1)S(1)}, u32[]{:S(2)}, u32[]{:S(2)}) collective-permute-start(bf16[384,1152]{1,0:T(8,128)(2,1)S(1)} %pad_maximum_fusion.16), channel_id=1, source_target_pairs={{0,8},{8,0},{16,24},{24,16},{1,9},{9,1},{17,25},{25,17},{2,10},{10... | collective-permute-start | bytes 2654216 | tf_op jit(solution)/shard_map/ppermute | solution.py:22
  118.8 7.2 %collective-permute-start.17 = (bf16[2,128,1536]{2,1,0:T(8,128)(2,1)S(1)}, bf16[2,128,1536]{2,1,0:T(8,128)(2,1)S(1)}, u32[]{:S(2)}, u32[]{:S(2)}) collective-permute-start(bf16[2,128,1536]{2,1,0:T(8,128)(2,1)S(1)} %pad_maximum_fusion.18), channel_id=1, source_target_pairs={{0,8},{8,0},{16,24},{24,16},{1,9},{9,1},{17,25},{25,17},{2,10},{10... | collective-permute-start | bytes 2359304 | tf_op jit(solution)/shard_map/ppermute | solution.py:22
  128.3 10.2 %collective-permute-start.19 = (bf16[128,1536]{1,0:T(8,128)(2,1)S(1)}, bf16[128,1536]{1,0:T(8,128)(2,1)S(1)}, u32[]{:S(2)}, u32[]{:S(2)}) collective-permute-start(bf16[128,1536]{1,0:T(8,128)(2,1)S(1)} %fusion.59), channel_id=1, source_target_pairs={{0,16},{8,24},{16,0},{24,8},{1,17},{9,25},{17,1},{25,9},{2,18},{10... | collective-permute-start | bytes 1179656 | tf_op jit(solution)/shard_map/ppermute | solution.py:22
  139.6 8.3 %collective-permute-done.19 = bf16[128,1536]{1,0:T(8,128)(2,1)S(1)} collective-permute-done((bf16[128,1536]{1,0:T(8,128)(2,1)S(1)}, bf16[128,1536]{1,0:T(8,128)(2,1)S(1)}, u32[]{:S(2)}, u32[]{:S(2)}) %collective-permute-start.19) | collective-permute-done | bytes 393248 | tf_op jit(solution)/shard_map/ppermute | solution.py:22
  150.3 8.6 %collective-permute-done.21 = bf16[128,1536]{1,0:T(8,128)(2,1)S(1)} collective-permute-done((bf16[128,1536]{1,0:T(8,128)(2,1)S(1)}, bf16[128,1536]{1,0:T(8,128)(2,1)S(1)}, u32[]{:S(2)}, u32[]{:S(2)}) %collective-permute-start.21) | collective-permute-done | bytes 393248 | tf_op jit(solution)/shard_map/ppermute | solution.py:22
  174.9 8.8 %collective-permute-done.26 = bf16[128,1536]{1,0:T(8,128)(2,1)} collective-permute-done((bf16[128,1536]{1,0:T(8,128)(2,1)S(1)}, bf16[128,1536]{1,0:T(8,128)(2,1)}, u32[]{:S(2)}, u32[]{:S(2)}) %collective-permute-start.26) | collective-permute-done | bytes 393248 | tf_op jit(solution)/shard_map/ppermute | solution.py:22
  201.3 16.3 %collective-permute-done.28 = bf16[512,192]{0,1:T(8,128)(2,1)S(1)} collective-permute-done((bf16[512,192]{0,1:T(8,128)(2,1)S(1)}, bf16[512,192]{0,1:T(8,128)(2,1)S(1)}, u32[]{:S(2)}, u32[]{:S(2)}) %collective-permute-start.28) | collective-permute-done | bytes 196640 | tf_op jit(solution)/shard_map/ppermute | solution.py:22
  250.8 11.7 %collective-permute-done.34 = bf16[512,192]{0,1:T(8,128)(2,1)S(1)} collective-permute-done((bf16[512,192]{0,1:T(8,128)(2,1)S(1)}, bf16[512,192]{0,1:T(8,128)(2,1)S(1)}, u32[]{:S(2)}, u32[]{:S(2)}) %collective-permute-start.34) | collective-permute-done | bytes 196640 | tf_op jit(solution)/shard_map/ppermute | solution.py:22
  274.4 5.0 collective-permute-done.37
  279.5 7.0 %collective-permute-done.40 = bf16[128,1536]{1,0:T(8,128)(2,1)S(1)} collective-permute-done((bf16[128,1536]{1,0:T(8,128)(2,1)S(1)}, bf16[128,1536]{1,0:T(8,128)(2,1)S(1)}, u32[]{:S(2)}, u32[]{:S(2)}) %collective-permute-start.40) | collective-permute-done | bytes 393248 | tf_op jit(solution)/shard_map/ppermute | solution.py:22
  317.9 6.2 %multiply_reduce_fusion = (f32[1536]{0:T(1024)S(1)}, f32[1536]{0:T(1024)S(1)}, f32[512,1536]{1,0:T(8,128)S(1)}) fusion(f32[512]{0:T(512)S(1)} %copy-done.86, f32[512,1536]{1,0:T(8,128)} %copy-done.8, f32[512,1536]{1,0:T(8,128)S(1)} %copy-done.7, bf16[512,1536]{1,0:T(8,128)(2,1)S(1)} %pad_maximum_fusion.5, bf16[1536,1536]{1,0:T(8,128)(2,1)} %param.29), kind=kOutput, calls=%fused_computation.43 | convolution fusion | flops 2419848192 | bytes 15742976 | tf_op jit(solution)/shard_map/dot_general | solution.py:17
  378.3 5.9 %convolution_convert_fusion.1 = bf16[768,1536]{1,0:T(8,128)(2,1)} fusion(bf16[1024,768]{1,0:T(8,128)(2,1)S(1)} %fusion.98, bf16[1024,1536]{1,0:T(8,128)(2,1)} %constant_dynamic-update-slice_fusion.3), kind=kOutput, calls=%fused_computation.31 | convolution fusion | flops 2417098752 | bytes 7077888 | tf_op jit(solution)/shard_map/dot_general | solution.py:17
  398.6 5.3 collective-permute-start.63
  404.0 4.9 collective-permute-start.61
  423.8 5.1 collective-permute-done.64
  439.3 6.2 %collective-permute-start.73 = (f32[2,20,1536]{2,1,0:T(8,128)S(1)}, f32[2,20,1536]{2,1,0:T(8,128)S(1)}, u32[]{:S(2)}, u32[]{:S(2)}) collective-permute-start(f32[2,20,1536]{2,1,0:T(8,128)S(1)} %pad_maximum_fusion.45), channel_id=1, source_target_pairs={{0,8},{8,0},{16,24},{24,16},{1,9},{9,1},{17,25},{25,17},{2,10},{10... | collective-permute-start | bytes 737288 | tf_op jit(solution)/shard_map/ppermute | solution.py:22
  464.7 5.8 %collective-permute-start.75 = (f32[32,1536]{1,0:T(8,128)S(1)}, f32[32,1536]{1,0:T(8,128)S(1)}, u32[]{:S(2)}, u32[]{:S(2)}) collective-permute-start(f32[32,1536]{1,0:T(8,128)S(1)} %pad_maximum_fusion.48), channel_id=1, source_target_pairs={{0,4},{1,5},{2,6},{3,7},{4,0},{5,1},{6,2},{7,3},{8,12},{9,13},{10,... | collective-permute-start | bytes 589832 | tf_op jit(solution)/shard_map/ppermute | solution.py:22
  471.8 18.3 %collective-permute-done.75 = f32[32,1536]{1,0:T(8,128)S(1)} collective-permute-done((f32[32,1536]{1,0:T(8,128)S(1)}, f32[32,1536]{1,0:T(8,128)S(1)}, u32[]{:S(2)}, u32[]{:S(2)}) %collective-permute-start.75) | collective-permute-done | bytes 196640 | tf_op jit(solution)/shard_map/ppermute | solution.py:22
  490.1 55.9 %collective-permute-done.76 = f32[32,1536]{1,0:T(8,128)S(1)} collective-permute-done((f32[32,1536]{1,0:T(8,128)S(1)}, f32[32,1536]{1,0:T(8,128)S(1)}, u32[]{:S(2)}, u32[]{:S(2)}) %collective-permute-start.76) | collective-permute-done | bytes 196640 | tf_op jit(solution)/shard_map/ppermute | solution.py:22
  (748 shorter events, 307.2 us)
Async XLA Ops:
  7.2 306.4 %reduce-scatter.14.cloned.1.call-start = ((), (), s32[]{:S(2)}) async-start(), calls=%async_computation.9 | async-start | bytes 737280 | tf_op jit(solution)/shard_map/reduce_scatter | solution.py:247
  14.0 36.5 %collective-permute-start.4 = (bf16[2,192,1536]{2,1,0:T(8,128)(2,1)}, bf16[2,192,1536]{2,1,0:T(8,128)(2,1)}, u32[]{:S(2)}, u32[]{:S(2)}) collective-permute-start(bf16[2,192,1536]{2,1,0:T(8,128)(2,1)} %pad_maximum_fusion.8), channel_id=1, source_target_pairs={{0,16},{8,24},{16,0},{24,8},{1,17},{9,25},{17,1},{25,9},{2,18},{10... | collective-permute-start | bytes 3538952 | tf_op jit(solution)/shard_map/ppermute | solution.py:22
  22.9 65.2 %collective-permute-start.8 = (bf16[384,1536]{1,0:T(8,128)(2,1)}, bf16[384,1536]{1,0:T(8,128)(2,1)}, u32[]{:S(2)}, u32[]{:S(2)}) collective-permute-start(bf16[384,1536]{1,0:T(8,128)(2,1)} %get-tuple-element.293), channel_id=1, source_target_pairs={{0,8},{8,0},{16,24},{24,16},{1,9},{9,1},{17,25},{25,17},{2,10},{10... | collective-permute-start | bytes 3538952 | tf_op jit(solution)/shard_map/ppermute | solution.py:22
  42.0 42.6 %collective-permute-start.7 = (bf16[2,192,1152]{2,1,0:T(8,128)(2,1)S(1)}, bf16[2,192,1152]{2,1,0:T(8,128)(2,1)S(1)}, u32[]{:S(2)}, u32[]{:S(2)}) collective-permute-start(bf16[2,192,1152]{2,1,0:T(8,128)(2,1)S(1)} %pad_maximum_fusion.14), channel_id=1, source_target_pairs={{0,16},{8,24},{16,0},{24,8},{1,17},{9,25},{17,1},{25,9},{2,18},{10... | collective-permute-start | bytes 2654216 | tf_op jit(solution)/shard_map/ppermute | solution.py:22
  50.5 30.7 %collective-permute-start.9 = (bf16[2,192,1536]{2,1,0:T(8,128)(2,1)}, bf16[2,192,1536]{2,1,0:T(8,128)(2,1)S(1)}, u32[]{:S(2)}, u32[]{:S(2)}) collective-permute-start(bf16[2,192,1536]{2,1,0:T(8,128)(2,1)} %collective-permute-done.4), channel_id=1, source_target_pairs={{0,2},{1,3},{2,0},{3,1},{4,6},{5,7},{6,4},{7,5},{8,10},{9,11},{10,... | collective-permute-start | bytes 3538952 | tf_op jit(solution)/shard_map/ppermute | solution.py:22
  84.6 29.4 %collective-permute-start.15 = (bf16[2,192,1152]{2,1,0:T(8,128)(2,1)S(1)}, bf16[2,192,1152]{2,1,0:T(8,128)(2,1)S(1)}, u32[]{:S(2)}, u32[]{:S(2)}) collective-permute-start(bf16[2,192,1152]{2,1,0:T(8,128)(2,1)S(1)} %collective-permute-done.7), channel_id=1, source_target_pairs={{0,2},{1,3},{2,0},{3,1},{4,6},{5,7},{6,4},{7,5},{8,10},{9,11},{10,... | collective-permute-start | bytes 2654216 | tf_op jit(solution)/shard_map/ppermute | solution.py:22
  105.2 59.3 %collective-permute-start.23 = (bf16[384,1152]{1,0:T(8,128)(2,1)S(1)}, bf16[384,1152]{1,0:T(8,128)(2,1)S(1)}, u32[]{:S(2)}, u32[]{:S(2)}) collective-permute-start(bf16[384,1152]{1,0:T(8,128)(2,1)S(1)} %pad_maximum_fusion.16), channel_id=1, source_target_pairs={{0,8},{8,0},{16,24},{24,16},{1,9},{9,1},{17,25},{25,17},{2,10},{10... | collective-permute-start | bytes 2654216 | tf_op jit(solution)/shard_map/ppermute | solution.py:22
  126.4 34.4 %collective-permute-start.30 = (bf16[77,1536]{1,0:T(8,128)(2,1)S(1)}, bf16[77,1536]{1,0:T(8,128)(2,1)S(1)}, u32[]{:S(2)}, u32[]{:S(2)}) collective-permute-start(bf16[77,1536]{1,0:T(8,128)(2,1)S(1)} %convolution_convert_fusion.3), channel_id=1, source_target_pairs={{0,8},{8,0},{16,24},{24,16},{1,9},{9,1},{17,25},{25,17},{2,10},{10... | collective-permute-start | bytes 709640 | tf_op jit(solution)/shard_map/ppermute | solution.py:22
  169.2 216.2 %collective-permute-start.59 = (bf16[2,128,1536]{2,1,0:T(8,128)(2,1)}, bf16[2,128,1536]{2,1,0:T(8,128)(2,1)}, u32[]{:S(2)}, u32[]{:S(2)}) collective-permute-start(bf16[2,128,1536]{2,1,0:T(8,128)(2,1)} %pad_maximum_fusion.25), channel_id=1, source_target_pairs={{0,8},{8,0},{16,24},{24,16},{1,9},{9,1},{17,25},{25,17},{2,10},{10... | collective-permute-start | bytes 2359304 | tf_op jit(solution)/shard_map/ppermute | solution.py:22
  194.1 44.9 %collective-permute-start.32 = (bf16[2,128,1536]{2,1,0:T(8,128)(2,1)S(1)}, bf16[2,128,1536]{2,1,0:T(8,128)(2,1)S(1)}, u32[]{:S(2)}, u32[]{:S(2)}) collective-permute-start(bf16[2,128,1536]{2,1,0:T(8,128)(2,1)S(1)} %copy-done.43), channel_id=1, source_target_pairs={{0,1},{1,0},{2,3},{3,2},{4,5},{5,4},{6,7},{7,6},{8,9},{9,8},{10,11... | collective-permute-start | bytes 2359304 | tf_op jit(solution)/shard_map/ppermute | solution.py:22
  239.0 32.0 %collective-permute-start.38 = (bf16[2,128,1536]{2,1,0:T(8,128)(2,1)S(1)}, bf16[2,128,1536]{2,1,0:T(8,128)(2,1)S(1)}, u32[]{:S(2)}, u32[]{:S(2)}) collective-permute-start(bf16[2,128,1536]{2,1,0:T(8,128)(2,1)S(1)} %collective-permute-done.32), channel_id=1, source_target_pairs={{0,8},{8,0},{16,24},{24,16},{1,9},{9,1},{17,25},{25,17},{2,10},{10... | collective-permute-start | bytes 2359304 | tf_op jit(solution)/shard_map/ppermute | solution.py:22
  293.8 103.0 %reduce-scatter.6.cloned.1.call-start = ((), (), s32[]{:S(2)}) async-start(), calls=%async_computation.5 | async-start | bytes 2211840 | tf_op jit(solution)/shard_map/reduce_scatter | solution.py:247
  302.0 107.0 %reduce-scatter.8.cloned.1.call-start = ((), (), s32[]{:S(2)}) async-start(), calls=%async_computation.6 | async-start | bytes 737280 | tf_op jit(solution)/shard_map/reduce_scatter | solution.py:247
  355.3 35.5 %collective-permute-start.60 = (bf16[512,768]{1,0:T(8,128)(2,1)}, bf16[512,768]{1,0:T(8,128)(2,1)}, u32[]{:S(2)}, u32[]{:S(2)}) collective-permute-start(bf16[512,768]{1,0:T(8,128)(2,1)} %get-tuple-element.346), channel_id=1, source_target_pairs={{0,1},{1,0},{2,3},{3,2},{4,5},{5,4},{6,7},{7,6},{8,9},{9,8},{10,11... | collective-permute-start | bytes 2359304 | tf_op jit(solution)/shard_map/ppermute | solution.py:22
  359.6 29.1 %collective-permute-start.56 = (bf16[128,1536]{1,0:T(8,128)(2,1)}, bf16[128,1536]{1,0:T(8,128)(2,1)}, u32[]{:S(2)}, u32[]{:S(2)}) collective-permute-start(bf16[128,1536]{1,0:T(8,128)(2,1)} %fusion.53), channel_id=1, source_target_pairs={{0,16},{8,24},{16,0},{24,8},{1,17},{9,25},{17,1},{25,9},{2,18},{10... | collective-permute-start | bytes 1179656 | tf_op jit(solution)/shard_map/ppermute | solution.py:22
  369.8 92.6 %reduce-scatter.10.cloned.1.call-start = ((), (), s32[]{:S(2)}) async-start(), calls=%async_computation.7 | async-start | bytes 2949120 | tf_op jit(solution)/shard_map/reduce_scatter | solution.py:247
  396.2 51.2 %collective-permute-start.68 = (bf16[384,768]{1,0:T(8,128)(2,1)}, bf16[384,768]{1,0:T(8,128)(2,1)}, u32[]{:S(2)}, u32[]{:S(2)}) collective-permute-start(bf16[384,768]{1,0:T(8,128)(2,1)} %get-tuple-element.325), channel_id=1, source_target_pairs={{0,16},{8,24},{16,0},{24,8},{1,17},{9,25},{17,1},{25,9},{2,18},{10... | collective-permute-start | bytes 1769480 | tf_op jit(solution)/shard_map/ppermute | solution.py:22
  396.5 50.9 %collective-permute-start.67 = (bf16[384,768]{1,0:T(8,128)(2,1)}, bf16[384,768]{1,0:T(8,128)(2,1)}, u32[]{:S(2)}, u32[]{:S(2)}) collective-permute-start(bf16[384,768]{1,0:T(8,128)(2,1)} %get-tuple-element.326), channel_id=1, source_target_pairs={{0,8},{8,0},{16,24},{24,16},{1,9},{9,1},{17,25},{25,17},{2,10},{10... | collective-permute-start | bytes 1769480 | tf_op jit(solution)/shard_map/ppermute | solution.py:22
  410.6 141.0 %reduce-scatter.12.cloned.1.call-start = ((), (), s32[]{:S(2)}) async-start(), calls=%async_computation.8 | async-start | bytes 2949120 | tf_op jit(solution)/shard_map/reduce_scatter | solution.py:247
  449.7 101.9 %collective-permute-start.70 = (bf16[128,1536]{1,0:T(8,128)(2,1)S(1)}, bf16[128,1536]{1,0:T(8,128)(2,1)}, u32[]{:S(2)}, u32[]{:S(2)}) collective-permute-start(bf16[128,1536]{1,0:T(8,128)(2,1)S(1)} %add_convert_fusion.2), channel_id=1, source_target_pairs={{0,0},{1,1},{2,8},{3,9},{4,16},{5,17},{6,24},{7,25},{8,2},{9,3},{1... | collective-permute-start | bytes 1179656 | tf_op jit(solution)/shard_map/ppermute | solution.py:230
  451.1 100.5 %collective-permute-start.69 = (bf16[128,1536]{1,0:T(8,128)(2,1)}, bf16[128,1536]{1,0:T(8,128)(2,1)}, u32[]{:S(2)}, u32[]{:S(2)}) collective-permute-start(bf16[128,1536]{1,0:T(8,128)(2,1)} %add_convert_fusion.3), channel_id=1, source_target_pairs={{0,0},{1,1},{2,8},{3,9},{4,16},{5,17},{6,24},{7,25},{8,2},{9,3},{1... | collective-permute-start | bytes 1179656 | tf_op jit(solution)/shard_map/ppermute | solution.py:230
  464.7 25.4 %collective-permute-start.75 = (f32[32,1536]{1,0:T(8,128)S(1)}, f32[32,1536]{1,0:T(8,128)S(1)}, u32[]{:S(2)}, u32[]{:S(2)}) collective-permute-start(f32[32,1536]{1,0:T(8,128)S(1)} %pad_maximum_fusion.48), channel_id=1, source_target_pairs={{0,4},{1,5},{2,6},{3,7},{4,0},{5,1},{6,2},{7,3},{8,12},{9,13},{10,... | collective-permute-start | bytes 589832 | tf_op jit(solution)/shard_map/ppermute | solution.py:22
  470.5 75.5 %collective-permute-start.76 = (f32[32,1536]{1,0:T(8,128)S(1)}, f32[32,1536]{1,0:T(8,128)S(1)}, u32[]{:S(2)}, u32[]{:S(2)}) collective-permute-start(f32[32,1536]{1,0:T(8,128)S(1)} %pad_maximum_fusion.48), channel_id=1, source_target_pairs={{0,6},{1,7},{2,4},{3,5},{4,2},{5,3},{6,0},{7,1},{8,14},{9,15},{10,... | collective-permute-start | bytes 589832 | tf_op jit(solution)/shard_map/ppermute | solution.py:22
  470.5 75.5 %collective-permute-start.74 = (f32[32,1536]{1,0:T(8,128)S(1)}, f32[32,1536]{1,0:T(8,128)S(1)}, u32[]{:S(2)}, u32[]{:S(2)}) collective-permute-start(f32[32,1536]{1,0:T(8,128)S(1)} %pad_maximum_fusion.48), channel_id=1, source_target_pairs={{0,2},{1,3},{2,0},{3,1},{4,6},{5,7},{6,4},{7,5},{8,10},{9,11},{10,... | collective-permute-start | bytes 589832 | tf_op jit(solution)/shard_map/ppermute | solution.py:22
  (190 other events, 2859.8 us)
Sparse Core Ops, SparseCore 0:
  293.9 19.6 reduce-scatter.13
  316.0 38.4 reduce-scatter.5
  369.9 17.2 reduce-scatter.7
  410.7 44.8 reduce-scatter.9
  464.8 76.1 reduce-scatter.11

commit v3 on v2

--- a/solution.py
+++ b/solution.py
@@ -249,6 +249,15 @@
         ).astype(f32)
 
     first_lane = (lane == 0).astype(f32)
+    def plane_pieces(shards):
+        if batch != 4:
+            return [over_planes(shards)]
+        own = [lax.dynamic_index_in_dim(shards, plane ^ d, 0, keepdims=False) for d in range(4)]
+        return own[:1] + [swap(own[d], "blk", ring * d) for d in range(1, 4)]
+
+    def add_up(pieces):
+        return tree_sum([cells.astype(f32) for cells in pieces])
+
     margin = WIDE + 1
     lat = turn(latent[0])
     facts = turn(
@@ -495,9 +504,9 @@
     )
 
     projected = to_heads(projected, 3 * span)
-    attn_sent = [swap(after(attn_pair, projected), "blk", e) for e in range(1, ring)]
-
-    projected, grad_heads = gate(projected, grad_heads)
+
+    wide = by_member([after(piece, attn_in) for piece in wide_pieces])
+    projected, grad_heads, project, wide = gate(projected, grad_heads, project, wide)
     seq = ring * half
     seq_rows = jnp.concatenate(
         [rows_of(bi ^ d, lane ^ e) for e in range(ring) for d in range(batch)]
@@ -510,9 +519,6 @@
     for head in range(per):
         at = slice(head * HDIM, (head + 1) * HDIM)
         heads.append(attend(projected[:, at], keys[:, at], values[:, at], grad_heads[:, at], live))
-        if head == per // 2:
-            key_cells, *attn_sent = gate(heads[-1][2], *attn_sent)
-            heads[-1] = heads[-1][:2] + (key_cells,) + heads[-1][3:]
     attended, dq, dk, dv = (jnp.concatenate(cells, axis=1).astype(bf16) for cells in zip(*heads))
     dqkv_seq = jnp.concatenate([dq, dk[:seq], dv[:seq]], axis=1)
     cot_sent = [
@@ -529,7 +535,7 @@
         dqkv = dqkv + [first_cells, then_cells]
     dqkv = jnp.concatenate(dqkv, axis=1)
     attended_sent = lanes([after(attended, dq_sent[0])] * (ring - 1))
-    attn_others = [batch_all(after(cells, dqkv)) for cells in attn_sent]
+    attn_sent = [swap(after(attn_pair, dq_sent[0]), "blk", e) for e in range(1, ring)]
     quarter = half // 4
     seconds = [second_in[n * quarter : (n + 1) * quarter] for n in range(4)]
     leaving = []
@@ -537,13 +543,8 @@
     dnormed_two = scatter_batch(split(dnormed_part), leaving)
     second_sent = [lanes([after(seconds[0], leaving[0])] * (ring - 1))]
     dtext_low = jnp.concatenate([jnp.zeros((text_count, span), bf16), dk[seq:], dv[seq:]], axis=1)
-    attn_all = jnp.concatenate([after(attn_in, *leaving)] + attn_others, axis=0)
-    project_grad = mm(attn_all, dqkv_seq, ((0,), (0,))) + mm(text_feat, dtext_low, ((0,), (0,)))
-    project_grad = project_grad.astype(bf16)
-    dnormed_two = after(dnormed_two, project_grad)
-    project_part = over_planes(project_grad.reshape(batch, wide_rows, 3 * span)).astype(bf16)
-    dnormed_two, *held = gate(dnormed_two, *attended_sent, *second_sent[0])
-    attended_sent, second_sent[0] = held[: ring - 1], held[ring - 1 :]
+    second_sent = [lanes([after(seconds[0], leaving[0])] * (ring - 1))]
+    dtext_low = jnp.concatenate([jnp.zeros((text_count, span), bf16), dk[seq:], dv[seq:]], axis=1)
     second_sent.append(lanes([after(seconds[1], dnormed_two)] * (ring - 1)))
     attended_all = jnp.concatenate([attended] + attended_sent, axis=1)
 
@@ -554,19 +555,14 @@
     dafter = dmodulated * scale_part
     dbranch_own = (keep_own * dafter).astype(bf16)
     dbranch_pair = batch_pair(dbranch_own)
-    dbranch_pair, *second_sent[1] = gate(dbranch_pair, *second_sent[1])
-    second_sent.append(lanes([after(seconds[2], dbranch_own)] * (ring - 1)))
-    dbranch = batch_all(dbranch_pair)
-    dbranch, *second_sent[2] = gate(dbranch, *second_sent[2])
-    dgrn = mm(dbranch, narrow_weight, ((1,), (1,)))
-    sums = lane_sum(jnp.stack([jnp.sum(dgrn * hidden, axis=0), jnp.sum(dgrn, axis=0)]))
-    drelative = gains[:1] * sums[:1]
-    gain_rows = jnp.concatenate([sums[:1] * relative, sums[1:]]) * first_lane
-    dmagnitude = drelative / mean_mag - total(drelative * magnitude) / (
-        mean_mag * mean_mag * units
-    )
-    dhidden = dgrn * (gains[:1] * relative + 1.0) + hidden * (dmagnitude / magnitude)
-    slope = gauss + pre_act * jnp.exp(-0.5 * pre_act * pre_act) * 0.3989422804014327
+    dbranch_pair, *second_sent[0] = gate(dbranch_pair, *second_sent[0])
+    attn_others = [batch_all(after(cells, dbranch_own)) for cells in attn_sent]
+    attn_all = jnp.concatenate([after(attn_in, dbranch_own)] + attn_others, axis=0)
+    project_grad = mm(attn_all, dqkv_seq, ((0,), (0,))) + mm(text_feat, dtext_low, ((0,), (0,)))
+    project_grad = project_grad.astype(bf16)
+    project_part = over_planes(project_grad.reshape(batch, wide_rows, 3 * span)).astype(bf16)
+    dbranch = after(batch_all(dbranch_pair), project_grad)
+    dbranch, *second_sent[1] = gate(dbranch, *second_sent[1])
     attended_own = jnp.concatenate(
         [attended]
         + [
@@ -581,10 +577,29 @@
         ],
         axis=1,
     )
+    attended_natural = jnp.concatenate(
+        by_lane([attended_own[:, e * span : (e + 1) * span] for e in range(ring)]), axis=1
+    )[:, :wide_rows]
+    cot_lane = jnp.concatenate(
+        [after(lane_columns(cot_rows)[0], dqkv)] + cot_lanes, axis=0
+    )
+    output_grad = mm(cot_lane, attended_natural, ((0,), (0,))).astype(bf16)
+    output_pieces = plane_pieces(output_grad.reshape(batch, shard, wide_rows))
+    dbranch, *output_pieces = gate(dbranch, *output_pieces)
+    dgrn = mm(dbranch, narrow_weight, ((1,), (1,)))
+    sums = lane_sum(jnp.stack([jnp.sum(dgrn * hidden, axis=0), jnp.sum(dgrn, axis=0)]))
     att_out = scatter_batch(
         split(mm(after(attended_own[:half], dbranch_own), output_own, ((1,), (0,))))
     )
-    att_out = after(att_out, sums)
+    sums, att_out = gate(sums, att_out)
+    drelative = gains[:1] * sums[:1]
+    gain_rows = jnp.concatenate([sums[:1] * relative, sums[1:]]) * first_lane
+    dmagnitude = drelative / mean_mag - total(drelative * magnitude) / (
+        mean_mag * mean_mag * units
+    )
+    dhidden = dgrn * (gains[:1] * relative + 1.0) + hidden * (dmagnitude / magnitude)
+    slope = gauss + pre_act * jnp.exp(-0.5 * pre_act * pre_act) * 0.3989422804014327
+    att_out = after(att_out, dmagnitude)
     block_low = (modulated + att_out + output_bias.astype(f32)).astype(bf16)
     dbranch_sent = [
         swap(cells, "blk", e)
@@ -592,37 +607,16 @@
     ]
     dpre = (keep * dhidden * slope).astype(bf16)
     widen_bias_part = jnp.sum(dpre.astype(f32), axis=0)
-    wide = by_member([after(piece, projected) for piece in wide_pieces])
     dnormed_part = mm(dpre, wide, ((1,), (1,)))
+    second_sent.append(lanes([after(seconds[2], sums)] * (ring - 1)))
+    second_sent.append(lanes([after(seconds[3], sums)] * (ring - 1)))
     dtext_part = mm(after(dtext_low, sums), project_own, ((1,), (1,)))
-    for axis, count in (("blk", ring), ("batch", batch)):
-        for bit in bits_of(count):
-            low = dtext_part.astype(bf16)
-            dtext_part = low.astype(f32) + swap(low, axis, bit).astype(f32)
-    second_sent.append(lanes([after(seconds[3], sums)] * (ring - 1)))
+    for bit in bits_of(ring):
+        low = dtext_part.astype(bf16)
+        dtext_part = low.astype(f32) + swap(low, "blk", bit).astype(f32)
     leaving = []
-    dnormed_one = scatter_batch(
-        split(dnormed_part), leaving, [dtext_part, *second_sent[3]]
-    )
-    dtext = leaving[1].astype(bf16)
-    second_sent[3] = leaving[2:]
-    second_others = [cells for chunk in zip(*second_sent) for cells in chunk]
-    text_cut = [
-        jnp.concatenate(
-            [dtext[:, (p * ring + g) * shard : (p * ring + g + 1) * shard] for p in range(batch)],
-            axis=1,
-        )
-        for g in range(ring)
-    ]
-    text_grad = mm(choose(text_cut, lane), soft, ((0,), (0,))).astype(bf16)
-    text_sum_grad = over_planes(text_grad.reshape(batch, shard, clip_rows))
-    dbranch_lanes = [batch_all(after(cells, leaving[0])) for cells in dbranch_sent]
-    dbranch_lane = jnp.concatenate(
-        [after(lane_columns(dbranch)[0], *leaving)] + dbranch_lanes, axis=0
-    )
-    second_all = jnp.concatenate([after(second_in, *leaving)] + second_others, axis=0)
-    narrow_grad = mm(dbranch_lane, second_all, ((0,), (0,))).astype(bf16)
-    project_part = after(project_part, *leaving)
+    dnormed_one = scatter_batch(split(dnormed_part), leaving)
+    project_part = after(project_part, leaving[0])
     out_cols = 3 * channels // blk
     blocks = channels // span
     if out_cols == 3 * span and blocks == blk and blocks % 3 == 2:
@@ -652,8 +646,20 @@
     dpre_cuts = [
         lax.dynamic_slice(dpre, (0, (lane ^ e) * width), (half, width)) for e in range(ring)
     ]
+    dpre_sent = lanes(dpre_cuts[1:])
+    block_output = turn(after(block_low, leaving[0]))
+    waiting = [project_sum, block_output, dbranch_sent, second_sent[2], second_sent[3], dpre_sent]
+    dnormed_one, waiting = lax.optimization_barrier((dnormed_one, waiting))
+    project_sum, block_output, dbranch_sent, second_sent[2], second_sent[3], dpre_sent = waiting
+    second_others = [cells for chunk in zip(*second_sent) for cells in chunk]
+    dbranch_lanes = [batch_all(after(cells, dnormed_one)) for cells in dbranch_sent]
+    dbranch_lane = jnp.concatenate(
+        [after(lane_columns(dbranch)[0], dnormed_one)] + dbranch_lanes, axis=0
+    )
+    second_all = jnp.concatenate([after(second_in, dnormed_one)] + second_others, axis=0)
+    narrow_grad = mm(dbranch_lane, second_all, ((0,), (0,))).astype(bf16)
     dpre_lane = jnp.concatenate(
-        [after(dpre_cuts[0], narrow_grad)] + lanes(dpre_cuts[1:]), axis=0
+        [after(dpre_cuts[0], narrow_grad)] + dpre_sent, axis=0
     )
     first_all = jnp.concatenate([after(first_in, narrow_grad)] + first_others, axis=0)
     widen_grad = mm(first_all, dpre_lane, ((0,), (0,))).astype(bf16)
@@ -661,26 +667,26 @@
     widen_pieces = exchange_batch(
         lambda member: lax.dynamic_index_in_dim(widen_grad, member, 0, keepdims=False)
     )
-    dnormed_one = after(dnormed_one, widen_grad)
-    dnormed_one, *project_sum = gate(dnormed_one, *project_sum)
-    narrow_sum = over_planes(after(narrow_grad, text_sum_grad).reshape(batch, shard, mine))
-    dconved = keep_own * row_norm_back(normed_one, inverse_one, dnormed_one)
-    dconved_low, *widen_pieces[3:] = gate(dconved.astype(bf16), *widen_pieces[3:])
-
-    attended_natural = jnp.concatenate(
-        by_lane([attended_own[:, e * span : (e + 1) * span] for e in range(ring)]), axis=1
-    )[:, :wide_rows]
-    cot_lane = jnp.concatenate(
-        [after(lane_columns(cot_rows)[0], dbranch_own)] + cot_lanes, axis=0
-    )
-    output_grad = mm(cot_lane, attended_natural, ((0,), (0,))).astype(bf16)
-    output_sum = over_planes(output_grad.reshape(batch, shard, wide_rows))
-
+    for bit in bits_of(batch):
+        low = dtext_part.astype(bf16)
+        low = after(low, leaving[0] if bit == 1 else narrow_grad)
+        dtext_part = low.astype(f32) + swap(low, "batch", bit).astype(f32)
+    dtext = dtext_part.astype(bf16)
+    narrow_sum = over_planes(after(narrow_grad, project_part).reshape(batch, shard, mine))
+    dconved = keep_own * row_norm_back(normed_one, inverse_one, after(dnormed_one, narrow_grad))
+    dconved_low = dconved.astype(bf16)
 
     grad_ext = halo(dconved_low, margin)
-    grad_ext, *widen_pieces[:3] = gate(grad_ext, *widen_pieces[:3])
+    text_cut = [
+        jnp.concatenate(
+            [dtext[:, (p * ring + g) * shard : (p * ring + g + 1) * shard] for p in range(batch)],
+            axis=1,
+        )
+        for g in range(ring)
+    ]
+    text_grad = mm(choose(text_cut, lane), soft, ((0,), (0,))).astype(bf16)
+    text_pieces = plane_pieces(text_grad.reshape(batch, shard, clip_rows))
     text_bias_part = jnp.sum(dtext.astype(f32), axis=0) * (first_lane * (bi == 0).astype(f32))
-    block_output = turn(after(block_low, widen_pieces[2]))
     dlatent = dafter
     depth_rows = []
     for tap, (step_row, step_col) in enumerate(taps):
@@ -709,22 +715,22 @@
     sliced = len(late)
     once = first_lane * (bi == 0).astype(f32)
     late = lane_sum(jnp.stack([line(cells) for cells in late + dshift + [time_own[0] * once]]))
+    late, *widen_pieces = gate(late, *widen_pieces)
+    by_plane = [late] + [swap(late, "blk", ring * d) for d in range(1, batch)]
+    by_plane[0], *text_pieces = gate(by_plane[0], *text_pieces)
+    late = jnp.concatenate(
+        [tree_sum([cells[:sliced] for cells in by_plane])] + [cells[sliced:] for cells in by_plane]
+    )
     members = gather_batch(late).reshape((batch,) + late.shape)
     both = tree_sum(members)
-    late = jnp.concatenate(
-        [both[:shared], members[:, shared:sliced].reshape(-1, pad), both[sliced:]]
-    )
-    by_plane = [late] + [swap(late, "blk", ring * d) for d in range(1, batch)]
-    both = tree_sum(by_plane)
-    members = both[shared : shared + batch * (sliced - shared)].reshape(batch, -1, pad)
-    widen_held = jnp.stack(widen_pieces)
+    widen_held = after(
+        jnp.stack(widen_pieces), narrow_sum, by_plane[0]
+    )
 
     def for_plane(member):
         return lax.dynamic_index_in_dim(widen_held, member ^ bi, 0, keepdims=False)
 
-    widen_sum = over_planes(
-        after(jnp.stack([for_plane(p) for p in range(batch)]), narrow_sum)
-    )
+    widen_sum = over_planes(jnp.stack([for_plane(p) for p in range(batch)]))
     arrived = grad_ext
 
     output_bias_sum, narrow_bias_sum, text_bias_sum, depth_bias_sum = (
@@ -732,16 +738,16 @@
     )
     depth_weight_sum = both[4:shared, :channels]
     shifts = [
-        jnp.concatenate([by_plane[d][-3, :channels], by_plane[d][-2, :channels]])
+        jnp.concatenate([both[sliced + 3 * d, :channels], both[sliced + 3 * d + 1, :channels]])
         for d in range(batch)
     ]
     time_bias_sum = tree_sum(shifts)
     time_weight_sum = tree_sum(
-        by_plane[d][-1, : time_embed.shape[1]][:, None] * shifts[d][None, :]
+        both[sliced + 3 * d + 2, : time_embed.shape[1]][:, None] * shifts[d][None, :]
         for d in range(batch)
     )
     ordered = jnp.stack(
-        [lax.dynamic_index_in_dim(members, l ^ bi, 0, keepdims=False) for l in range(batch)]
+        [lax.dynamic_index_in_dim(members[:, shared:sliced], l ^ bi, 0, keepdims=False) for l in range(batch)]
     )
     project_bias_sum = jnp.concatenate(
         [
@@ -767,11 +773,11 @@
         narrow_bias_sum,
         time_weight_sum,
         time_bias_sum,
-        after(text_sum_grad, arrived).T,
+        add_up(text_pieces).T,
         text_bias_sum,
         project_sum,
         project_bias_sum,
-        after(output_sum, arrived).T,
+        after(add_up(output_pieces), arrived).T,
         output_bias_sum,
     )
 

time: 569 us -> 531 us (0.933)
  waiting for transfers between devices: 175 us -> 156 us
  matrix products: 65.9 us -> 57.4 us
    ppermute x65 -> x71, waiting for transfers between devices: 168 us -> 107 us  [swap(): return lax.ppermute(cells, axis, [(i, i ^ distance) for i in range(count)])]
    reduce_scatter x5 -> x3, waiting for transfers between devices: 4.51 us -> 48.1 us  [over_planes(): lax.psum_scatter(shards, 'blk', scatter_dimension=0, tiled=False, axis_in...]
    dot_general x42, matrix products: 65.9 us -> 57.4 us  [mm(): lax.dot_general(left, right, (dims, ((), ())), preferred_element_type=f32)]
    unnamed x292 -> x329, local copies, waits for them, and re-layouts: 21.2 us -> 16.3 us
    ppermute x65 -> x71, starting transfers between devices: 118 us -> 121 us  [swap(): return lax.ppermute(cells, axis, [(i, i ^ distance) for i in range(count)])]
  transfers between devices with their start and end apart: 83 -> 87, of which waited for: 20 -> 25; matrix products, arithmetic and copies ran while one was open for 37% -> 32% of each run, Pallas kernels for 0% -> 0%
where the time goes in v3:
time: 531 us; the launch traced here: 527 us
  waiting for transfers between devices  156 us (29%)
  starting transfers between devices  148 us (28%)
  other arithmetic  73.7 us (14%)
  local copies, waits for them, and re-layouts  72.8 us (14%)
  matrix products  57.4 us (11%)
  between operations  18.9 us (4%)
    ppermute x71, starting transfers between devices, swap(): return lax.ppermute(cells, axis, [(i, i ^ distance) for i in range(count)])  121 us
    ppermute x71, waiting for transfers between devices, swap(): return lax.ppermute(cells, axis, [(i, i ^ distance) for i in range(count)])  107 us
    dot_general x42, matrix products, mm(): lax.dot_general(left, right, (dims, ((), ())), preferred_element_type=f32)  57.4 us
    reduce_scatter x3, waiting for transfers between devices, over_planes(): lax.psum_scatter(shards, 'blk', scatter_dimension=0, tiled=False, axis_in...  48.1 us
    unnamed x329, local copies, waits for them, and re-layouts  16.3 us
    another operation x18, local copies, waits for them, and re-layouts, on_device(): jnp.stack([line(cells) for cells in late + dshift + [time_own[0] * once]])  10.8 us
  transfers between devices with their start and end apart: 87, of which 25 were waited for; matrix products, arithmetic and copies ran while one was open for 32% of the time, Pallas kernels for 0%

profile of v3, /device:TPU:9, one launch (start us, length us, event | category | flops | bytes accessed | tf_op | source)
XLA Modules:
  0.0 526.8 jit_solution(7525428719090982939)
XLA Ops:
  14.0 6.1 %collective-permute-start.4 = (bf16[2,192,1536]{2,1,0:T(8,128)(2,1)}, bf16[2,192,1536]{2,1,0:T(8,128)(2,1)}, u32[]{:S(2)}, u32[]{:S(2)}) collective-permute-start(bf16[2,192,1536]{2,1,0:T(8,128)(2,1)} %pad_maximum_fusion.8), channel_id=1, source_target_pairs={{0,16},{8,24},{16,0},{24,8},{1,17},{9,25},{17,1},{25,9},{2,18},{10... | collective-permute-start | bytes 3538952 | tf_op jit(solution)/shard_map/ppermute | solution.py:22
  34.3 4.5 constant_dynamic-slice_fusion.15
  42.6 6.0 %collective-permute-start.7 = (bf16[2,192,1152]{2,1,0:T(8,128)(2,1)S(1)}, bf16[2,192,1152]{2,1,0:T(8,128)(2,1)S(1)}, u32[]{:S(2)}, u32[]{:S(2)}) collective-permute-start(bf16[2,192,1152]{2,1,0:T(8,128)(2,1)S(1)} %pad_maximum_fusion.14), channel_id=1, source_target_pairs={{0,16},{8,24},{16,0},{24,8},{1,17},{9,25},{17,1},{25,9},{2,18},{10... | collective-permute-start | bytes 2654216 | tf_op jit(solution)/shard_map/ppermute | solution.py:22
  50.5 5.1 collective-permute-start.9
  66.3 9.9 %collective-permute-done.5 = bf16[128,1536]{1,0:T(8,128)(2,1)S(1)} collective-permute-done((bf16[128,1536]{1,0:T(8,128)(2,1)S(1)}, bf16[128,1536]{1,0:T(8,128)(2,1)S(1)}, u32[]{:S(2)}, u32[]{:S(2)}) %collective-permute-start.5) | collective-permute-done | bytes 393248 | tf_op jit(solution)/shard_map/ppermute | solution.py:22
  92.6 4.9 collective-permute-start.11
  105.2 8.0 %collective-permute-start.23 = (bf16[384,1152]{1,0:T(8,128)(2,1)S(1)}, bf16[384,1152]{1,0:T(8,128)(2,1)S(1)}, u32[]{:S(2)}, u32[]{:S(2)}) collective-permute-start(bf16[384,1152]{1,0:T(8,128)(2,1)S(1)} %pad_maximum_fusion.16), channel_id=1, source_target_pairs={{0,8},{8,0},{16,24},{24,16},{1,9},{9,1},{17,25},{25,17},{2,10},{10... | collective-permute-start | bytes 2654216 | tf_op jit(solution)/shard_map/ppermute | solution.py:22
  118.9 7.2 %collective-permute-start.17 = (bf16[2,128,1536]{2,1,0:T(8,128)(2,1)S(1)}, bf16[2,128,1536]{2,1,0:T(8,128)(2,1)S(1)}, u32[]{:S(2)}, u32[]{:S(2)}) collective-permute-start(bf16[2,128,1536]{2,1,0:T(8,128)(2,1)S(1)} %pad_maximum_fusion.18), channel_id=1, source_target_pairs={{0,8},{8,0},{16,24},{24,16},{1,9},{9,1},{17,25},{25,17},{2,10},{10... | collective-permute-start | bytes 2359304 | tf_op jit(solution)/shard_map/ppermute | solution.py:22
  128.3 9.5 %collective-permute-start.19 = (bf16[128,1536]{1,0:T(8,128)(2,1)S(1)}, bf16[128,1536]{1,0:T(8,128)(2,1)S(1)}, u32[]{:S(2)}, u32[]{:S(2)}) collective-permute-start(bf16[128,1536]{1,0:T(8,128)(2,1)S(1)} %fusion.61), channel_id=1, source_target_pairs={{0,16},{8,24},{16,0},{24,8},{1,17},{9,25},{17,1},{25,9},{2,18},{10... | collective-permute-start | bytes 1179656 | tf_op jit(solution)/shard_map/ppermute | solution.py:22
  139.0 8.0 %collective-permute-done.19 = bf16[128,1536]{1,0:T(8,128)(2,1)S(1)} collective-permute-done((bf16[128,1536]{1,0:T(8,128)(2,1)S(1)}, bf16[128,1536]{1,0:T(8,128)(2,1)S(1)}, u32[]{:S(2)}, u32[]{:S(2)}) %collective-permute-start.19) | collective-permute-done | bytes 393248 | tf_op jit(solution)/shard_map/ppermute | solution.py:22
  149.3 8.4 %collective-permute-done.21 = bf16[128,1536]{1,0:T(8,128)(2,1)S(1)} collective-permute-done((bf16[128,1536]{1,0:T(8,128)(2,1)S(1)}, bf16[128,1536]{1,0:T(8,128)(2,1)S(1)}, u32[]{:S(2)}, u32[]{:S(2)}) %collective-permute-start.21) | collective-permute-done | bytes 393248 | tf_op jit(solution)/shard_map/ppermute | solution.py:22
  176.5 6.4 %collective-permute-done.26 = bf16[128,1536]{1,0:T(8,128)(2,1)} collective-permute-done((bf16[128,1536]{1,0:T(8,128)(2,1)S(1)}, bf16[128,1536]{1,0:T(8,128)(2,1)}, u32[]{:S(2)}, u32[]{:S(2)}) %collective-permute-start.26) | collective-permute-done | bytes 393248 | tf_op jit(solution)/shard_map/ppermute | solution.py:22
  232.5 8.6 %collective-permute-done.33 = bf16[512,192]{0,1:T(8,128)(2,1)S(1)} collective-permute-done((bf16[512,192]{0,1:T(8,128)(2,1)S(1)}, bf16[512,192]{0,1:T(8,128)(2,1)S(1)}, u32[]{:S(2)}, u32[]{:S(2)}) %collective-permute-start.33) | collective-permute-done | bytes 196640 | tf_op jit(solution)/shard_map/ppermute | solution.py:22
  259.8 6.3 %collective-permute-done.40 = bf16[2,128,1536]{2,1,0:T(8,128)(2,1)S(1)} collective-permute-done((bf16[2,128,1536]{2,1,0:T(8,128)(2,1)S(1)}, bf16[2,128,1536]{2,1,0:T(8,128)(2,1)S(1)}, u32[]{:S(2)}, u32[]{:S(2)}) %collective-permute-start.40) | collective-permute-done | bytes 786464 | tf_op jit(solution)/shard_map/ppermute | solution.py:22
  266.1 6.5 %collective-permute-start.41 = (bf16[2,128,1536]{2,1,0:T(8,128)(2,1)S(1)}, bf16[2,128,1536]{2,1,0:T(8,128)(2,1)S(1)}, u32[]{:S(2)}, u32[]{:S(2)}) collective-permute-start(bf16[2,128,1536]{2,1,0:T(8,128)(2,1)S(1)} %collective-permute-done.40), channel_id=1, source_target_pairs={{0,8},{8,0},{16,24},{24,16},{1,9},{9,1},{17,25},{25,17},{2,10},{10... | collective-permute-start | bytes 2359304 | tf_op jit(solution)/shard_map/ppermute | solution.py:22
  289.4 5.7 %collective-permute-done.42 = bf16[128,1536]{1,0:T(8,128)(2,1)S(1)} collective-permute-done((bf16[128,1536]{1,0:T(8,128)(2,1)}, bf16[128,1536]{1,0:T(8,128)(2,1)S(1)}, u32[]{:S(2)}, u32[]{:S(2)}) %collective-permute-start.42) | collective-permute-done | bytes 393248 | tf_op jit(solution)/shard_map/ppermute | solution.py:22
  295.9 4.7 multiply_reduce_fusion
  338.3 5.0 collective-permute-done.62
  343.4 5.7 %collective-permute-start.56 = (bf16[384,192]{0,1:T(8,128)(2,1)S(1)}, bf16[384,192]{0,1:T(8,128)(2,1)S(1)}, u32[]{:S(2)}, u32[]{:S(2)}) collective-permute-start(bf16[384,192]{0,1:T(8,128)(2,1)S(1)} %get-tuple-element.449), channel_id=1, source_target_pairs={{0,0},{9,1},{24,2},{1,3},{16,4},{25,5},{8,6},{17,7},{2,8},{11,9},{... | collective-permute-start | bytes 442376 | tf_op jit(solution)/shard_map/ppermute | solution.py:636
  351.3 12.1 %collective-permute-done.63 = bf16[512,768]{1,0:T(8,128)(2,1)} collective-permute-done((bf16[512,768]{1,0:T(8,128)(2,1)}, bf16[512,768]{1,0:T(8,128)(2,1)}, u32[]{:S(2)}, u32[]{:S(2)}) %collective-permute-start.63) | collective-permute-done | bytes 786464 | tf_op jit(solution)/shard_map/ppermute | solution.py:22
  368.9 4.1 convolution_convert_fusion.1
  395.5 4.1 convolution_convert_fusion
  419.2 10.3 %collective-permute-done.74 = bf16[384,768]{1,0:T(8,128)(2,1)} collective-permute-done((bf16[384,768]{1,0:T(8,128)(2,1)}, bf16[384,768]{1,0:T(8,128)(2,1)}, u32[]{:S(2)}, u32[]{:S(2)}) %collective-permute-start.74) | collective-permute-done | bytes 589856 | tf_op jit(solution)/shard_map/ppermute | solution.py:22
  468.2 48.1 %reduce-scatter.8.cloned.1.call-done = bf16[1,384,768]{2,1,0:T(8,128)(2,1)} async-done(((bf16[4,384,768]{2,1,0:T(8,128)(2,1)}), bf16[1,384,768]{2,1,0:T(8,128)(2,1)}) %reduce-scatter.8.cloned.1.call-update) | async-done | bytes 589840 | tf_op jit(solution)/shard_map/reduce_scatter | solution.py:247
  (783 shorter events, 302.5 us)
Async XLA Ops:
  7.2 322.6 %reduce-scatter.4.cloned.1.call-start = ((), (), s32[]{:S(2)}) async-start(), calls=%async_computation.3 | async-start | bytes 2211840 | tf_op jit(solution)/shard_map/reduce_scatter | solution.py:247
  14.0 36.5 %collective-permute-start.4 = (bf16[2,192,1536]{2,1,0:T(8,128)(2,1)}, bf16[2,192,1536]{2,1,0:T(8,128)(2,1)}, u32[]{:S(2)}, u32[]{:S(2)}) collective-permute-start(bf16[2,192,1536]{2,1,0:T(8,128)(2,1)} %pad_maximum_fusion.8), channel_id=1, source_target_pairs={{0,16},{8,24},{16,0},{24,8},{1,17},{9,25},{17,1},{25,9},{2,18},{10... | collective-permute-start | bytes 3538952 | tf_op jit(solution)/shard_map/ppermute | solution.py:22
  22.9 65.2 %collective-permute-start.8 = (bf16[384,1536]{1,0:T(8,128)(2,1)}, bf16[384,1536]{1,0:T(8,128)(2,1)}, u32[]{:S(2)}, u32[]{:S(2)}) collective-permute-start(bf16[384,1536]{1,0:T(8,128)(2,1)} %get-tuple-element.323), channel_id=1, source_target_pairs={{0,8},{8,0},{16,24},{24,16},{1,9},{9,1},{17,25},{25,17},{2,10},{10... | collective-permute-start | bytes 3538952 | tf_op jit(solution)/shard_map/ppermute | solution.py:22
  42.6 42.0 %collective-permute-start.7 = (bf16[2,192,1152]{2,1,0:T(8,128)(2,1)S(1)}, bf16[2,192,1152]{2,1,0:T(8,128)(2,1)S(1)}, u32[]{:S(2)}, u32[]{:S(2)}) collective-permute-start(bf16[2,192,1152]{2,1,0:T(8,128)(2,1)S(1)} %pad_maximum_fusion.14), channel_id=1, source_target_pairs={{0,16},{8,24},{16,0},{24,8},{1,17},{9,25},{17,1},{25,9},{2,18},{10... | collective-permute-start | bytes 2654216 | tf_op jit(solution)/shard_map/ppermute | solution.py:22
  50.5 30.7 %collective-permute-start.9 = (bf16[2,192,1536]{2,1,0:T(8,128)(2,1)}, bf16[2,192,1536]{2,1,0:T(8,128)(2,1)S(1)}, u32[]{:S(2)}, u32[]{:S(2)}) collective-permute-start(bf16[2,192,1536]{2,1,0:T(8,128)(2,1)} %collective-permute-done.4), channel_id=1, source_target_pairs={{0,2},{1,3},{2,0},{3,1},{4,6},{5,7},{6,4},{7,5},{8,10},{9,11},{10,... | collective-permute-start | bytes 3538952 | tf_op jit(solution)/shard_map/ppermute | solution.py:22
  84.6 29.4 %collective-permute-start.15 = (bf16[2,192,1152]{2,1,0:T(8,128)(2,1)S(1)}, bf16[2,192,1152]{2,1,0:T(8,128)(2,1)S(1)}, u32[]{:S(2)}, u32[]{:S(2)}) collective-permute-start(bf16[2,192,1152]{2,1,0:T(8,128)(2,1)S(1)} %collective-permute-done.7), channel_id=1, source_target_pairs={{0,2},{1,3},{2,0},{3,1},{4,6},{5,7},{6,4},{7,5},{8,10},{9,11},{10,... | collective-permute-start | bytes 2654216 | tf_op jit(solution)/shard_map/ppermute | solution.py:22
  105.2 58.4 %collective-permute-start.23 = (bf16[384,1152]{1,0:T(8,128)(2,1)S(1)}, bf16[384,1152]{1,0:T(8,128)(2,1)S(1)}, u32[]{:S(2)}, u32[]{:S(2)}) collective-permute-start(bf16[384,1152]{1,0:T(8,128)(2,1)S(1)} %pad_maximum_fusion.16), channel_id=1, source_target_pairs={{0,8},{8,0},{16,24},{24,16},{1,9},{9,1},{17,25},{25,17},{2,10},{10... | collective-permute-start | bytes 2654216 | tf_op jit(solution)/shard_map/ppermute | solution.py:22
  126.4 33.5 %collective-permute-start.30 = (bf16[77,1536]{1,0:T(8,128)(2,1)S(1)}, bf16[77,1536]{1,0:T(8,128)(2,1)S(1)}, u32[]{:S(2)}, u32[]{:S(2)}) collective-permute-start(bf16[77,1536]{1,0:T(8,128)(2,1)S(1)} %convolution_convert_fusion.3), channel_id=1, source_target_pairs={{0,8},{8,0},{16,24},{24,16},{1,9},{9,1},{17,25},{25,17},{2,10},{10... | collective-permute-start | bytes 709640 | tf_op jit(solution)/shard_map/ppermute | solution.py:22
  241.1 24.9 %collective-permute-start.40 = (bf16[2,128,1536]{2,1,0:T(8,128)(2,1)S(1)}, bf16[2,128,1536]{2,1,0:T(8,128)(2,1)S(1)}, u32[]{:S(2)}, u32[]{:S(2)}) collective-permute-start(bf16[2,128,1536]{2,1,0:T(8,128)(2,1)S(1)} %copy-done.45), channel_id=1, source_target_pairs={{0,1},{1,0},{2,3},{3,2},{4,5},{5,4},{6,7},{7,6},{8,9},{9,8},{10,11... | collective-permute-start | bytes 2359304 | tf_op jit(solution)/shard_map/ppermute | solution.py:22
  253.3 41.9 %collective-permute-start.47 = (bf16[192,384]{1,0:T(8,128)(2,1)}, bf16[192,384]{1,0:T(8,128)(2,1)}, u32[]{:S(2)}, u32[]{:S(2)}) collective-permute-start(bf16[192,384]{1,0:T(8,128)(2,1)} %get-tuple-element.444), channel_id=1, source_target_pairs={{0,6},{1,7},{2,4},{3,5},{4,2},{5,3},{6,0},{7,1},{8,14},{9,15},{10,... | collective-permute-start | bytes 442376 | tf_op jit(solution)/shard_map/ppermute | solution.py:22
  254.0 41.1 %collective-permute-start.46 = (bf16[192,384]{1,0:T(8,128)(2,1)}, bf16[192,384]{1,0:T(8,128)(2,1)}, u32[]{:S(2)}, u32[]{:S(2)}) collective-permute-start(bf16[192,384]{1,0:T(8,128)(2,1)} %get-tuple-element.445), channel_id=1, source_target_pairs={{0,4},{1,5},{2,6},{3,7},{4,0},{5,1},{6,2},{7,3},{8,12},{9,13},{10,... | collective-permute-start | bytes 442376 | tf_op jit(solution)/shard_map/ppermute | solution.py:22
  255.2 23.7 %collective-permute-start.38 = (bf16[128,1536]{1,0:T(8,128)(2,1)S(1)}, bf16[128,1536]{1,0:T(8,128)(2,1)S(1)}, u32[]{:S(2)}, u32[]{:S(2)}) collective-permute-start(bf16[128,1536]{1,0:T(8,128)(2,1)S(1)} %copy-done.54), channel_id=1, source_target_pairs={{0,1},{1,0},{2,3},{3,2},{4,5},{5,4},{6,7},{7,6},{8,9},{9,8},{10,11... | collective-permute-start | bytes 1179656 | tf_op jit(solution)/shard_map/ppermute | solution.py:22
  284.0 161.5 %reduce-scatter.6.cloned.1.call-start = ((), (), s32[]{:S(2)}) async-start(), calls=%async_computation.4 | async-start | bytes 2949120 | tf_op jit(solution)/shard_map/reduce_scatter | solution.py:247
  315.2 28.2 %collective-permute-start.62 = (bf16[128,1536]{1,0:T(8,128)(2,1)}, bf16[128,1536]{1,0:T(8,128)(2,1)}, u32[]{:S(2)}, u32[]{:S(2)}) collective-permute-start(bf16[128,1536]{1,0:T(8,128)(2,1)} %get-tuple-element.192), channel_id=1, source_target_pairs={{0,1},{1,0},{2,3},{3,2},{4,5},{5,4},{6,7},{7,6},{8,9},{9,8},{10,11... | collective-permute-start | bytes 1179656 | tf_op jit(solution)/shard_map/ppermute | solution.py:22
  323.7 39.7 %collective-permute-start.63 = (bf16[512,768]{1,0:T(8,128)(2,1)}, bf16[512,768]{1,0:T(8,128)(2,1)}, u32[]{:S(2)}, u32[]{:S(2)}) collective-permute-start(bf16[512,768]{1,0:T(8,128)(2,1)} %get-tuple-element.368), channel_id=1, source_target_pairs={{0,1},{1,0},{2,3},{3,2},{4,5},{5,4},{6,7},{7,6},{8,9},{9,8},{10,11... | collective-permute-start | bytes 2359304 | tf_op jit(solution)/shard_map/ppermute | solution.py:22
  331.0 33.8 %collective-permute-start.59 = (bf16[128,1536]{1,0:T(8,128)(2,1)}, bf16[128,1536]{1,0:T(8,128)(2,1)S(1)}, u32[]{:S(2)}, u32[]{:S(2)}) collective-permute-start(bf16[128,1536]{1,0:T(8,128)(2,1)} %add_convert_fusion.3), channel_id=1, source_target_pairs={{0,0},{1,1},{2,8},{3,9},{4,16},{5,17},{6,24},{7,25},{8,2},{9,3},{1... | collective-permute-start | bytes 1179656 | tf_op jit(solution)/shard_map/ppermute | solution.py:230
  335.0 29.8 %collective-permute-start.58 = (bf16[384,192]{0,1:T(8,128)(2,1)S(1)}, bf16[384,192]{0,1:T(8,128)(2,1)S(1)}, u32[]{:S(2)}, u32[]{:S(2)}) collective-permute-start(bf16[384,192]{0,1:T(8,128)(2,1)S(1)} %get-tuple-element.448), channel_id=1, source_target_pairs={{8,0},{17,1},{0,2},{9,3},{24,4},{1,5},{16,6},{25,7},{10,8},{19,9},... | collective-permute-start | bytes 442376 | tf_op jit(solution)/shard_map/ppermute | solution.py:636
  343.4 21.4 %collective-permute-start.56 = (bf16[384,192]{0,1:T(8,128)(2,1)S(1)}, bf16[384,192]{0,1:T(8,128)(2,1)S(1)}, u32[]{:S(2)}, u32[]{:S(2)}) collective-permute-start(bf16[384,192]{0,1:T(8,128)(2,1)S(1)} %get-tuple-element.449), channel_id=1, source_target_pairs={{0,0},{9,1},{24,2},{1,3},{16,4},{25,5},{8,6},{17,7},{2,8},{11,9},{... | collective-permute-start | bytes 442376 | tf_op jit(solution)/shard_map/ppermute | solution.py:636
  363.4 29.0 %collective-permute-start.72 = (bf16[2,128,1536]{2,1,0:T(8,128)(2,1)}, bf16[2,128,1536]{2,1,0:T(8,128)(2,1)}, u32[]{:S(2)}, u32[]{:S(2)}) collective-permute-start(bf16[2,128,1536]{2,1,0:T(8,128)(2,1)} %pad_maximum_fusion.25), channel_id=1, source_target_pairs={{0,8},{8,0},{16,24},{24,16},{1,9},{9,1},{17,25},{25,17},{2,10},{10... | collective-permute-start | bytes 2359304 | tf_op jit(solution)/shard_map/ppermute | solution.py:22
  373.1 143.3 %reduce-scatter.8.cloned.1.call-start = ((), (), s32[]{:S(2)}) async-start(), calls=%async_computation.5 | async-start | bytes 2949120 | tf_op jit(solution)/shard_map/reduce_scatter | solution.py:247
  401.6 28.0 %collective-permute-start.74 = (bf16[384,768]{1,0:T(8,128)(2,1)}, bf16[384,768]{1,0:T(8,128)(2,1)}, u32[]{:S(2)}, u32[]{:S(2)}) collective-permute-start(bf16[384,768]{1,0:T(8,128)(2,1)} %get-tuple-element.356), channel_id=1, source_target_pairs={{0,16},{8,24},{16,0},{24,8},{1,17},{9,25},{17,1},{25,9},{2,18},{10... | collective-permute-start | bytes 1769480 | tf_op jit(solution)/shard_map/ppermute | solution.py:22
  402.9 26.7 %collective-permute-start.73 = (bf16[384,768]{1,0:T(8,128)(2,1)}, bf16[384,768]{1,0:T(8,128)(2,1)}, u32[]{:S(2)}, u32[]{:S(2)}) collective-permute-start(bf16[384,768]{1,0:T(8,128)(2,1)} %get-tuple-element.357), channel_id=1, source_target_pairs={{0,8},{8,0},{16,24},{24,16},{1,9},{9,1},{17,25},{25,17},{2,10},{10... | collective-permute-start | bytes 1769480 | tf_op jit(solution)/shard_map/ppermute | solution.py:22
  408.6 24.9 %collective-permute-start.78 = (bf16[192,320]{1,0:T(8,128)(2,1)S(1)}, bf16[192,320]{1,0:T(8,128)(2,1)S(1)}, u32[]{:S(2)}, u32[]{:S(2)}) collective-permute-start(bf16[192,320]{1,0:T(8,128)(2,1)S(1)} %get-tuple-element.440), channel_id=1, source_target_pairs={{0,6},{1,7},{2,4},{3,5},{4,2},{5,3},{6,0},{7,1},{8,14},{9,15},{10,... | collective-permute-start | bytes 368648 | tf_op jit(solution)/shard_map/ppermute | solution.py:22
  412.1 21.5 %collective-permute-start.77 = (bf16[192,320]{1,0:T(8,128)(2,1)S(1)}, bf16[192,320]{1,0:T(8,128)(2,1)S(1)}, u32[]{:S(2)}, u32[]{:S(2)}) collective-permute-start(bf16[192,320]{1,0:T(8,128)(2,1)S(1)} %get-tuple-element.441), channel_id=1, source_target_pairs={{0,4},{1,5},{2,6},{3,7},{4,0},{5,1},{6,2},{7,3},{8,12},{9,13},{10,... | collective-permute-start | bytes 368648 | tf_op jit(solution)/shard_map/ppermute | solution.py:22
  (216 other events, 2657.2 us)
Sparse Core Ops, SparseCore 0:
  284.1 36.8 reduce-scatter.3
  373.1 57.1 reduce-scatter.5
  451.5 64.8 reduce-scatter.7

commit v4 on v3

--- a/solution.py
+++ b/solution.py
@@ -584,6 +584,7 @@
         [after(lane_columns(cot_rows)[0], dqkv)] + cot_lanes, axis=0
     )
     output_grad = mm(cot_lane, attended_natural, ((0,), (0,))).astype(bf16)
+    output_grad = after(output_grad, dbranch_own)
     output_pieces = plane_pieces(output_grad.reshape(batch, shard, wide_rows))
     dbranch, *output_pieces = gate(dbranch, *output_pieces)
     dgrn = mm(dbranch, narrow_weight, ((1,), (1,)))
@@ -648,11 +649,11 @@
     ]
     dpre_sent = lanes(dpre_cuts[1:])
     block_output = turn(after(block_low, leaving[0]))
-    waiting = [project_sum, block_output, dbranch_sent, second_sent[2], second_sent[3], dpre_sent]
+    dbranch_lanes = [batch_all(after(cells, leaving[0])) for cells in dbranch_sent]
+    waiting = [project_sum, block_output, dbranch_lanes, second_sent[2], second_sent[3]]
     dnormed_one, waiting = lax.optimization_barrier((dnormed_one, waiting))
-    project_sum, block_output, dbranch_sent, second_sent[2], second_sent[3], dpre_sent = waiting
+    project_sum, block_output, dbranch_lanes, second_sent[2], second_sent[3] = waiting
     second_others = [cells for chunk in zip(*second_sent) for cells in chunk]
-    dbranch_lanes = [batch_all(after(cells, dnormed_one)) for cells in dbranch_sent]
     dbranch_lane = jnp.concatenate(
         [after(lane_columns(dbranch)[0], dnormed_one)] + dbranch_lanes, axis=0
     )
@@ -667,14 +668,14 @@
     widen_pieces = exchange_batch(
         lambda member: lax.dynamic_index_in_dim(widen_grad, member, 0, keepdims=False)
     )
+    narrow_sum = over_planes(after(narrow_grad, project_part).reshape(batch, shard, mine))
+    dconved = keep_own * row_norm_back(normed_one, inverse_one, after(dnormed_one, widen_grad))
+    dconved_low = dconved.astype(bf16)
     for bit in bits_of(batch):
         low = dtext_part.astype(bf16)
-        low = after(low, leaving[0] if bit == 1 else narrow_grad)
+        low = after(low, leaving[0] if bit == 1 else dconved_low)
         dtext_part = low.astype(f32) + swap(low, "batch", bit).astype(f32)
     dtext = dtext_part.astype(bf16)
-    narrow_sum = over_planes(after(narrow_grad, project_part).reshape(batch, shard, mine))
-    dconved = keep_own * row_norm_back(normed_one, inverse_one, after(dnormed_one, narrow_grad))
-    dconved_low = dconved.astype(bf16)
 
     grad_ext = halo(dconved_low, margin)
     text_cut = [
@@ -715,7 +716,6 @@
     sliced = len(late)
     once = first_lane * (bi == 0).astype(f32)
     late = lane_sum(jnp.stack([line(cells) for cells in late + dshift + [time_own[0] * once]]))
-    late, *widen_pieces = gate(late, *widen_pieces)
     by_plane = [late] + [swap(late, "blk", ring * d) for d in range(1, batch)]
     by_plane[0], *text_pieces = gate(by_plane[0], *text_pieces)
     late = jnp.concatenate(
@@ -723,14 +723,13 @@
     )
     members = gather_batch(late).reshape((batch,) + late.shape)
     both = tree_sum(members)
-    widen_held = after(
-        jnp.stack(widen_pieces), narrow_sum, by_plane[0]
-    )
+    widen_held = jnp.stack(widen_pieces)
 
     def for_plane(member):
         return lax.dynamic_index_in_dim(widen_held, member ^ bi, 0, keepdims=False)
 
-    widen_sum = over_planes(jnp.stack([for_plane(p) for p in range(batch)]))
+    widen_held = jnp.stack([for_plane(p) for p in range(batch)])
+    widen_sum = over_planes(widen_held)
     arrived = grad_ext
 
     output_bias_sum, narrow_bias_sum, text_bias_sum, depth_bias_sum = (

time: 531 us -> 526 us (level)
  local copies, waits for them, and re-layouts: 72.8 us -> 62.5 us
  starting transfers between devices: 148 us -> 158 us
    reduce_scatter x3, waiting for transfers between devices: 48.1 us -> 35.5 us  [over_planes(): lax.psum_scatter(shards, 'blk', scatter_dimension=0, tiled=False, axis_in...]
    another operation x18, local copies, waits for them, and re-layouts: 10.8 us -> 3.97 us  [on_device(): jnp.stack([line(cells) for cells in late + dshift + [time_own[0] * once]])]
    ppermute x71, starting transfers between devices: 121 us -> 128 us  [swap(): return lax.ppermute(cells, axis, [(i, i ^ distance) for i in range(count)])]
    unnamed x329 -> x291, local copies, waits for them, and re-layouts: 16.3 us -> 11.8 us
  transfers between devices with their start and end apart: 87 -> 87, of which waited for: 25 -> 26; matrix products, arithmetic and copies ran while one was open for 32% -> 31% of each run, Pallas kernels for 0% -> 0%
where the time goes in v4:
time: 526 us; the launch traced here: 521 us
  starting transfers between devices  158 us (30%)
  waiting for transfers between devices  151 us (29%)
  other arithmetic  72.3 us (14%)
  local copies, waits for them, and re-layouts  62.5 us (12%)
  matrix products  58.2 us (11%)
  between operations  18.9 us (4%)
    ppermute x71, starting transfers between devices, swap(): return lax.ppermute(cells, axis, [(i, i ^ distance) for i in range(count)])  128 us
    ppermute x71, waiting for transfers between devices, swap(): return lax.ppermute(cells, axis, [(i, i ^ distance) for i in range(count)])  112 us
    dot_general x42, matrix products, mm(): lax.dot_general(left, right, (dims, ((), ())), preferred_element_type=f32)  58.2 us
    reduce_scatter x3, waiting for transfers between devices, over_planes(): lax.psum_scatter(shards, 'blk', scatter_dimension=0, tiled=False, axis_in...  35.5 us
    unnamed x291, local copies, waits for them, and re-layouts  11.8 us
  transfers between devices with their start and end apart: 87, of which 26 were waited for; matrix products, arithmetic and copies ran while one was open for 31% of the time, Pallas kernels for 0%

profile of v4, /device:TPU:9, one launch (start us, length us, event | category | flops | bytes accessed | tf_op | source)
XLA Modules:
  0.0 521.2 jit_solution(3024868877957292392)
XLA Ops:
  14.0 6.1 %collective-permute-start.4 = (bf16[2,192,1536]{2,1,0:T(8,128)(2,1)}, bf16[2,192,1536]{2,1,0:T(8,128)(2,1)}, u32[]{:S(2)}, u32[]{:S(2)}) collective-permute-start(bf16[2,192,1536]{2,1,0:T(8,128)(2,1)} %pad_maximum_fusion.8), channel_id=1, source_target_pairs={{0,16},{8,24},{16,0},{24,8},{1,17},{9,25},{17,1},{25,9},{2,18},{10... | collective-permute-start | bytes 3538952 | tf_op jit(solution)/shard_map/ppermute | solution.py:22
  42.6 6.0 %collective-permute-start.7 = (bf16[2,192,1152]{2,1,0:T(8,128)(2,1)S(1)}, bf16[2,192,1152]{2,1,0:T(8,128)(2,1)S(1)}, u32[]{:S(2)}, u32[]{:S(2)}) collective-permute-start(bf16[2,192,1152]{2,1,0:T(8,128)(2,1)S(1)} %pad_maximum_fusion.14), channel_id=1, source_target_pairs={{0,16},{8,24},{16,0},{24,8},{1,17},{9,25},{17,1},{25,9},{2,18},{10... | collective-permute-start | bytes 2654216 | tf_op jit(solution)/shard_map/ppermute | solution.py:22
  50.5 5.1 collective-permute-start.9
  65.7 10.5 %collective-permute-done.5 = bf16[128,1536]{1,0:T(8,128)(2,1)S(1)} collective-permute-done((bf16[128,1536]{1,0:T(8,128)(2,1)S(1)}, bf16[128,1536]{1,0:T(8,128)(2,1)S(1)}, u32[]{:S(2)}, u32[]{:S(2)}) %collective-permute-start.5) | collective-permute-done | bytes 393248 | tf_op jit(solution)/shard_map/ppermute | solution.py:22
  92.6 4.9 collective-permute-start.11
  105.2 8.0 %collective-permute-start.23 = (bf16[384,1152]{1,0:T(8,128)(2,1)S(1)}, bf16[384,1152]{1,0:T(8,128)(2,1)S(1)}, u32[]{:S(2)}, u32[]{:S(2)}) collective-permute-start(bf16[384,1152]{1,0:T(8,128)(2,1)S(1)} %pad_maximum_fusion.16), channel_id=1, source_target_pairs={{0,8},{8,0},{16,24},{24,16},{1,9},{9,1},{17,25},{25,17},{2,10},{10... | collective-permute-start | bytes 2654216 | tf_op jit(solution)/shard_map/ppermute | solution.py:22
  119.5 7.2 %collective-permute-start.17 = (bf16[2,128,1536]{2,1,0:T(8,128)(2,1)S(1)}, bf16[2,128,1536]{2,1,0:T(8,128)(2,1)S(1)}, u32[]{:S(2)}, u32[]{:S(2)}) collective-permute-start(bf16[2,128,1536]{2,1,0:T(8,128)(2,1)S(1)} %pad_maximum_fusion.18), channel_id=1, source_target_pairs={{0,8},{8,0},{16,24},{24,16},{1,9},{9,1},{17,25},{25,17},{2,10},{10... | collective-permute-start | bytes 2359304 | tf_op jit(solution)/shard_map/ppermute | solution.py:22
  128.9 9.0 %collective-permute-start.19 = (bf16[128,1536]{1,0:T(8,128)(2,1)S(1)}, bf16[128,1536]{1,0:T(8,128)(2,1)S(1)}, u32[]{:S(2)}, u32[]{:S(2)}) collective-permute-start(bf16[128,1536]{1,0:T(8,128)(2,1)S(1)} %fusion.64), channel_id=1, source_target_pairs={{0,16},{8,24},{16,0},{24,8},{1,17},{9,25},{17,1},{25,9},{2,18},{10... | collective-permute-start | bytes 1179656 | tf_op jit(solution)/shard_map/ppermute | solution.py:22
  139.1 8.0 %collective-permute-done.19 = bf16[128,1536]{1,0:T(8,128)(2,1)S(1)} collective-permute-done((bf16[128,1536]{1,0:T(8,128)(2,1)S(1)}, bf16[128,1536]{1,0:T(8,128)(2,1)S(1)}, u32[]{:S(2)}, u32[]{:S(2)}) %collective-permute-start.19) | collective-permute-done | bytes 393248 | tf_op jit(solution)/shard_map/ppermute | solution.py:22
  149.3 8.4 %collective-permute-done.21 = bf16[128,1536]{1,0:T(8,128)(2,1)S(1)} collective-permute-done((bf16[128,1536]{1,0:T(8,128)(2,1)S(1)}, bf16[128,1536]{1,0:T(8,128)(2,1)S(1)}, u32[]{:S(2)}, u32[]{:S(2)}) %collective-permute-start.21) | collective-permute-done | bytes 393248 | tf_op jit(solution)/shard_map/ppermute | solution.py:22
  176.5 6.4 %collective-permute-done.26 = bf16[128,1536]{1,0:T(8,128)(2,1)} collective-permute-done((bf16[128,1536]{1,0:T(8,128)(2,1)S(1)}, bf16[128,1536]{1,0:T(8,128)(2,1)}, u32[]{:S(2)}, u32[]{:S(2)}) %collective-permute-start.26) | collective-permute-done | bytes 393248 | tf_op jit(solution)/shard_map/ppermute | solution.py:22
  232.5 8.7 %collective-permute-done.33 = bf16[512,192]{0,1:T(8,128)(2,1)S(1)} collective-permute-done((bf16[512,192]{0,1:T(8,128)(2,1)S(1)}, bf16[512,192]{0,1:T(8,128)(2,1)S(1)}, u32[]{:S(2)}, u32[]{:S(2)}) %collective-permute-start.33) | collective-permute-done | bytes 196640 | tf_op jit(solution)/shard_map/ppermute | solution.py:22
  269.9 6.5 %collective-permute-start.41 = (bf16[2,128,1536]{2,1,0:T(8,128)(2,1)S(1)}, bf16[2,128,1536]{2,1,0:T(8,128)(2,1)S(1)}, u32[]{:S(2)}, u32[]{:S(2)}) collective-permute-start(bf16[2,128,1536]{2,1,0:T(8,128)(2,1)S(1)} %collective-permute-done.40), channel_id=1, source_target_pairs={{0,8},{8,0},{16,24},{24,16},{1,9},{9,1},{17,25},{25,17},{2,10},{10... | collective-permute-start | bytes 2359304 | tf_op jit(solution)/shard_map/ppermute | solution.py:22
  292.3 5.3 %collective-permute-done.42 = bf16[128,1536]{1,0:T(8,128)(2,1)S(1)} collective-permute-done((bf16[128,1536]{1,0:T(8,128)(2,1)}, bf16[128,1536]{1,0:T(8,128)(2,1)S(1)}, u32[]{:S(2)}, u32[]{:S(2)}) %collective-permute-start.42) | collective-permute-done | bytes 393248 | tf_op jit(solution)/shard_map/ppermute | solution.py:22
  298.4 4.7 multiply_reduce_fusion
  342.8 6.2 %collective-permute-start.56 = (bf16[384,192]{0,1:T(8,128)(2,1)S(1)}, bf16[384,192]{0,1:T(8,128)(2,1)S(1)}, u32[]{:S(2)}, u32[]{:S(2)}) collective-permute-start(bf16[384,192]{0,1:T(8,128)(2,1)S(1)} %get-tuple-element.437), channel_id=1, source_target_pairs={{0,0},{9,1},{24,2},{1,3},{16,4},{25,5},{8,6},{17,7},{2,8},{11,9},{... | collective-permute-start | bytes 442376 | tf_op jit(solution)/shard_map/ppermute | solution.py:637
  366.4 6.4 %collective-permute-done.65 = bf16[512,768]{1,0:T(8,128)(2,1)} collective-permute-done((bf16[512,768]{1,0:T(8,128)(2,1)}, bf16[512,768]{1,0:T(8,128)(2,1)}, u32[]{:S(2)}, u32[]{:S(2)}) %collective-permute-start.65) | collective-permute-done | bytes 786464 | tf_op jit(solution)/shard_map/ppermute | solution.py:22
  380.4 10.9 %collective-permute-start.71 = (bf16[77,1536]{1,0:T(8,128)(2,1)S(1)}, bf16[77,1536]{1,0:T(8,128)(2,1)S(1)}, u32[]{:S(2)}, u32[]{:S(2)}) collective-permute-start(bf16[77,1536]{1,0:T(8,128)(2,1)S(1)} %copy-done.40), channel_id=1, source_target_pairs={{0,16},{8,24},{16,0},{24,8},{1,17},{9,25},{17,1},{25,9},{2,18},{10... | collective-permute-start | bytes 709640 | tf_op jit(solution)/shard_map/ppermute | solution.py:22
  405.8 10.8 %collective-permute-done.72 = f32[20,1536]{1,0:T(8,128)} collective-permute-done((f32[20,1536]{1,0:T(8,128)S(1)}, f32[20,1536]{1,0:T(8,128)}, u32[]{:S(2)}, u32[]{:S(2)}) %collective-permute-start.72) | collective-permute-done | bytes 122912 | tf_op jit(solution)/shard_map/ppermute | solution.py:22
  420.4 5.7 %collective-permute-done.75 = bf16[192,320]{1,0:T(8,128)(2,1)S(1)} collective-permute-done((bf16[192,320]{1,0:T(8,128)(2,1)S(1)}, bf16[192,320]{1,0:T(8,128)(2,1)S(1)}, u32[]{:S(2)}, u32[]{:S(2)}) %collective-permute-start.75) | collective-permute-done | bytes 122912 | tf_op jit(solution)/shard_map/ppermute | solution.py:22
  426.8 8.9 %collective-permute-done.74 = bf16[192,320]{1,0:T(8,128)(2,1)S(1)} collective-permute-done((bf16[192,320]{1,0:T(8,128)(2,1)S(1)}, bf16[192,320]{1,0:T(8,128)(2,1)S(1)}, u32[]{:S(2)}, u32[]{:S(2)}) %collective-permute-start.74) | collective-permute-done | bytes 122912 | tf_op jit(solution)/shard_map/ppermute | solution.py:22
  439.3 4.9 collective-permute-done.78
  455.7 5.8 %collective-permute-done.79 = f32[29,1536]{1,0:T(8,128)S(1)} collective-permute-done((f32[29,1536]{1,0:T(8,128)S(1)}, f32[29,1536]{1,0:T(8,128)S(1)}, u32[]{:S(2)}, u32[]{:S(2)}) %collective-permute-start.79) | collective-permute-done | bytes 178208 | tf_op jit(solution)/shard_map/ppermute | solution.py:22
  474.3 35.5 %reduce-scatter.6.cloned.1.call-done = bf16[1,384,768]{2,1,0:T(8,128)(2,1)} async-done(((bf16[4,384,768]{2,1,0:T(8,128)(2,1)}), bf16[1,384,768]{2,1,0:T(8,128)(2,1)}) %reduce-scatter.6.cloned.1.call-update) | async-done | bytes 589840 | tf_op jit(solution)/shard_map/reduce_scatter | solution.py:247
  (747 shorter events, 302.3 us)
Async XLA Ops:
  7.2 332.3 %reduce-scatter.4.cloned.1.call-start = ((), (), s32[]{:S(2)}) async-start(), calls=%async_computation.3 | async-start | bytes 2211840 | tf_op jit(solution)/shard_map/reduce_scatter | solution.py:247
  14.0 36.5 %collective-permute-start.4 = (bf16[2,192,1536]{2,1,0:T(8,128)(2,1)}, bf16[2,192,1536]{2,1,0:T(8,128)(2,1)}, u32[]{:S(2)}, u32[]{:S(2)}) collective-permute-start(bf16[2,192,1536]{2,1,0:T(8,128)(2,1)} %pad_maximum_fusion.8), channel_id=1, source_target_pairs={{0,16},{8,24},{16,0},{24,8},{1,17},{9,25},{17,1},{25,9},{2,18},{10... | collective-permute-start | bytes 3538952 | tf_op jit(solution)/shard_map/ppermute | solution.py:22
  22.9 65.2 %collective-permute-start.8 = (bf16[384,1536]{1,0:T(8,128)(2,1)}, bf16[384,1536]{1,0:T(8,128)(2,1)}, u32[]{:S(2)}, u32[]{:S(2)}) collective-permute-start(bf16[384,1536]{1,0:T(8,128)(2,1)} %get-tuple-element.311), channel_id=1, source_target_pairs={{0,8},{8,0},{16,24},{24,16},{1,9},{9,1},{17,25},{25,17},{2,10},{10... | collective-permute-start | bytes 3538952 | tf_op jit(solution)/shard_map/ppermute | solution.py:22
  28.6 20.8 %collective-permute-start.2 = (bf16[113,1536]{1,0:T(8,128)(2,1)S(1)}, bf16[113,1536]{1,0:T(8,128)(2,1)S(1)}, u32[]{:S(2)}, u32[]{:S(2)}) collective-permute-start(bf16[113,1536]{1,0:T(8,128)(2,1)S(1)} %get-tuple-element.452), channel_id=1, source_target_pairs={{0,1},{1,8},{8,9},{9,16},{16,17},{17,24},{24,25},{2,3},{3,10},{10,... | collective-permute-start | bytes 1041416 | tf_op jit(solution)/shard_map/ppermute | solution.py:241
  42.6 42.0 %collective-permute-start.7 = (bf16[2,192,1152]{2,1,0:T(8,128)(2,1)S(1)}, bf16[2,192,1152]{2,1,0:T(8,128)(2,1)S(1)}, u32[]{:S(2)}, u32[]{:S(2)}) collective-permute-start(bf16[2,192,1152]{2,1,0:T(8,128)(2,1)S(1)} %pad_maximum_fusion.14), channel_id=1, source_target_pairs={{0,16},{8,24},{16,0},{24,8},{1,17},{9,25},{17,1},{25,9},{2,18},{10... | collective-permute-start | bytes 2654216 | tf_op jit(solution)/shard_map/ppermute | solution.py:22
  50.5 30.7 %collective-permute-start.9 = (bf16[2,192,1536]{2,1,0:T(8,128)(2,1)}, bf16[2,192,1536]{2,1,0:T(8,128)(2,1)S(1)}, u32[]{:S(2)}, u32[]{:S(2)}) collective-permute-start(bf16[2,192,1536]{2,1,0:T(8,128)(2,1)} %collective-permute-done.4), channel_id=1, source_target_pairs={{0,2},{1,3},{2,0},{3,1},{4,6},{5,7},{6,4},{7,5},{8,10},{9,11},{10,... | collective-permute-start | bytes 3538952 | tf_op jit(solution)/shard_map/ppermute | solution.py:22
  84.6 29.4 %collective-permute-start.15 = (bf16[2,192,1152]{2,1,0:T(8,128)(2,1)S(1)}, bf16[2,192,1152]{2,1,0:T(8,128)(2,1)S(1)}, u32[]{:S(2)}, u32[]{:S(2)}) collective-permute-start(bf16[2,192,1152]{2,1,0:T(8,128)(2,1)S(1)} %collective-permute-done.7), channel_id=1, source_target_pairs={{0,2},{1,3},{2,0},{3,1},{4,6},{5,7},{6,4},{7,5},{8,10},{9,11},{10,... | collective-permute-start | bytes 2654216 | tf_op jit(solution)/shard_map/ppermute | solution.py:22
  105.2 58.4 %collective-permute-start.23 = (bf16[384,1152]{1,0:T(8,128)(2,1)S(1)}, bf16[384,1152]{1,0:T(8,128)(2,1)S(1)}, u32[]{:S(2)}, u32[]{:S(2)}) collective-permute-start(bf16[384,1152]{1,0:T(8,128)(2,1)S(1)} %pad_maximum_fusion.16), channel_id=1, source_target_pairs={{0,8},{8,0},{16,24},{24,16},{1,9},{9,1},{17,25},{25,17},{2,10},{10... | collective-permute-start | bytes 2654216 | tf_op jit(solution)/shard_map/ppermute | solution.py:22
  127.0 33.0 %collective-permute-start.30 = (bf16[77,1536]{1,0:T(8,128)(2,1)S(1)}, bf16[77,1536]{1,0:T(8,128)(2,1)S(1)}, u32[]{:S(2)}, u32[]{:S(2)}) collective-permute-start(bf16[77,1536]{1,0:T(8,128)(2,1)S(1)} %convolution_convert_fusion.3), channel_id=1, source_target_pairs={{0,8},{8,0},{16,24},{24,16},{1,9},{9,1},{17,25},{25,17},{2,10},{10... | collective-permute-start | bytes 709640 | tf_op jit(solution)/shard_map/ppermute | solution.py:22
  241.2 24.8 %collective-permute-start.40 = (bf16[2,128,1536]{2,1,0:T(8,128)(2,1)S(1)}, bf16[2,128,1536]{2,1,0:T(8,128)(2,1)S(1)}, u32[]{:S(2)}, u32[]{:S(2)}) collective-permute-start(bf16[2,128,1536]{2,1,0:T(8,128)(2,1)S(1)} %copy-done.42), channel_id=1, source_target_pairs={{0,1},{1,0},{2,3},{3,2},{4,5},{5,4},{6,7},{7,6},{8,9},{9,8},{10,11... | collective-permute-start | bytes 2359304 | tf_op jit(solution)/shard_map/ppermute | solution.py:22
  252.6 29.0 %collective-permute-start.38 = (bf16[128,1536]{1,0:T(8,128)(2,1)S(1)}, bf16[128,1536]{1,0:T(8,128)(2,1)S(1)}, u32[]{:S(2)}, u32[]{:S(2)}) collective-permute-start(bf16[128,1536]{1,0:T(8,128)(2,1)S(1)} %copy-done.45), channel_id=1, source_target_pairs={{0,1},{1,0},{2,3},{3,2},{4,5},{5,4},{6,7},{7,6},{8,9},{9,8},{10,11... | collective-permute-start | bytes 1179656 | tf_op jit(solution)/shard_map/ppermute | solution.py:22
  258.6 21.7 %collective-permute-start.37 = (bf16[128,1536]{1,0:T(8,128)(2,1)S(1)}, bf16[128,1536]{1,0:T(8,128)(2,1)S(1)}, u32[]{:S(2)}, u32[]{:S(2)}) collective-permute-start(bf16[128,1536]{1,0:T(8,128)(2,1)S(1)} %get-tuple-element.287), channel_id=1, source_target_pairs={{0,16},{8,24},{16,0},{24,8},{1,17},{9,25},{17,1},{25,9},{2,18},{10... | collective-permute-start | bytes 1179656 | tf_op jit(solution)/shard_map/ppermute | solution.py:22
  266.8 30.8 %collective-permute-start.47 = (bf16[192,384]{1,0:T(8,128)(2,1)}, bf16[192,384]{1,0:T(8,128)(2,1)}, u32[]{:S(2)}, u32[]{:S(2)}) collective-permute-start(bf16[192,384]{1,0:T(8,128)(2,1)} %get-tuple-element.432), channel_id=1, source_target_pairs={{0,6},{1,7},{2,4},{3,5},{4,2},{5,3},{6,0},{7,1},{8,14},{9,15},{10,... | collective-permute-start | bytes 442376 | tf_op jit(solution)/shard_map/ppermute | solution.py:22
  268.2 29.4 %collective-permute-start.46 = (bf16[192,384]{1,0:T(8,128)(2,1)}, bf16[192,384]{1,0:T(8,128)(2,1)}, u32[]{:S(2)}, u32[]{:S(2)}) collective-permute-start(bf16[192,384]{1,0:T(8,128)(2,1)} %get-tuple-element.433), channel_id=1, source_target_pairs={{0,4},{1,5},{2,6},{3,7},{4,0},{5,1},{6,2},{7,3},{8,12},{9,13},{10,... | collective-permute-start | bytes 442376 | tf_op jit(solution)/shard_map/ppermute | solution.py:22
  286.7 185.3 %reduce-scatter.8.cloned.1.call-start = ((), (), s32[]{:S(2)}) async-start(), calls=%async_computation.5 | async-start | bytes 2949120 | tf_op jit(solution)/shard_map/reduce_scatter | solution.py:247
  317.5 25.3 %collective-permute-start.62 = (bf16[128,1536]{1,0:T(8,128)(2,1)}, bf16[128,1536]{1,0:T(8,128)(2,1)}, u32[]{:S(2)}, u32[]{:S(2)}) collective-permute-start(bf16[128,1536]{1,0:T(8,128)(2,1)} %get-tuple-element.187), channel_id=1, source_target_pairs={{0,1},{1,0},{2,3},{3,2},{4,5},{5,4},{6,7},{7,6},{8,9},{9,8},{10,11... | collective-permute-start | bytes 1179656 | tf_op jit(solution)/shard_map/ppermute | solution.py:22
  317.9 32.3 %collective-permute-start.63 = (bf16[128,1536]{1,0:T(8,128)(2,1)}, bf16[128,1536]{1,0:T(8,128)(2,1)}, u32[]{:S(2)}, u32[]{:S(2)}) collective-permute-start(bf16[128,1536]{1,0:T(8,128)(2,1)} %get-tuple-element.188), channel_id=1, source_target_pairs={{0,1},{1,0},{2,3},{3,2},{4,5},{5,4},{6,7},{7,6},{8,9},{9,8},{10,11... | collective-permute-start | bytes 1179656 | tf_op jit(solution)/shard_map/ppermute | solution.py:22
  350.4 22.4 %collective-permute-start.65 = (bf16[512,768]{1,0:T(8,128)(2,1)}, bf16[512,768]{1,0:T(8,128)(2,1)}, u32[]{:S(2)}, u32[]{:S(2)}) collective-permute-start(bf16[512,768]{1,0:T(8,128)(2,1)} %get-tuple-element.356), channel_id=1, source_target_pairs={{0,1},{1,0},{2,3},{3,2},{4,5},{5,4},{6,7},{7,6},{8,9},{9,8},{10,11... | collective-permute-start | bytes 2359304 | tf_op jit(solution)/shard_map/ppermute | solution.py:22
  362.6 147.1 %reduce-scatter.6.cloned.1.call-start = ((), (), s32[]{:S(2)}) async-start(), calls=%async_computation.4 | async-start | bytes 2949120 | tf_op jit(solution)/shard_map/reduce_scatter | solution.py:247
  392.4 25.1 %collective-permute-start.67 = (bf16[113,1536]{1,0:T(8,128)(2,1)}, bf16[113,1536]{1,0:T(8,128)(2,1)S(1)}, u32[]{:S(2)}, u32[]{:S(2)}) collective-permute-start(bf16[113,1536]{1,0:T(8,128)(2,1)} %get-tuple-element.442), channel_id=1, source_target_pairs={{1,0},{8,1},{9,8},{16,9},{17,16},{24,17},{25,24},{3,2},{10,3},{11,... | collective-permute-start | bytes 1041416 | tf_op jit(solution)/shard_map/ppermute | solution.py:242
  397.0 20.6 %collective-permute-start.66 = (bf16[113,1536]{1,0:T(8,128)(2,1)}, bf16[113,1536]{1,0:T(8,128)(2,1)S(1)}, u32[]{:S(2)}, u32[]{:S(2)}) collective-permute-start(bf16[113,1536]{1,0:T(8,128)(2,1)} %get-tuple-element.443), channel_id=1, source_target_pairs={{0,1},{1,8},{8,9},{9,16},{16,17},{17,24},{24,25},{2,3},{3,10},{10,... | collective-permute-start | bytes 1041416 | tf_op jit(solution)/shard_map/ppermute | solution.py:241
  400.3 51.8 %collective-permute-start.83 = (bf16[384,768]{1,0:T(8,128)(2,1)}, bf16[384,768]{1,0:T(8,128)(2,1)}, u32[]{:S(2)}, u32[]{:S(2)}) collective-permute-start(bf16[384,768]{1,0:T(8,128)(2,1)} %get-tuple-element.344), channel_id=1, source_target_pairs={{0,24},{8,16},{16,8},{24,0},{1,25},{9,17},{17,9},{25,1},{2,26},{10... | collective-permute-start | bytes 1769480 | tf_op jit(solution)/shard_map/ppermute | solution.py:22
  417.6 26.7 %collective-permute-start.78 = (f32[20,1536]{1,0:T(8,128)S(1)}, f32[20,1536]{1,0:T(8,128)S(1)}, u32[]{:S(2)}, u32[]{:S(2)}) collective-permute-start(f32[20,1536]{1,0:T(8,128)S(1)} %add.1129), channel_id=1, source_target_pairs={{0,6},{1,7},{2,4},{3,5},{4,2},{5,3},{6,0},{7,1},{8,14},{9,15},{10,... | collective-permute-start | bytes 368648 | tf_op jit(solution)/shard_map/ppermute | solution.py:22
  426.1 26.0 %collective-permute-start.82 = (bf16[384,768]{1,0:T(8,128)(2,1)}, bf16[384,768]{1,0:T(8,128)(2,1)}, u32[]{:S(2)}, u32[]{:S(2)}) collective-permute-start(bf16[384,768]{1,0:T(8,128)(2,1)} %get-tuple-element.345), channel_id=1, source_target_pairs={{0,16},{8,24},{16,0},{24,8},{1,17},{9,25},{17,1},{25,9},{2,18},{10... | collective-permute-start | bytes 1769480 | tf_op jit(solution)/shard_map/ppermute | solution.py:22
  (199 other events, 3426.0 us)
Sparse Core Ops, SparseCore 0:
  286.9 36.5 reduce-scatter.3
  362.7 76.4 reduce-scatter.7
  455.8 53.8 reduce-scatter.5
